TPU v7x, 32 devices: a whole 2x2x4 slice. The times are simulated.
32 devices in a mesh: freq: 4 (over y, x), tile: 8 (over z, core).
Axes of the slice: x: 2, y: 2, z: 4, core: 2. Of those that a mesh axis runs over, the one named last changes fastest.
Arguments:
- x_field: bfloat16 [4, 2, 5120, 256], P('freq', None, 'tile'), may hold values from -6 to 6
- data: bfloat16 [4, 2, 5120, 256], P('freq', None, 'tile'), may hold values from -6 to 6
- u_bases: bfloat16 [4, 8, 8, 128, 2, 640], P('freq', 'tile'), may hold values from -0.21875 to 0.21875
- v_bases: bfloat16 [4, 8, 8, 128, 2, 640], P('freq', None, 'tile'), may hold values from -0.15625 to 0.15625
- ranks: int32 [4, 8, 8], P('freq'), may hold values from 49 to 96, as said below
- onset: int32 [5120, 256], P(('tile', 'freq')), may hold values from 0 to 3
Outputs:
- gradient: float32 [8, 5120, 256], P(None, ('tile', 'freq'))
Inputs may be any that keep to these rules, and one draw needn't show every extreme that they name: ranks[f,r,c] is the rank of tile (r, c) at frequency f; it is at most 96, and equal to 96 for some tile of every frequency.
All inputs are finite; a program needn't handle non-finite values.
Results may differ from a plain program's by a relative error of at most 0.0055.
Values may be sent and summed in bfloat16 or wider, within the bound.
No kernel may reach another device: no remote copies, remote signals or barrier semaphores. Data moves between devices by JAX's collectives and lax.ppermute only.
A program may use at most 64 MiB of HBM per device.

v0:
```python
import functools
import math

import jax
import jax.numpy as jnp
from jax import lax
from jax.experimental import pallas as pl
from jax.experimental.pallas import tpu as pltpu
from jax.sharding import PartitionSpec as P


RMAX = 96
LANES = 128
BF16 = jnp.bfloat16
F32 = jnp.float32
VMEM = pl.BlockSpec(memory_space=pltpu.VMEM)
SMEM = pl.BlockSpec(memory_space=pltpu.SMEM)
ANY = pl.BlockSpec(memory_space=pl.ANY)
HBM = pl.BlockSpec(memory_space=pltpu.MemorySpace.HBM)


def params():
    return pltpu.CompilerParams(vmem_limit_bytes=20 * 1024 * 1024)


def level_mask(rank):
    level = lax.broadcasted_iota(jnp.int32, (RMAX, LANES), 0)
    return (level < rank).astype(F32)


def masked(value, mask):
    copies = value.shape[1] // LANES
    return (value * jnp.concatenate([mask] * copies, axis=1)).astype(BF16)


def cost(flops):
    return pl.CostEstimate(flops=flops, bytes_accessed=10**7, transcendentals=0)


def coeff_outputs(ks, masks, factors, field, product, outs):
    stations = factors.shape[3]
    left = factors[...].reshape(len(ks) * 2 * RMAX, stations)
    half = field.shape[2] // LANES
    parts = 2 * half
    for p in range(2):
        result = jnp.dot(left, field[p], preferred_element_type=F32)
        for j in range(half):
            product[p * half + j] = result[:, j * LANES : (j + 1) * LANES]
    for i, k in enumerate(ks):
        mask = masks[i]
        base = i * 2 * RMAX
        even = [product[j, pl.ds(base, RMAX, stride=2), :] for j in range(parts)]
        odd = [product[j, pl.ds(base + 1, RMAX, stride=2), :] for j in range(parts)]
        for j in range(half):
            real = masked(even[j] + odd[half + j], mask)
            imag = masked(even[half + j] - odd[j], mask)
            outs[i][:, j * LANES : (j + 1) * LANES] = real
            outs[i][:, (half + j) * LANES : (half + j + 1) * LANES] = imag


def coeff_first_kernel(first, rest, *refs):
    rank_hbm, v_hbm, x_hbm = refs[:3]
    outs = refs[3 : 3 + len(first)]
    field, rest_factors, rest_masks = refs[3 + len(first) : 6 + len(first)]
    rank_ref, factors, product, sems, rest_sems, field_sem, rank_sem = refs[6 + len(first) :]
    me = lax.axis_index("tile")

    def load(k, target, sem):
        return pltpu.make_async_copy(v_hbm.at[me ^ k, pl.ds(0, RMAX)], target, sem)

    rank_copy = pltpu.make_async_copy(rank_hbm, rank_ref, rank_sem)
    field_copy = pltpu.make_async_copy(x_hbm, field, field_sem)
    copies = [load(k, factors.at[i], sems.at[i]) for i, k in enumerate(first)]
    rest_copies = [load(k, rest_factors.at[i], rest_sems.at[i]) for i, k in enumerate(rest)]
    field_copy.start()
    for copy in copies:
        copy.start()
    rank_copy.start()
    for copy in rest_copies:
        copy.start()
    rank_copy.wait()
    for i, k in enumerate(rest):
        rest_masks[i] = level_mask(rank_ref[me ^ k, me])
    masks = [level_mask(rank_ref[me ^ k, me]) for k in first]
    field_copy.wait()
    for copy in copies:
        copy.wait()
    coeff_outputs(first, masks, factors, field, product, outs)
    for copy in rest_copies:
        copy.wait()


def coeff_first(ranks, v, x, first, rest):
    stations, virtual = x.shape[1], x.shape[2]
    outs = [jax.ShapeDtypeStruct((RMAX, 2 * virtual), BF16) for _ in first]
    outs.append(jax.ShapeDtypeStruct(x.shape, BF16))
    outs.append(jax.ShapeDtypeStruct((len(rest), RMAX, 2, stations), BF16))
    outs.append(jax.ShapeDtypeStruct((len(rest), RMAX, LANES), F32))
    return pl.pallas_call(
        functools.partial(coeff_first_kernel, first, rest),
        out_shape=outs,
        in_specs=[HBM, HBM, HBM],
        out_specs=[VMEM for _ in outs],
        scratch_shapes=[
            pltpu.SMEM(ranks.shape, jnp.int32),
            pltpu.VMEM((len(first), RMAX, 2, stations), BF16),
            pltpu.VMEM((2 * virtual // LANES, len(first) * 2 * RMAX, LANES), F32),
            pltpu.SemaphoreType.DMA((len(first),)),
            pltpu.SemaphoreType.DMA((len(rest),)),
            pltpu.SemaphoreType.DMA,
            pltpu.SemaphoreType.DMA,
        ],
        compiler_params=params(),
        cost_estimate=cost(10**9),
        name="coeff_first",
    )(ranks, v, x)


def coeff_rest_kernel(rest, *refs):
    masks, field, factors = refs[:3]
    outs = refs[3 : 3 + len(rest)]
    coeff_outputs(rest, [masks[i] for i in range(len(rest))], factors, field, refs[-1], outs)


def coeff_rest(masks, field, factors, rest):
    width = 2 * field.shape[2]
    return pl.pallas_call(
        functools.partial(coeff_rest_kernel, rest),
        out_shape=[jax.ShapeDtypeStruct((RMAX, width), BF16) for _ in rest],
        in_specs=[VMEM, VMEM, VMEM],
        out_specs=[VMEM for _ in rest],
        scratch_shapes=[pltpu.VMEM((width // LANES, len(rest) * 2 * RMAX, LANES), F32)],
        compiler_params=params(),
        cost_estimate=cost(10**9),
        name="coeff_rest",
    )(masks, field, factors)


def prepare_kernel(want_rows, *refs):
    w_hbm, rank_ref = refs[:2]
    turned_ref = refs[3]
    if want_rows:
        rows_ref, masks = refs[4:6]
        factors, spread, paired, sems = refs[6:]
    else:
        rows_ref = masks = None
        factors, spread, paired, sems = refs[4:]
    me = lax.axis_index("tile")
    count = factors.shape[0]
    stations = factors.shape[3]
    columns = stations // LANES
    copies = [
        pltpu.make_async_copy(w_hbm.at[me ^ k, pl.ds(0, RMAX)], factors.at[k], sems.at[k])
        for k in range(count)
    ]
    for copy in copies:
        copy.start()
    if masks is not None:
        for k in range(count):
            masks[k] = level_mask(rank_ref[me, me ^ k])
    for k in range(count):
        copies[k].wait()
        flat = factors[k].reshape(2 * RMAX, stations).astype(F32)
        for j in range(columns):
            spread[j] = flat[:, j * LANES : (j + 1) * LANES]
        for p in range(2):
            for j in range(columns):
                piece = spread[j, pl.ds(p, RMAX, stride=2), :].astype(BF16)
                row = (2 * p + k % 2) * RMAX
                paired[row : row + RMAX, j * LANES : (j + 1) * LANES] = piece
                if rows_ref is not None:
                    column = p * stations + j * LANES
                    rows_ref[k * RMAX : (k + 1) * RMAX, column : column + LANES] = piece
        if k % 2:
            for i in range(4 * RMAX // LANES):
                block = paired[i * LANES : (i + 1) * LANES, :]
                turned_ref[k // 2, :, i * LANES : (i + 1) * LANES] = block.T


def prepare(w, ranks, after, want_rows):
    count, _, _, stations = w.shape
    outs = [jax.ShapeDtypeStruct((count // 2, stations, 4 * RMAX), BF16)]
    if want_rows:
        outs.append(jax.ShapeDtypeStruct((count * RMAX, 2 * stations), BF16))
        outs.append(jax.ShapeDtypeStruct((count, RMAX, LANES), F32))
    return pl.pallas_call(
        functools.partial(prepare_kernel, want_rows),
        out_shape=outs,
        in_specs=[HBM, SMEM, ANY],
        out_specs=[VMEM for _ in outs],
        scratch_shapes=[
            pltpu.VMEM((count, RMAX, 2, stations), BF16),
            pltpu.VMEM((stations // LANES, 2 * RMAX, LANES), F32),
            pltpu.VMEM((4 * RMAX, stations), BF16),
            pltpu.SemaphoreType.DMA((count,)),
        ],
        compiler_params=params(),
        cost_estimate=cost(10**9),
        name="prepare",
    )(w, ranks, after)


def apply_pairs(bases, blocks, turned_ref):
    virtual = blocks[0].shape[1] // 2
    total = None
    for i, base in enumerate(bases):
        pair = [blocks[2 * i][...], blocks[2 * i + 1][...]]
        turned = [jnp.concatenate([-b[:, virtual:], b[:, :virtual]], axis=1) for b in pair]
        stack = jnp.concatenate(pair + turned, axis=0)
        term = jnp.dot(turned_ref[base // 2], stack, preferred_element_type=F32)
        total = term if total is None else total + term
    return total


def partial_kernel(bases, *refs):
    turned_ref = refs[0]
    out_ref = refs[-1]
    out_ref[...] = apply_pairs(bases, refs[1:-1], turned_ref)


def partial_sum(turned, bases, blocks):
    stations = turned.shape[1]
    width = blocks[0].shape[1]
    return pl.pallas_call(
        functools.partial(partial_kernel, bases),
        out_shape=jax.ShapeDtypeStruct((stations, width), F32),
        in_specs=[VMEM] * (1 + len(blocks)),
        out_specs=VMEM,
        compiler_params=params(),
        cost_estimate=cost(10**9),
        name="partial_sum",
    )(turned, *blocks)


def adjoint_outputs(ks, masks, rows_ref, stacked, outs):
    low = min(ks)
    rows = rows_ref[low * RMAX : (low + len(ks)) * RMAX, :]
    product = jnp.dot(rows, stacked[...], preferred_element_type=F32)
    for i, k in enumerate(ks):
        block = product[(k - low) * RMAX : (k - low + 1) * RMAX, :]
        outs[i][...] = masked(block, masks[k])


def residual_kernel(base, ks, *refs):
    masks, rows_ref, turned_ref, data_ref, partial_ref = refs[:5]
    blocks = refs[5:7]
    outs = refs[7 : 7 + len(ks)]
    stacked = refs[7 + len(ks)]
    stations, virtual = data_ref.shape[1], data_ref.shape[2]
    predicted = partial_ref[...] + apply_pairs((base,), blocks, turned_ref)
    real = (predicted[:, :virtual] - data_ref[0].astype(F32)).astype(BF16)
    imag = (predicted[:, virtual:] - data_ref[1].astype(F32)).astype(BF16)
    stacked[:stations, :virtual] = real
    stacked[:stations, virtual:] = imag
    stacked[stations:, :virtual] = imag
    stacked[stations:, virtual:] = -real
    adjoint_outputs(ks, masks, rows_ref, stacked, outs)


def residual_blocks(masks, rows, turned, data, partial, base, blocks, ks):
    stations, virtual = data.shape[1], data.shape[2]
    outs = [jax.ShapeDtypeStruct((RMAX, 2 * virtual), BF16) for _ in ks]
    outs.append(jax.ShapeDtypeStruct((2 * stations, 2 * virtual), BF16))
    return pl.pallas_call(
        functools.partial(residual_kernel, base, ks),
        out_shape=outs,
        in_specs=[VMEM] * 7,
        out_specs=[VMEM for _ in outs],
        compiler_params=params(),
        cost_estimate=cost(10**9),
        name="residual_blocks",
    )(masks, rows, turned, data, partial, *blocks)


def adjoint_kernel(ks, *refs):
    adjoint_outputs(ks, *refs[:3], refs[3:])


def adjoint_blocks(masks, rows, stacked, ks):
    width = stacked.shape[1]
    return pl.pallas_call(
        functools.partial(adjoint_kernel, ks),
        out_shape=[jax.ShapeDtypeStruct((RMAX, width), BF16) for _ in ks],
        in_specs=[VMEM, VMEM, VMEM],
        out_specs=[VMEM for _ in ks],
        compiler_params=params(),
        cost_estimate=cost(10**9),
        name="adjoint_blocks",
    )(masks, rows, stacked)


def spectrum_kernel(base, freqs, chunk, *refs):
    turned_ref, partial_ref = refs[:2]
    pair = refs[2:4]
    outs = refs[4 : 4 + freqs]
    spectrum = refs[4 + freqs]
    mine = lax.axis_index("freq")
    virtual = partial_ref.shape[1] // 2
    real = slice(chunk * LANES, (chunk + 1) * LANES)
    imag = slice(virtual + chunk * LANES, virtual + (chunk + 1) * LANES)
    stack = [jnp.concatenate([b[:, real], b[:, imag]], axis=1) for b in pair]
    stack += [jnp.concatenate([-b[:, imag], b[:, real]], axis=1) for b in pair]
    late = jnp.dot(
        turned_ref[base // 2], jnp.concatenate(stack, axis=0), preferred_element_type=F32
    )
    spectrum[:, :LANES] = partial_ref[:, real] + late[:, :LANES]
    spectrum[:, LANES:] = partial_ref[:, imag] + late[:, LANES:]
    share = outs[0].shape[0]
    for k in range(freqs):
        rows = pl.ds(pl.multiple_of((mine ^ k) * share, 8), share)
        outs[k][...] = spectrum[rows, :].astype(BF16)


def spectrum_blocks(turned, partial, base, blocks, freqs, chunk):
    stations = partial.shape[0]
    return pl.pallas_call(
        functools.partial(spectrum_kernel, base, freqs, chunk),
        out_shape=[
            jax.ShapeDtypeStruct((stations // freqs, 2 * LANES), BF16) for _ in range(freqs)
        ],
        in_specs=[VMEM] * 4,
        out_specs=[VMEM] * freqs,
        scratch_shapes=[pltpu.VMEM((stations, 2 * LANES), F32)],
        compiler_params=params(),
        cost_estimate=cost(5 * 10**8),
        name="spectrum_blocks",
    )(turned, partial, *blocks)


def traces_kernel(freqs, chunk, *refs):
    onset_ref = refs[0]
    blocks = refs[1 : 1 + freqs]
    out_hbm, gathered, traces, sems = refs[-4:]
    mine = lax.axis_index("freq")
    for k in range(freqs):
        gathered[mine ^ k] = blocks[k][...]
    times = 2 * freqs
    scaling = 1.0 / math.sqrt(freqs)
    lanes = pl.ds(chunk * LANES, LANES)
    copies = [
        pltpu.make_async_copy(traces.at[t], out_hbm.at[t, :, lanes], sems.at[t])
        for t in range(times)
    ]
    onset = onset_ref[:, lanes]
    for t in range(freqs):
        sums = [None, None]
        for f in range(freqs):
            turn = (f + 1) * t % times
            angle = 2.0 * math.pi * turn / times
            quarter = 4 * turn % times == 0
            for part, weight in ((0, math.cos(angle)), (1, -math.sin(angle))):
                if quarter:
                    weight = float(round(weight))
                if weight != 0.0:
                    value = gathered[f, :, part * LANES : (part + 1) * LANES]
                    term = value.astype(F32) * (weight * scaling)
                    old = sums[f % 2]
                    sums[f % 2] = term if old is None else old + term
        odd, even = sums
        traces[t] = jnp.where(t >= onset, even + odd, 0.0)
        copies[t].start()
        traces[t + freqs] = jnp.where(t + freqs >= onset, even - odd, 0.0)
        copies[t + freqs].start()
    for copy in copies:
        copy.wait()


def gated_traces(onset, blocks, chunk, before):
    freqs = len(blocks)
    share, virtual = onset.shape
    operands = (onset, *blocks)
    specs = [VMEM] * (1 + freqs)
    aliases = {}
    if before is not None:
        aliases = {len(operands): 0}
        operands += (before,)
        specs.append(HBM)
    return pl.pallas_call(
        functools.partial(traces_kernel, freqs, chunk),
        out_shape=jax.ShapeDtypeStruct((2 * freqs, share, virtual), F32),
        in_specs=specs,
        out_specs=HBM,
        scratch_shapes=[
            pltpu.VMEM((freqs, share, 2 * LANES), BF16),
            pltpu.VMEM((2 * freqs, share, LANES), F32),
            pltpu.SemaphoreType.DMA((2 * freqs,)),
        ],
        input_output_aliases=aliases,
        compiler_params=params(),
        cost_estimate=cost(5 * 10**8),
        name="gated_traces",
    )(*operands)


def send(block, axis, k):
    count = lax.axis_size(axis)
    return lax.ppermute(block, axis, [(i, i ^ k) for i in range(count)])


def exchange(ks, blocks):
    return {k: send(b, "tile", k) if k else b for k, b in zip(ks, blocks)}


def pick(arrived, bases):
    return [arrived[base + b] for base in bases for b in range(2)]


def pair_bases(count):
    return list(range(count - 2, -1, -2))


def peer_order(count):
    far = [base + b for base in pair_bases(count) if base >= count // 2 for b in range(2)]
    near = [base + b for base in pair_bases(count) if 0 < base < count // 2 for b in range(2)]
    return tuple(far[:2]), tuple(far[2:3] + near + far[3:] + [1, 0])


def hbm(array):
    return pltpu.with_memory_space_constraint(array, pltpu.MemorySpace.HBM)


def body(x_field, data, u_bases, v_bases, ranks, onset):
    count = lax.axis_size("tile")
    freqs = lax.axis_size("freq")
    table = ranks[0]
    u = hbm(u_bases[0, 0])
    v = hbm(v_bases[0, :, 0])
    x = hbm(x_field[0])
    late = count // 2
    early = tuple(base for base in pair_bases(count) if base != late)
    first, rest = peer_order(count)
    *blocks, field, rest_factors, rest_masks = coeff_first(hbm(table), v, x, first, rest)
    arrived = exchange(first, blocks)
    blocks = coeff_rest(rest_masks, field, rest_factors, rest)
    arrived |= exchange(rest, blocks)
    u_turned, u_rows, masks = prepare(u, table, blocks[0], True)
    partial = partial_sum(u_turned, early, pick(arrived, early))
    *blocks, stacked = residual_blocks(
        masks, u_rows, u_turned, data[0], partial, late, pick(arrived, (late,)), first
    )
    returned = exchange(first, blocks)
    blocks = adjoint_blocks(masks, u_rows, stacked, rest)
    returned |= exchange(rest, blocks)
    (v_turned,) = prepare(v, table, stacked, False)
    partial = partial_sum(v_turned, early, pick(returned, early))
    spectra = []
    for chunk in range(x.shape[2] // LANES):
        blocks = spectrum_blocks(
            v_turned, partial, late, pick(returned, (late,)), freqs, chunk
        )
        spectra.append([send(b, "freq", k) if k else b for k, b in enumerate(blocks)])
    result = None
    for chunk, blocks in enumerate(spectra):
        result = gated_traces(onset, blocks, chunk, result)
    return result


def solution(mesh):
    in_specs = (
        P("freq", None, "tile", None),
        P("freq", None, "tile", None),
        P("freq", "tile", None, None, None, None),
        P("freq", None, "tile", None, None, None),
        P("freq", None, None),
        P(("tile", "freq"), None),
    )
    out_specs = P(None, ("tile", "freq"), None)

    return jax.shard_map(body, mesh=mesh, in_specs=in_specs, out_specs=out_specs, check_vma=False)
```

profile of v0, /device:TPU:0, one launch (start us, length us, event | category | flops | bytes accessed | tf_op | source)
XLA Modules:
  0.0 61.2 jit_solution(5697347445721931234)
XLA Ops:
  0.0 2.4 %coeff_first.1 = (bf16[96,512]{1,0:T(8,128)(2,1)S(1)}, bf16[96,512]{1,0:T(8,128)(2,1)S(1)}, bf16[2,640,256]{2,1,0:T(8,128)(2,1)S(1)}, bf16[6,96,2,640]{3,2,1,0:T(2,128)(2,1)S(1)}, f32[6,96,128]{2,1,0:T(8,128)S(1)}) custom-call(s32[8,8]{1,0:T(8,128)} %bitcast.6, bf16[8,128,2,640]{3,2,1,0:T(2,128)(2,1)} %bitcast.9, bf16[2,640,256]{2,1,0:T(8,128)(2,1)} %bitcast.12), custom_call_target="tpu_custom_call" | custom-call | flops 1000000000 | bytes 10000000 | tf_op jit(solution)/shard_map/coeff_first/pallas_call | solution.py:99
  2.4 1.3 %coeff_rest.1 = (bf16[96,512]{1,0:T(8,128)(2,1)S(1)}, bf16[96,512]{1,0:T(8,128)(2,1)S(1)}, bf16[96,512]{1,0:T(8,128)(2,1)S(1)}, bf16[96,512]{1,0:T(8,128)(2,1)S(...) custom-call(f32[6,96,128]{2,1,0:T(8,128)S(1)} %get-tuple-element.36.refs_0_, ...), custom_call_target="tpu_custom_call" | custom-call | flops 1000000000 | bytes 10000000 | tf_op jit(solution)/shard_map/coeff_rest/pallas_call | solution.py:127
  3.6 3.1 %collective-permute-start.2 = (bf16[96,512]{1,0:T(8,128)(2,1)S(1)}, bf16[96,512]{1,0:T(8,128)(2,1)S(1)}, u32[]{:S(2)}, u32[]{:S(2)}) collective-permute-start(bf16[96,512]{1,0:T(8,128)(2,1)S(1)} %get-tuple-element.45), channel_id=1, source_target_pairs={{0,2},{1,3},{2,0},{3,1},{4,6},{5,7},{6,4},{7,5},{8,10},{9,11},{10,... | collective-permute-start | bytes 294920 | tf_op jit(solution)/shard_map/ppermute | solution.py:397
  7.0 4.0 %collective-permute-start = (bf16[96,512]{1,0:T(8,128)(2,1)S(1)}, bf16[96,512]{1,0:T(8,128)(2,1)S(1)}, u32[]{:S(2)}, u32[]{:S(2)}) collective-permute-start(bf16[96,512]{1,0:T(8,128)(2,1)S(1)} %get-tuple-element.43), channel_id=1, source_target_pairs={{0,6},{1,7},{2,4},{3,5},{4,2},{5,3},{6,0},{7,1},{8,14},{9,15},{10,... | collective-permute-start | bytes 294920 | tf_op jit(solution)/shard_map/ppermute | solution.py:397
  10.9 0.7 %collective-permute-start.6 = (bf16[96,512]{1,0:T(8,128)(2,1)S(1)}, bf16[96,512]{1,0:T(8,128)(2,1)S(1)}, u32[]{:S(2)}, u32[]{:S(2)}) collective-permute-start(bf16[96,512]{1,0:T(8,128)(2,1)S(1)} %get-tuple-element.49), channel_id=1, source_target_pairs={{0,5},{1,4},{2,7},{3,6},{4,1},{5,0},{6,3},{7,2},{8,13},{9,12},{10,... | collective-permute-start | bytes 294920 | tf_op jit(solution)/shard_map/ppermute | solution.py:397
  11.7 2.8 %collective-permute-start.5 = (bf16[96,512]{1,0:T(8,128)(2,1)S(1)}, bf16[96,512]{1,0:T(8,128)(2,1)S(1)}, u32[]{:S(2)}, u32[]{:S(2)}) collective-permute-start(bf16[96,512]{1,0:T(8,128)(2,1)S(1)} %get-tuple-element.39.refs_2_), channel_id=1, source_target_pairs={{0,4},{1,5},{2,6},{3,7},{4,0},{5,1},{6,2},{7,3},{8,12},{9,13},{10,... | collective-permute-start | bytes 294920 | tf_op jit(solution)/shard_map/ppermute | solution.py:397
  14.4 4.1 %prepare.2 = (bf16[4,640,384]{2,1,0:T(8,128)(2,1)S(1)}, bf16[768,1280]{1,0:T(8,128)(2,1)S(1)}, f32[8,96,128]{2,1,0:T(8,128)S(1)}) custom-call(bf16[8,128,2,640]{3,2,1,0:T(2,128)(2,1)} %bitcast.11, s32[8,8]{1,0:T(8,128)S(1)} %bitcast.7, bf16[96,512]{1,0:T(8,128)(2,1)S(1)} %get-tuple-element.39.refs_2_), custom_call_target="tpu_custom_call" | custom-call | flops 1000000000 | bytes 10000000 | tf_op jit(solution)/shard_map/prepare/pallas_call | solution.py:186
  18.6 1.2 %partial_sum.2.refs_4_ = f32[640,512]{1,0:T(8,128)S(1)} custom-call(bf16[4,640,384]{2,1,0:T(8,128)(2,1)S(1)} %get-tuple-element.42.refs_0_.refs_2_, bf16[96,512]{1,0:T(8,128)(2,1)S(1)} %collective-permute-done.refs_1_, bf16[96,512]{1,0:T(8,128)(2,1)S(1)} %collective-permute-done.1.refs_2_, bf16[96,512]{1,0:T(8,128)(2,1)S(1)} %collective-permute-done.2.refs_3_, ...), custom_call_target="tpu_custom_call" | custom-call | flops 1000000000 | bytes 10000000 | tf_op jit(solution)/shard_map/partial_sum/pallas_call | solution.py:224
  19.7 5.8 %collective-permute-done.6.refs_6_ = bf16[96,512]{1,0:T(8,128)(2,1)S(1)} collective-permute-done((bf16[96,512]{1,0:T(8,128)(2,1)S(1)}, bf16[96,512]{1,0:T(8,128)(2,1)S(1)}, u32[]{:S(2)}, u32[]{:S(2)}) %collective-permute-start.6) | collective-permute-done | bytes 98336 | tf_op jit(solution)/shard_map/ppermute | solution.py:397
  25.5 2.2 %collective-permute-done.5.refs_5_ = bf16[96,512]{1,0:T(8,128)(2,1)S(1)} collective-permute-done((bf16[96,512]{1,0:T(8,128)(2,1)S(1)}, bf16[96,512]{1,0:T(8,128)(2,1)S(1)}, u32[]{:S(2)}, u32[]{:S(2)}) %collective-permute-start.5) | collective-permute-done | bytes 98336 | tf_op jit(solution)/shard_map/ppermute | solution.py:397
  27.8 0.9 %residual_blocks.1 = (bf16[96,512]{1,0:T(8,128)(2,1)S(1)}, bf16[96,512]{1,0:T(8,128)(2,1)S(1)}, bf16[1280,512]{1,0:T(8,128)(2,1)S(1)}) custom-call(f32[8,96,128]{2,1,0:T(8,128)S(1)} %get-tuple-element.40.refs_0_, bf16[768,1280]{1,0:T(8,128)(2,1)S(1)} %get-tuple-element.41.refs_1_, bf16[4,640,384]{2,1,0:T(8,128)(2,1)S(1)} %get-tuple-element.42.refs_0_.refs_2_, ...), custom_call_target="tpu_custom_call" | custom-call | flops 1000000000 | bytes 10000000 | tf_op jit(solution)/shard_map/residual_blocks/pallas_call | solution.py:264
  28.6 2.5 %collective-permute-start.7 = (bf16[96,512]{1,0:T(8,128)(2,1)S(1)}, bf16[96,512]{1,0:T(8,128)(2,1)S(1)}, u32[]{:S(2)}, u32[]{:S(2)}) collective-permute-start(bf16[96,512]{1,0:T(8,128)(2,1)S(1)} %get-tuple-element.51), channel_id=1, source_target_pairs={{0,6},{1,7},{2,4},{3,5},{4,2},{5,3},{6,0},{7,1},{8,14},{9,15},{10,... | collective-permute-start | bytes 294920 | tf_op jit(solution)/shard_map/ppermute | solution.py:397
  31.2 0.7 %collective-permute-start.8 = (bf16[96,512]{1,0:T(8,128)(2,1)S(1)}, bf16[96,512]{1,0:T(8,128)(2,1)S(1)}, u32[]{:S(2)}, u32[]{:S(2)}) collective-permute-start(bf16[96,512]{1,0:T(8,128)(2,1)S(1)} %get-tuple-element.52), channel_id=1, source_target_pairs={{0,7},{1,6},{2,5},{3,4},{4,3},{5,2},{6,1},{7,0},{8,15},{9,14},{10,... | collective-permute-start | bytes 294920 | tf_op jit(solution)/shard_map/ppermute | solution.py:397
  31.8 0.9 %adjoint_blocks.1 = (bf16[96,512]{1,0:T(8,128)(2,1)S(1)}, bf16[96,512]{1,0:T(8,128)(2,1)S(1)}, bf16[96,512]{1,0:T(8,128)(2,1)S(1)}, bf16[96,512]{1,0:T(8,128)(2,...) custom-call(f32[8,96,128]{2,1,0:T(8,128)S(1)} %get-tuple-element.40.refs_0_, ...), custom_call_target="tpu_custom_call" | custom-call | flops 1000000000 | bytes 10000000 | tf_op jit(solution)/shard_map/adjoint_blocks/pallas_call | solution.py:281
  32.8 2.1 %collective-permute-start.10 = (bf16[96,512]{1,0:T(8,128)(2,1)S(1)}, bf16[96,512]{1,0:T(8,128)(2,1)S(1)}, u32[]{:S(2)}, u32[]{:S(2)}) collective-permute-start(bf16[96,512]{1,0:T(8,128)(2,1)S(1)} %get-tuple-element.54), channel_id=1, source_target_pairs={{0,3},{1,2},{2,1},{3,0},{4,7},{5,6},{6,5},{7,4},{8,11},{9,10},{10,... | collective-permute-start | bytes 294920 | tf_op jit(solution)/shard_map/ppermute | solution.py:397
  35.3 1.1 %collective-permute-start.12 = (bf16[96,512]{1,0:T(8,128)(2,1)S(1)}, bf16[96,512]{1,0:T(8,128)(2,1)S(1)}, u32[]{:S(2)}, u32[]{:S(2)}) collective-permute-start(bf16[96,512]{1,0:T(8,128)(2,1)S(1)} %get-tuple-element.57), channel_id=1, source_target_pairs={{0,4},{1,5},{2,6},{3,7},{4,0},{5,1},{6,2},{7,3},{8,12},{9,13},{10,... | collective-permute-start | bytes 294920 | tf_op jit(solution)/shard_map/ppermute | solution.py:397
  36.4 1.7 %collective-permute-done.8.refs_2_ = bf16[96,512]{1,0:T(8,128)(2,1)S(1)} collective-permute-done((bf16[96,512]{1,0:T(8,128)(2,1)S(1)}, bf16[96,512]{1,0:T(8,128)(2,1)S(1)}, u32[]{:S(2)}, u32[]{:S(2)}) %collective-permute-start.8) | collective-permute-done | bytes 98336 | tf_op jit(solution)/shard_map/ppermute | solution.py:397
  38.1 0.9 %collective-permute-start.13 = (bf16[96,512]{1,0:T(8,128)(2,1)S(1)}, bf16[96,512]{1,0:T(8,128)(2,1)S(1)}, u32[]{:S(2)}, u32[]{:S(2)}) collective-permute-start(bf16[96,512]{1,0:T(8,128)(2,1)S(1)} %get-tuple-element.58), channel_id=1, source_target_pairs={{0,5},{1,4},{2,7},{3,6},{4,1},{5,0},{6,3},{7,2},{8,13},{9,12},{10,... | collective-permute-start | bytes 294920 | tf_op jit(solution)/shard_map/ppermute | solution.py:397
  39.0 3.9 %prepare.3.refs_0_ = bf16[4,640,384]{2,1,0:T(8,128)(2,1)S(1)} custom-call(bf16[8,128,2,640]{3,2,1,0:T(2,128)(2,1)} %bitcast.10, s32[8,8]{1,0:T(8,128)S(1)} %bitcast.8, bf16[1280,512]{1,0:T(8,128)(2,1)S(1)} %get-tuple-element.50.refs_2_), custom_call_target="tpu_custom_call" | custom-call | flops 1000000000 | bytes 10000000 | tf_op jit(solution)/shard_map/prepare/pallas_call | solution.py:186
  42.9 1.3 %collective-permute-done.10.refs_4_ = bf16[96,512]{1,0:T(8,128)(2,1)S(1)} collective-permute-done((bf16[96,512]{1,0:T(8,128)(2,1)S(1)}, bf16[96,512]{1,0:T(8,128)(2,1)S(1)}, u32[]{:S(2)}, u32[]{:S(2)}) %collective-permute-start.10) | collective-permute-done | bytes 98336 | tf_op jit(solution)/shard_map/ppermute | solution.py:397
  44.2 1.2 %partial_sum.3.refs_1_ = f32[640,512]{1,0:T(8,128)S(1)} custom-call(bf16[4,640,384]{2,1,0:T(8,128)(2,1)S(1)} %prepare.3.refs_0_, bf16[96,512]{1,0:T(8,128)(2,1)S(1)} %collective-permute-done.7.refs_1_, bf16[96,512]{1,0:T(8,128)(2,1)S(1)} %collective-permute-done.8.refs_2_, bf16[96,512]{1,0:T(8,128)(2,1)S(1)} %collective-permute-done.9.refs_3_, ...), custom_call_target="tpu_custom_call" | custom-call | flops 1000000000 | bytes 10000000 | tf_op jit(solution)/shard_map/partial_sum/pallas_call | solution.py:224
  45.4 2.1 %collective-permute-done.13.refs_3_ = bf16[96,512]{1,0:T(8,128)(2,1)S(1)} collective-permute-done((bf16[96,512]{1,0:T(8,128)(2,1)S(1)}, bf16[96,512]{1,0:T(8,128)(2,1)S(1)}, u32[]{:S(2)}, u32[]{:S(2)}) %collective-permute-start.13) | collective-permute-done | bytes 98336 | tf_op jit(solution)/shard_map/ppermute | solution.py:397
  47.9 1.6 %collective-permute-start.17 = (bf16[160,256]{1,0:T(8,128)(2,1)S(1)}, bf16[160,256]{1,0:T(8,128)(2,1)S(1)}, u32[]{:S(2)}, u32[]{:S(2)}) collective-permute-start(bf16[160,256]{1,0:T(8,128)(2,1)S(1)} %get-tuple-element.64), channel_id=1, source_target_pairs={{0,8},{8,0},{16,24},{24,16},{1,9},{9,1},{17,25},{25,17},{2,10},{10... | collective-permute-start | bytes 245768 | tf_op jit(solution)/shard_map/ppermute | solution.py:397
  49.4 1.5 %collective-permute-start.18 = (bf16[160,256]{1,0:T(8,128)(2,1)S(1)}, bf16[160,256]{1,0:T(8,128)(2,1)S(1)}, u32[]{:S(2)}, u32[]{:S(2)}) collective-permute-start(bf16[160,256]{1,0:T(8,128)(2,1)S(1)} %get-tuple-element.65), channel_id=1, source_target_pairs={{0,16},{8,24},{16,0},{24,8},{1,17},{9,25},{17,1},{25,9},{2,18},{10... | collective-permute-start | bytes 245768 | tf_op jit(solution)/shard_map/ppermute | solution.py:397
  51.8 1.6 %collective-permute-start.14 = (bf16[160,256]{1,0:T(8,128)(2,1)S(1)}, bf16[160,256]{1,0:T(8,128)(2,1)S(1)}, u32[]{:S(2)}, u32[]{:S(2)}) collective-permute-start(bf16[160,256]{1,0:T(8,128)(2,1)S(1)} %get-tuple-element.60), channel_id=1, source_target_pairs={{0,8},{8,0},{16,24},{24,16},{1,9},{9,1},{17,25},{25,17},{2,10},{10... | collective-permute-start | bytes 245768 | tf_op jit(solution)/shard_map/ppermute | solution.py:397
  53.4 1.6 %collective-permute-start.15 = (bf16[160,256]{1,0:T(8,128)(2,1)S(1)}, bf16[160,256]{1,0:T(8,128)(2,1)S(1)}, u32[]{:S(2)}, u32[]{:S(2)}) collective-permute-start(bf16[160,256]{1,0:T(8,128)(2,1)S(1)} %get-tuple-element.61), channel_id=1, source_target_pairs={{0,16},{8,24},{16,0},{24,8},{1,17},{9,25},{17,1},{25,9},{2,18},{10... | collective-permute-start | bytes 245768 | tf_op jit(solution)/shard_map/ppermute | solution.py:397
  54.9 0.7 %collective-permute-start.16 = (bf16[160,256]{1,0:T(8,128)(2,1)S(1)}, bf16[160,256]{1,0:T(8,128)(2,1)S(1)}, u32[]{:S(2)}, u32[]{:S(2)}) collective-permute-start(bf16[160,256]{1,0:T(8,128)(2,1)S(1)} %get-tuple-element.62), channel_id=1, source_target_pairs={{0,24},{8,16},{16,8},{24,0},{1,25},{9,17},{17,9},{25,1},{2,26},{10... | collective-permute-start | bytes 245768 | tf_op jit(solution)/shard_map/ppermute | solution.py:397
  55.6 0.8 %collective-permute-done.19.refs_4_ = bf16[160,256]{1,0:T(8,128)(2,1)S(1)} collective-permute-done((bf16[160,256]{1,0:T(8,128)(2,1)S(1)}, bf16[160,256]{1,0:T(8,128)(2,1)S(1)}, u32[]{:S(2)}, u32[]{:S(2)}) %collective-permute-start.19) | collective-permute-done | bytes 81952 | tf_op jit(solution)/shard_map/ppermute | solution.py:397
  56.4 1.0 %gated_traces.2.refs_5_ = f32[8,160,256]{2,1,0:T(8,128)} custom-call(s32[160,256]{1,0:T(8,128)S(1)} %copy-done.1, bf16[160,256]{1,0:T(8,128)(2,1)S(1)} %get-tuple-element.63.refs_1_, bf16[160,256]{1,0:T(8,128)(2,1)S(1)} %collective-permute-done.17.refs_2_, bf16[160,256]{1,0:T(8,128)(2,1)S(1)} %collective-permute-done.18.refs_3_, ...), custom_call_target="tpu_custom_call" | custom-call | flops 500000000 | bytes 10000000 | tf_op jit(solution)/shard_map/gated_traces/pallas_call | solution.py:378
  57.4 1.1 %collective-permute-done.15.refs_3_ = bf16[160,256]{1,0:T(8,128)(2,1)S(1)} collective-permute-done((bf16[160,256]{1,0:T(8,128)(2,1)S(1)}, bf16[160,256]{1,0:T(8,128)(2,1)S(1)}, u32[]{:S(2)}, u32[]{:S(2)}) %collective-permute-start.15) | collective-permute-done | bytes 81952 | tf_op jit(solution)/shard_map/ppermute | solution.py:397
  58.5 1.7 %collective-permute-done.16.refs_4_ = bf16[160,256]{1,0:T(8,128)(2,1)S(1)} collective-permute-done((bf16[160,256]{1,0:T(8,128)(2,1)S(1)}, bf16[160,256]{1,0:T(8,128)(2,1)S(1)}, u32[]{:S(2)}, u32[]{:S(2)}) %collective-permute-start.16) | collective-permute-done | bytes 81952 | tf_op jit(solution)/shard_map/ppermute | solution.py:397
  60.3 1.0 %gated_traces.3 = f32[8,160,256]{2,1,0:T(8,128)} custom-call(s32[160,256]{1,0:T(8,128)S(1)} %copy-done.1, bf16[160,256]{1,0:T(8,128)(2,1)S(1)} %get-tuple-element.59.refs_1_, bf16[160,256]{1,0:T(8,128)(2,1)S(1)} %collective-permute-done.14.refs_2_, bf16[160,256]{1,0:T(8,128)(2,1)S(1)} %collective-permute-done.15.refs_3_, ...), custom_call_target="tpu_custom_call", output_to_operand_aliasing={{}: (5, {})} | custom-call | flops 500000000 | bytes 10000000 | tf_op jit(solution)/shard_map/gated_traces/pallas_call | solution.py:378
  (26 shorter events, 1.8 us)
Async XLA Ops:
  2.4 12.1 %copy-start.2 = (s32[1,8,8]{2,1,0:T(8,128)S(1)}, s32[1,8,8]{2,1,0:T(8,128)}, u32[]{:S(2)}) copy-start(s32[1,8,8]{2,1,0:T(8,128)} %param.10) | copy-start | bytes 772
  3.6 7.3 %collective-permute-start.2 = (bf16[96,512]{1,0:T(8,128)(2,1)S(1)}, bf16[96,512]{1,0:T(8,128)(2,1)S(1)}, u32[]{:S(2)}, u32[]{:S(2)}) collective-permute-start(bf16[96,512]{1,0:T(8,128)(2,1)S(1)} %get-tuple-element.45), channel_id=1, source_target_pairs={{0,2},{1,3},{2,0},{3,1},{4,6},{5,7},{6,4},{7,5},{8,10},{9,11},{10,... | collective-permute-start | bytes 294920 | tf_op jit(solution)/shard_map/ppermute | solution.py:397
  6.8 4.9 %collective-permute-start.3 = (bf16[96,512]{1,0:T(8,128)(2,1)S(1)}, bf16[96,512]{1,0:T(8,128)(2,1)S(1)}, u32[]{:S(2)}, u32[]{:S(2)}) collective-permute-start(bf16[96,512]{1,0:T(8,128)(2,1)S(1)} %get-tuple-element.46), channel_id=1, source_target_pairs={{0,3},{1,2},{2,1},{3,0},{4,7},{5,6},{6,5},{7,4},{8,11},{9,10},{10,... | collective-permute-start | bytes 294920 | tf_op jit(solution)/shard_map/ppermute | solution.py:397
  6.8 11.8 %collective-permute-start.4 = (bf16[96,512]{1,0:T(8,128)(2,1)S(1)}, bf16[96,512]{1,0:T(8,128)(2,1)S(1)}, u32[]{:S(2)}, u32[]{:S(2)}) collective-permute-start(bf16[96,512]{1,0:T(8,128)(2,1)S(1)} %get-tuple-element.48), channel_id=1, source_target_pairs={{0,1},{1,0},{2,3},{3,2},{4,5},{5,4},{6,7},{7,6},{8,9},{9,8},{10,11... | collective-permute-start | bytes 294920 | tf_op jit(solution)/shard_map/ppermute | solution.py:397
  7.0 11.6 %collective-permute-start = (bf16[96,512]{1,0:T(8,128)(2,1)S(1)}, bf16[96,512]{1,0:T(8,128)(2,1)S(1)}, u32[]{:S(2)}, u32[]{:S(2)}) collective-permute-start(bf16[96,512]{1,0:T(8,128)(2,1)S(1)} %get-tuple-element.43), channel_id=1, source_target_pairs={{0,6},{1,7},{2,4},{3,5},{4,2},{5,3},{6,0},{7,1},{8,14},{9,15},{10,... | collective-permute-start | bytes 294920 | tf_op jit(solution)/shard_map/ppermute | solution.py:397
  10.9 7.6 %collective-permute-start.1 = (bf16[96,512]{1,0:T(8,128)(2,1)S(1)}, bf16[96,512]{1,0:T(8,128)(2,1)S(1)}, u32[]{:S(2)}, u32[]{:S(2)}) collective-permute-start(bf16[96,512]{1,0:T(8,128)(2,1)S(1)} %get-tuple-element.44), channel_id=1, source_target_pairs={{0,7},{1,6},{2,5},{3,4},{4,3},{5,2},{6,1},{7,0},{8,15},{9,14},{10,... | collective-permute-start | bytes 294920 | tf_op jit(solution)/shard_map/ppermute | solution.py:397
  10.9 14.6 %collective-permute-start.6 = (bf16[96,512]{1,0:T(8,128)(2,1)S(1)}, bf16[96,512]{1,0:T(8,128)(2,1)S(1)}, u32[]{:S(2)}, u32[]{:S(2)}) collective-permute-start(bf16[96,512]{1,0:T(8,128)(2,1)S(1)} %get-tuple-element.49), channel_id=1, source_target_pairs={{0,5},{1,4},{2,7},{3,6},{4,1},{5,0},{6,3},{7,2},{8,13},{9,12},{10,... | collective-permute-start | bytes 294920 | tf_op jit(solution)/shard_map/ppermute | solution.py:397
  11.7 16.1 %collective-permute-start.5 = (bf16[96,512]{1,0:T(8,128)(2,1)S(1)}, bf16[96,512]{1,0:T(8,128)(2,1)S(1)}, u32[]{:S(2)}, u32[]{:S(2)}) collective-permute-start(bf16[96,512]{1,0:T(8,128)(2,1)S(1)} %get-tuple-element.39.refs_2_), channel_id=1, source_target_pairs={{0,4},{1,5},{2,6},{3,7},{4,0},{5,1},{6,2},{7,3},{8,12},{9,13},{10,... | collective-permute-start | bytes 294920 | tf_op jit(solution)/shard_map/ppermute | solution.py:397
  18.5 9.2 %copy-start = (bf16[1,2,640,256]{3,2,1,0:T(8,128)(2,1)S(1)}, bf16[1,2,640,256]{3,2,1,0:T(8,128)(2,1)}, u32[]{:S(2)}) copy-start(bf16[1,2,640,256]{3,2,1,0:T(8,128)(2,1)} %param.7) | copy-start | bytes 1966084
  28.6 6.6 %collective-permute-start.7 = (bf16[96,512]{1,0:T(8,128)(2,1)S(1)}, bf16[96,512]{1,0:T(8,128)(2,1)S(1)}, u32[]{:S(2)}, u32[]{:S(2)}) collective-permute-start(bf16[96,512]{1,0:T(8,128)(2,1)S(1)} %get-tuple-element.51), channel_id=1, source_target_pairs={{0,6},{1,7},{2,4},{3,5},{4,2},{5,3},{6,0},{7,1},{8,14},{9,15},{10,... | collective-permute-start | bytes 294920 | tf_op jit(solution)/shard_map/ppermute | solution.py:397
  31.2 6.9 %collective-permute-start.8 = (bf16[96,512]{1,0:T(8,128)(2,1)S(1)}, bf16[96,512]{1,0:T(8,128)(2,1)S(1)}, u32[]{:S(2)}, u32[]{:S(2)}) collective-permute-start(bf16[96,512]{1,0:T(8,128)(2,1)S(1)} %get-tuple-element.52), channel_id=1, source_target_pairs={{0,7},{1,6},{2,5},{3,4},{4,3},{5,2},{6,1},{7,0},{8,15},{9,14},{10,... | collective-permute-start | bytes 294920 | tf_op jit(solution)/shard_map/ppermute | solution.py:397
  32.8 10.1 %collective-permute-start.9 = (bf16[96,512]{1,0:T(8,128)(2,1)S(1)}, bf16[96,512]{1,0:T(8,128)(2,1)S(1)}, u32[]{:S(2)}, u32[]{:S(2)}) collective-permute-start(bf16[96,512]{1,0:T(8,128)(2,1)S(1)} %get-tuple-element.53), channel_id=1, source_target_pairs={{0,2},{1,3},{2,0},{3,1},{4,6},{5,7},{6,4},{7,5},{8,10},{9,11},{10,... | collective-permute-start | bytes 294920 | tf_op jit(solution)/shard_map/ppermute | solution.py:397
  32.8 11.3 %collective-permute-start.10 = (bf16[96,512]{1,0:T(8,128)(2,1)S(1)}, bf16[96,512]{1,0:T(8,128)(2,1)S(1)}, u32[]{:S(2)}, u32[]{:S(2)}) collective-permute-start(bf16[96,512]{1,0:T(8,128)(2,1)S(1)} %get-tuple-element.54), channel_id=1, source_target_pairs={{0,3},{1,2},{2,1},{3,0},{4,7},{5,6},{6,5},{7,4},{8,11},{9,10},{10,... | collective-permute-start | bytes 294920 | tf_op jit(solution)/shard_map/ppermute | solution.py:397
  35.0 9.2 %collective-permute-start.11 = (bf16[96,512]{1,0:T(8,128)(2,1)S(1)}, bf16[96,512]{1,0:T(8,128)(2,1)S(1)}, u32[]{:S(2)}, u32[]{:S(2)}) collective-permute-start(bf16[96,512]{1,0:T(8,128)(2,1)S(1)} %get-tuple-element.56), channel_id=1, source_target_pairs={{0,1},{1,0},{2,3},{3,2},{4,5},{5,4},{6,7},{7,6},{8,9},{9,8},{10,11... | collective-permute-start | bytes 294920 | tf_op jit(solution)/shard_map/ppermute | solution.py:397
  35.3 10.1 %collective-permute-start.12 = (bf16[96,512]{1,0:T(8,128)(2,1)S(1)}, bf16[96,512]{1,0:T(8,128)(2,1)S(1)}, u32[]{:S(2)}, u32[]{:S(2)}) collective-permute-start(bf16[96,512]{1,0:T(8,128)(2,1)S(1)} %get-tuple-element.57), channel_id=1, source_target_pairs={{0,4},{1,5},{2,6},{3,7},{4,0},{5,1},{6,2},{7,3},{8,12},{9,13},{10,... | collective-permute-start | bytes 294920 | tf_op jit(solution)/shard_map/ppermute | solution.py:397
  38.1 9.4 %collective-permute-start.13 = (bf16[96,512]{1,0:T(8,128)(2,1)S(1)}, bf16[96,512]{1,0:T(8,128)(2,1)S(1)}, u32[]{:S(2)}, u32[]{:S(2)}) collective-permute-start(bf16[96,512]{1,0:T(8,128)(2,1)S(1)} %get-tuple-element.58), channel_id=1, source_target_pairs={{0,5},{1,4},{2,7},{3,6},{4,1},{5,0},{6,3},{7,2},{8,13},{9,12},{10,... | collective-permute-start | bytes 294920 | tf_op jit(solution)/shard_map/ppermute | solution.py:397
  47.9 7.1 %collective-permute-start.17 = (bf16[160,256]{1,0:T(8,128)(2,1)S(1)}, bf16[160,256]{1,0:T(8,128)(2,1)S(1)}, u32[]{:S(2)}, u32[]{:S(2)}) collective-permute-start(bf16[160,256]{1,0:T(8,128)(2,1)S(1)} %get-tuple-element.64), channel_id=1, source_target_pairs={{0,8},{8,0},{16,24},{24,16},{1,9},{9,1},{17,25},{25,17},{2,10},{10... | collective-permute-start | bytes 245768 | tf_op jit(solution)/shard_map/ppermute | solution.py:397
  49.4 6.2 %collective-permute-start.18 = (bf16[160,256]{1,0:T(8,128)(2,1)S(1)}, bf16[160,256]{1,0:T(8,128)(2,1)S(1)}, u32[]{:S(2)}, u32[]{:S(2)}) collective-permute-start(bf16[160,256]{1,0:T(8,128)(2,1)S(1)} %get-tuple-element.65), channel_id=1, source_target_pairs={{0,16},{8,24},{16,0},{24,8},{1,17},{9,25},{17,1},{25,9},{2,18},{10... | collective-permute-start | bytes 245768 | tf_op jit(solution)/shard_map/ppermute | solution.py:397
  51.0 5.4 %copy-start.1 = (s32[160,256]{1,0:T(8,128)S(1)}, s32[160,256]{1,0:T(8,128)}, u32[]{:S(2)}) copy-start(s32[160,256]{1,0:T(8,128)} %refs_0_.3) | copy-start | bytes 491524
  51.0 5.4 %collective-permute-start.19 = (bf16[160,256]{1,0:T(8,128)(2,1)S(1)}, bf16[160,256]{1,0:T(8,128)(2,1)S(1)}, u32[]{:S(2)}, u32[]{:S(2)}) collective-permute-start(bf16[160,256]{1,0:T(8,128)(2,1)S(1)} %get-tuple-element.66), channel_id=1, source_target_pairs={{0,24},{8,16},{16,8},{24,0},{1,25},{9,17},{17,9},{25,1},{2,26},{10... | collective-permute-start | bytes 245768 | tf_op jit(solution)/shard_map/ppermute | solution.py:397
  51.8 5.6 %collective-permute-start.14 = (bf16[160,256]{1,0:T(8,128)(2,1)S(1)}, bf16[160,256]{1,0:T(8,128)(2,1)S(1)}, u32[]{:S(2)}, u32[]{:S(2)}) collective-permute-start(bf16[160,256]{1,0:T(8,128)(2,1)S(1)} %get-tuple-element.60), channel_id=1, source_target_pairs={{0,8},{8,0},{16,24},{24,16},{1,9},{9,1},{17,25},{25,17},{2,10},{10... | collective-permute-start | bytes 245768 | tf_op jit(solution)/shard_map/ppermute | solution.py:397
  53.4 5.2 %collective-permute-start.15 = (bf16[160,256]{1,0:T(8,128)(2,1)S(1)}, bf16[160,256]{1,0:T(8,128)(2,1)S(1)}, u32[]{:S(2)}, u32[]{:S(2)}) collective-permute-start(bf16[160,256]{1,0:T(8,128)(2,1)S(1)} %get-tuple-element.61), channel_id=1, source_target_pairs={{0,16},{8,24},{16,0},{24,8},{1,17},{9,25},{17,1},{25,9},{2,18},{10... | collective-permute-start | bytes 245768 | tf_op jit(solution)/shard_map/ppermute | solution.py:397
  54.9 5.3 %collective-permute-start.16 = (bf16[160,256]{1,0:T(8,128)(2,1)S(1)}, bf16[160,256]{1,0:T(8,128)(2,1)S(1)}, u32[]{:S(2)}, u32[]{:S(2)}) collective-permute-start(bf16[160,256]{1,0:T(8,128)(2,1)S(1)} %get-tuple-element.62), channel_id=1, source_target_pairs={{0,24},{8,16},{16,8},{24,0},{1,25},{9,17},{17,9},{25,1},{2,26},{10... | collective-permute-start | bytes 245768 | tf_op jit(solution)/shard_map/ppermute | solution.py:397
where the time goes:
time: 61.4 us; the launch traced here: 61.2 us
  starting transfers between devices  25.6 us (42%)
  Pallas kernels  18.4 us (30%)
  waiting for transfers between devices  17 us (28%)
    ppermute x20, starting transfers between devices, send(): return lax.ppermute(block, axis, [(i, i ^ k) for i in range(count)])  25.6 us
    ppermute x20, waiting for transfers between devices, send(): return lax.ppermute(block, axis, [(i, i ^ k) for i in range(count)])  17 us
    pallas_call x2, Pallas kernels, prepare(): pl.pallas_call(functools.partial(prepare_kernel, want_rows), out_shape=ou...  7.97 us
    pallas_call x2, Pallas kernels, partial_sum(): pl.pallas_call(functools.partial(partial_kernel, bases), out_shape=jax.Sh...  2.35 us
    pallas_call x1, Pallas kernels, coeff_first(): pl.pallas_call(functools.partial(coeff_first_kernel, first, rest), out_sh...  2.35 us
    pallas_call x2, Pallas kernels, gated_traces(): pl.pallas_call(functools.partial(traces_kernel, freqs, chunk), out_shape=...  1.94 us
    pallas_call x1, Pallas kernels, coeff_rest(): pl.pallas_call(functools.partial(coeff_rest_kernel, rest), out_shape=[jax...  1.26 us
  transfers between devices with their start and end apart: 20, of which 9 were waited for; matrix products, arithmetic and copies ran while one was open for 0% of the time, Pallas kernels for 21%

commit v1 on v0

--- a/solution.py
+++ b/solution.py
@@ -21,6 +21,31 @@
 
 def params():
     return pltpu.CompilerParams(vmem_limit_bytes=20 * 1024 * 1024)
+
+
+def chip_rounds(chips):
+    if chips == 4:
+        return [[0, 1, 2, 3], [1, 3, 0, 2], [3, 2, 1, 0], [2, 0, 3, 1]]
+    return [[chip ^ turn for chip in range(chips)] for turn in range(chips)]
+
+
+def targets(count):
+    return [
+        [2 * dest[tile // 2] + (tile % 2 ^ cross) for tile in range(count)]
+        for dest in chip_rounds(count // 2)
+        for cross in range(2)
+    ]
+
+
+def sources(count):
+    return [[row.index(tile) for tile in range(count)] for row in targets(count)]
+
+
+def lookup(row, me):
+    result = jnp.int32(row[0])
+    for tile in range(1, len(row)):
+        result = jnp.where(me == tile, row[tile], result)
+    return result
 
 
 def level_mask(rank):
@@ -66,8 +91,9 @@
     me = lax.axis_index("tile")
 
     def load(k, target, sem):
-        return pltpu.make_async_copy(v_hbm.at[me ^ k, pl.ds(0, RMAX)], target, sem)
-
+        return pltpu.make_async_copy(v_hbm.at[tiles[k], pl.ds(0, RMAX)], target, sem)
+
+    tiles = [lookup(row, me) for row in targets(len(first) + len(rest))]
     rank_copy = pltpu.make_async_copy(rank_hbm, rank_ref, rank_sem)
     field_copy = pltpu.make_async_copy(x_hbm, field, field_sem)
     copies = [load(k, factors.at[i], sems.at[i]) for i, k in enumerate(first)]
@@ -80,8 +106,8 @@
         copy.start()
     rank_copy.wait()
     for i, k in enumerate(rest):
-        rest_masks[i] = level_mask(rank_ref[me ^ k, me])
-    masks = [level_mask(rank_ref[me ^ k, me]) for k in first]
+        rest_masks[i] = level_mask(rank_ref[tiles[k], me])
+    masks = [level_mask(rank_ref[tiles[k], me]) for k in first]
     field_copy.wait()
     for copy in copies:
         copy.wait()
@@ -149,15 +175,17 @@
     count = factors.shape[0]
     stations = factors.shape[3]
     columns = stations // LANES
+    slots = sources(count) if want_rows else targets(count)
+    tiles = [lookup(row, me) for row in slots]
     copies = [
-        pltpu.make_async_copy(w_hbm.at[me ^ k, pl.ds(0, RMAX)], factors.at[k], sems.at[k])
+        pltpu.make_async_copy(w_hbm.at[tiles[k], pl.ds(0, RMAX)], factors.at[k], sems.at[k])
         for k in range(count)
     ]
     for copy in copies:
         copy.start()
     if masks is not None:
         for k in range(count):
-            masks[k] = level_mask(rank_ref[me, me ^ k])
+            masks[k] = level_mask(rank_ref[me, tiles[k]])
     for k in range(count):
         copies[k].wait()
         flat = factors[k].reshape(2 * RMAX, stations).astype(F32)
@@ -392,27 +420,21 @@
     )(*operands)
 
 
-def send(block, axis, k):
-    count = lax.axis_size(axis)
-    return lax.ppermute(block, axis, [(i, i ^ k) for i in range(count)])
-
-
-def exchange(ks, blocks):
-    return {k: send(b, "tile", k) if k else b for k, b in zip(ks, blocks)}
+def send(block, axis, row):
+    return lax.ppermute(block, axis, list(enumerate(row)))
+
+
+def exchange(rows, ks, blocks):
+    return {k: send(b, "tile", rows[k]) if k else b for k, b in zip(ks, blocks)}
 
 
 def pick(arrived, bases):
     return [arrived[base + b] for base in bases for b in range(2)]
 
 
-def pair_bases(count):
-    return list(range(count - 2, -1, -2))
-
-
-def peer_order(count):
-    far = [base + b for base in pair_bases(count) if base >= count // 2 for b in range(2)]
-    near = [base + b for base in pair_bases(count) if 0 < base < count // 2 for b in range(2)]
-    return tuple(far[:2]), tuple(far[2:3] + near + far[3:] + [1, 0])
+def slot_order(bases):
+    slots = [base + b for base in bases for b in range(2)]
+    return tuple(slots[:2]), tuple(slots[2:] + [1, 0])
 
 
 def hbm(array):
@@ -426,29 +448,38 @@
     u = hbm(u_bases[0, 0])
     v = hbm(v_bases[0, :, 0])
     x = hbm(x_field[0])
-    late = count // 2
-    early = tuple(base for base in pair_bases(count) if base != late)
-    first, rest = peer_order(count)
+    bases = list(range(2, count, 2))
+    first, rest = slot_order(bases)
     *blocks, field, rest_factors, rest_masks = coeff_first(hbm(table), v, x, first, rest)
-    arrived = exchange(first, blocks)
+    arrived = exchange(targets(count), first, blocks)
     blocks = coeff_rest(rest_masks, field, rest_factors, rest)
-    arrived |= exchange(rest, blocks)
+    arrived |= exchange(targets(count), rest, blocks)
     u_turned, u_rows, masks = prepare(u, table, blocks[0], True)
+    late = bases[-1]
+    early = (0, *bases[:-1])
     partial = partial_sum(u_turned, early, pick(arrived, early))
+    first, rest = slot_order(bases[::-1])
     *blocks, stacked = residual_blocks(
         masks, u_rows, u_turned, data[0], partial, late, pick(arrived, (late,)), first
     )
-    returned = exchange(first, blocks)
+    returned = exchange(sources(count), first, blocks)
     blocks = adjoint_blocks(masks, u_rows, stacked, rest)
-    returned |= exchange(rest, blocks)
+    returned |= exchange(sources(count), rest, blocks)
     (v_turned,) = prepare(v, table, stacked, False)
+    late = bases[0]
+    early = (0, *bases[1:])
     partial = partial_sum(v_turned, early, pick(returned, early))
     spectra = []
     for chunk in range(x.shape[2] // LANES):
         blocks = spectrum_blocks(
             v_turned, partial, late, pick(returned, (late,)), freqs, chunk
         )
-        spectra.append([send(b, "freq", k) if k else b for k, b in enumerate(blocks)])
+        spectra.append(
+            [
+                send(b, "freq", [f ^ k for f in range(freqs)]) if k else b
+                for k, b in enumerate(blocks)
+            ]
+        )
     result = None
     for chunk, blocks in enumerate(spectra):
         result = gated_traces(onset, blocks, chunk, result)

time: 61.4 us -> 62.2 us (1.013)
  the two profiles are of different devices: /device:TPU:0 before, /device:TPU:16 now
where the time goes in v1:
time: 62.2 us; the launch traced here: 62.1 us
  starting transfers between devices  31.9 us (51%)
  Pallas kernels  18.4 us (30%)
  waiting for transfers between devices  11.5 us (18%)
    ppermute x20, starting transfers between devices, send(): return lax.ppermute(block, axis, list(enumerate(row)))  31.9 us
    ppermute x20, waiting for transfers between devices, send(): return lax.ppermute(block, axis, list(enumerate(row)))  11.5 us
    pallas_call x2, Pallas kernels, prepare(): pl.pallas_call(functools.partial(prepare_kernel, want_rows), out_shape=ou...  7.99 us
    pallas_call x2, Pallas kernels, partial_sum(): pl.pallas_call(functools.partial(partial_kernel, bases), out_shape=jax.Sh...  2.35 us
    pallas_call x1, Pallas kernels, coeff_first(): pl.pallas_call(functools.partial(coeff_first_kernel, first, rest), out_sh...  2.35 us
    pallas_call x2, Pallas kernels, gated_traces(): pl.pallas_call(functools.partial(traces_kernel, freqs, chunk), out_shape=...  1.94 us
    pallas_call x1, Pallas kernels, coeff_rest(): pl.pallas_call(functools.partial(coeff_rest_kernel, rest), out_shape=[jax...  1.26 us
  transfers between devices with their start and end apart: 20, of which 7 were waited for; matrix products, arithmetic and copies ran while one was open for 0% of the time, Pallas kernels for 20%

profile of v1, /device:TPU:16, one launch (start us, length us, event | category | flops | bytes accessed | tf_op | source)
XLA Modules:
  0.0 62.1 jit_solution(2488192626758853262)
XLA Ops:
  0.0 2.4 %coeff_first.1 = (bf16[96,512]{1,0:T(8,128)(2,1)S(1)}, bf16[96,512]{1,0:T(8,128)(2,1)S(1)}, bf16[2,640,256]{2,1,0:T(8,128)(2,1)S(1)}, bf16[6,96,2,640]{3,2,1,0:T(2,128)(2,1)S(1)}, f32[6,96,128]{2,1,0:T(8,128)S(1)}) custom-call(s32[8,8]{1,0:T(8,128)} %bitcast.6, bf16[8,128,2,640]{3,2,1,0:T(2,128)(2,1)} %bitcast.9, bf16[2,640,256]{2,1,0:T(8,128)(2,1)} %bitcast.12), custom_call_target="tpu_custom_call" | custom-call | flops 1000000000 | bytes 10000000 | tf_op jit(solution)/shard_map/coeff_first/pallas_call | solution.py:125
  2.4 1.3 %coeff_rest.1 = (bf16[96,512]{1,0:T(8,128)(2,1)S(1)}, bf16[96,512]{1,0:T(8,128)(2,1)S(1)}, bf16[96,512]{1,0:T(8,128)(2,1)S(1)}, bf16[96,512]{1,0:T(8,128)(2,1)S(...) custom-call(f32[6,96,128]{2,1,0:T(8,128)S(1)} %get-tuple-element.36.refs_0_, ...), custom_call_target="tpu_custom_call" | custom-call | flops 1000000000 | bytes 10000000 | tf_op jit(solution)/shard_map/coeff_rest/pallas_call | solution.py:153
  3.7 0.5 collective-permute-start.4
  4.3 1.6 %collective-permute-start.3 = (bf16[96,512]{1,0:T(8,128)(2,1)S(1)}, bf16[96,512]{1,0:T(8,128)(2,1)S(1)}, u32[]{:S(2)}, u32[]{:S(2)}) collective-permute-start(bf16[96,512]{1,0:T(8,128)(2,1)S(1)} %get-tuple-element.39.refs_2_), channel_id=1, source_target_pairs={{0,6},{1,7},{2,4},{3,5},{4,2},{5,3},{6,0},{7,1},{8,14},{9,15},{10,... | collective-permute-start | bytes 294920 | tf_op jit(solution)/shard_map/ppermute | solution.py:424
  5.8 2.0 %collective-permute-start.1 = (bf16[96,512]{1,0:T(8,128)(2,1)S(1)}, bf16[96,512]{1,0:T(8,128)(2,1)S(1)}, u32[]{:S(2)}, u32[]{:S(2)}) collective-permute-start(bf16[96,512]{1,0:T(8,128)(2,1)S(1)} %get-tuple-element.45), channel_id=1, source_target_pairs={{0,2},{1,3},{2,6},{3,7},{4,0},{5,1},{6,4},{7,5},{8,10},{9,11},{10,... | collective-permute-start | bytes 294920 | tf_op jit(solution)/shard_map/ppermute | solution.py:424
  7.8 1.5 %collective-permute-start.5 = (bf16[96,512]{1,0:T(8,128)(2,1)S(1)}, bf16[96,512]{1,0:T(8,128)(2,1)S(1)}, u32[]{:S(2)}, u32[]{:S(2)}) collective-permute-start(bf16[96,512]{1,0:T(8,128)(2,1)S(1)} %get-tuple-element.48), channel_id=1, source_target_pairs={{0,4},{1,5},{2,0},{3,1},{4,6},{5,7},{6,2},{7,3},{8,12},{9,13},{10,... | collective-permute-start | bytes 294920 | tf_op jit(solution)/shard_map/ppermute | solution.py:424
  9.3 1.7 %collective-permute-done.4.refs_6_ = bf16[96,512]{1,0:T(8,128)(2,1)S(1)} collective-permute-done((bf16[96,512]{1,0:T(8,128)(2,1)S(1)}, bf16[96,512]{1,0:T(8,128)(2,1)S(1)}, u32[]{:S(2)}, u32[]{:S(2)}) %collective-permute-start.4) | collective-permute-done | bytes 98336 | tf_op jit(solution)/shard_map/ppermute | solution.py:424
  10.9 1.5 %collective-permute-start.6 = (bf16[96,512]{1,0:T(8,128)(2,1)S(1)}, bf16[96,512]{1,0:T(8,128)(2,1)S(1)}, u32[]{:S(2)}, u32[]{:S(2)}) collective-permute-start(bf16[96,512]{1,0:T(8,128)(2,1)S(1)} %get-tuple-element.49), channel_id=1, source_target_pairs={{0,5},{1,4},{2,1},{3,0},{4,7},{5,6},{6,3},{7,2},{8,13},{9,12},{10,... | collective-permute-start | bytes 294920 | tf_op jit(solution)/shard_map/ppermute | solution.py:424
  12.4 4.1 %prepare.2 = (bf16[4,640,384]{2,1,0:T(8,128)(2,1)S(1)}, bf16[768,1280]{1,0:T(8,128)(2,1)S(1)}, f32[8,96,128]{2,1,0:T(8,128)S(1)}) custom-call(bf16[8,128,2,640]{3,2,1,0:T(2,128)(2,1)} %bitcast.11, s32[8,8]{1,0:T(8,128)S(1)} %bitcast.7, bf16[96,512]{1,0:T(8,128)(2,1)S(1)} %get-tuple-element.39.refs_2_), custom_call_target="tpu_custom_call" | custom-call | flops 1000000000 | bytes 10000000 | tf_op jit(solution)/shard_map/prepare/pallas_call | solution.py:214
  16.5 3.4 %collective-permute-done.1.refs_3_ = bf16[96,512]{1,0:T(8,128)(2,1)S(1)} collective-permute-done((bf16[96,512]{1,0:T(8,128)(2,1)S(1)}, bf16[96,512]{1,0:T(8,128)(2,1)S(1)}, u32[]{:S(2)}, u32[]{:S(2)}) %collective-permute-start.1) | collective-permute-done | bytes 98336 | tf_op jit(solution)/shard_map/ppermute | solution.py:424
  20.0 1.6 %collective-permute-done.2.refs_4_ = bf16[96,512]{1,0:T(8,128)(2,1)S(1)} collective-permute-done((bf16[96,512]{1,0:T(8,128)(2,1)S(1)}, bf16[96,512]{1,0:T(8,128)(2,1)S(1)}, u32[]{:S(2)}, u32[]{:S(2)}) %collective-permute-start.2) | collective-permute-done | bytes 98336 | tf_op jit(solution)/shard_map/ppermute | solution.py:424
  21.6 1.2 %partial_sum.2.refs_4_ = f32[640,512]{1,0:T(8,128)S(1)} custom-call(bf16[4,640,384]{2,1,0:T(8,128)(2,1)S(1)} %get-tuple-element.42.refs_0_.refs_2_, bf16[96,512]{1,0:T(8,128)(2,1)S(1)} %get-tuple-element.43.refs_1_, bf16[96,512]{1,0:T(8,128)(2,1)S(1)} %collective-permute-done.refs_2_, bf16[96,512]{1,0:T(8,128)(2,1)S(1)} %collective-permute-done.1.refs_3_, ...), custom_call_target="tpu_custom_call" | custom-call | flops 1000000000 | bytes 10000000 | tf_op jit(solution)/shard_map/partial_sum/pallas_call | solution.py:252
  22.8 0.9 %residual_blocks.1 = (bf16[96,512]{1,0:T(8,128)(2,1)S(1)}, bf16[96,512]{1,0:T(8,128)(2,1)S(1)}, bf16[1280,512]{1,0:T(8,128)(2,1)S(1)}) custom-call(f32[8,96,128]{2,1,0:T(8,128)S(1)} %get-tuple-element.40.refs_0_, bf16[768,1280]{1,0:T(8,128)(2,1)S(1)} %get-tuple-element.41.refs_1_, bf16[4,640,384]{2,1,0:T(8,128)(2,1)S(1)} %get-tuple-element.42.refs_0_.refs_2_, ...), custom_call_target="tpu_custom_call" | custom-call | flops 1000000000 | bytes 10000000 | tf_op jit(solution)/shard_map/residual_blocks/pallas_call | solution.py:292
  23.7 2.8 %collective-permute-start.10 = (bf16[96,512]{1,0:T(8,128)(2,1)S(1)}, bf16[96,512]{1,0:T(8,128)(2,1)S(1)}, u32[]{:S(2)}, u32[]{:S(2)}) collective-permute-start(bf16[96,512]{1,0:T(8,128)(2,1)S(1)} %get-tuple-element.55), channel_id=1, source_target_pairs={{0,2},{1,3},{2,6},{3,7},{4,0},{5,1},{6,4},{7,5},{8,10},{9,11},{10,... | collective-permute-start | bytes 294920 | tf_op jit(solution)/shard_map/ppermute | solution.py:424
  26.6 0.9 %adjoint_blocks.1 = (bf16[96,512]{1,0:T(8,128)(2,1)S(1)}, bf16[96,512]{1,0:T(8,128)(2,1)S(1)}, bf16[96,512]{1,0:T(8,128)(2,1)S(1)}, bf16[96,512]{1,0:T(8,128)(2,...) custom-call(f32[8,96,128]{2,1,0:T(8,128)S(1)} %get-tuple-element.40.refs_0_, ...), custom_call_target="tpu_custom_call" | custom-call | flops 1000000000 | bytes 10000000 | tf_op jit(solution)/shard_map/adjoint_blocks/pallas_call | solution.py:309
  27.9 1.4 %collective-permute-start.8 = (bf16[96,512]{1,0:T(8,128)(2,1)S(1)}, bf16[96,512]{1,0:T(8,128)(2,1)S(1)}, u32[]{:S(2)}, u32[]{:S(2)}) collective-permute-start(bf16[96,512]{1,0:T(8,128)(2,1)S(1)} %get-tuple-element.53), channel_id=1, source_target_pairs={{0,6},{1,7},{2,4},{3,5},{4,2},{5,3},{6,0},{7,1},{8,14},{9,15},{10,... | collective-permute-start | bytes 294920 | tf_op jit(solution)/shard_map/ppermute | solution.py:424
  29.5 0.8 %collective-permute-done.10.refs_5_ = bf16[96,512]{1,0:T(8,128)(2,1)S(1)} collective-permute-done((bf16[96,512]{1,0:T(8,128)(2,1)S(1)}, bf16[96,512]{1,0:T(8,128)(2,1)S(1)}, u32[]{:S(2)}, u32[]{:S(2)}) %collective-permute-start.10) | collective-permute-done | bytes 98336 | tf_op jit(solution)/shard_map/ppermute | solution.py:424
  30.3 2.9 %collective-permute-start.12 = (bf16[96,512]{1,0:T(8,128)(2,1)S(1)}, bf16[96,512]{1,0:T(8,128)(2,1)S(1)}, u32[]{:S(2)}, u32[]{:S(2)}) collective-permute-start(bf16[96,512]{1,0:T(8,128)(2,1)S(1)} %get-tuple-element.57), channel_id=1, source_target_pairs={{0,4},{1,5},{2,0},{3,1},{4,6},{5,7},{6,2},{7,3},{8,12},{9,13},{10,... | collective-permute-start | bytes 294920 | tf_op jit(solution)/shard_map/ppermute | solution.py:424
  33.2 10.0 %collective-permute-start.13 = (bf16[96,512]{1,0:T(8,128)(2,1)S(1)}, bf16[96,512]{1,0:T(8,128)(2,1)S(1)}, u32[]{:S(2)}, u32[]{:S(2)}) collective-permute-start(bf16[96,512]{1,0:T(8,128)(2,1)S(1)} %get-tuple-element.58), channel_id=1, source_target_pairs={{0,5},{1,4},{2,1},{3,0},{4,7},{5,6},{6,3},{7,2},{8,13},{9,12},{10,... | collective-permute-start | bytes 294920 | tf_op jit(solution)/shard_map/ppermute | solution.py:424
  43.1 3.9 %prepare.3.refs_0_ = bf16[4,640,384]{2,1,0:T(8,128)(2,1)S(1)} custom-call(bf16[8,128,2,640]{3,2,1,0:T(2,128)(2,1)} %bitcast.10, s32[8,8]{1,0:T(8,128)S(1)} %bitcast.8, bf16[1280,512]{1,0:T(8,128)(2,1)S(1)} %get-tuple-element.50.refs_2_), custom_call_target="tpu_custom_call" | custom-call | flops 1000000000 | bytes 10000000 | tf_op jit(solution)/shard_map/prepare/pallas_call | solution.py:214
  47.1 1.2 %partial_sum.3.refs_1_ = f32[640,512]{1,0:T(8,128)S(1)} custom-call(bf16[4,640,384]{2,1,0:T(8,128)(2,1)S(1)} %prepare.3.refs_0_, bf16[96,512]{1,0:T(8,128)(2,1)S(1)} %get-tuple-element.51.refs_1_, bf16[96,512]{1,0:T(8,128)(2,1)S(1)} %collective-permute-done.7.refs_2_, bf16[96,512]{1,0:T(8,128)(2,1)S(1)} %collective-permute-done.8.refs_3_, ...), custom_call_target="tpu_custom_call" | custom-call | flops 1000000000 | bytes 10000000 | tf_op jit(solution)/shard_map/partial_sum/pallas_call | solution.py:252
  48.3 0.4 spectrum_blocks.3
  48.7 1.5 %collective-permute-start.17 = (bf16[160,256]{1,0:T(8,128)(2,1)S(1)}, bf16[160,256]{1,0:T(8,128)(2,1)S(1)}, u32[]{:S(2)}, u32[]{:S(2)}) collective-permute-start(bf16[160,256]{1,0:T(8,128)(2,1)S(1)} %get-tuple-element.64), channel_id=1, source_target_pairs={{0,8},{8,0},{16,24},{24,16},{1,9},{9,1},{17,25},{25,17},{2,10},{10... | collective-permute-start | bytes 245768 | tf_op jit(solution)/shard_map/ppermute | solution.py:424
  50.2 1.5 %collective-permute-start.18 = (bf16[160,256]{1,0:T(8,128)(2,1)S(1)}, bf16[160,256]{1,0:T(8,128)(2,1)S(1)}, u32[]{:S(2)}, u32[]{:S(2)}) collective-permute-start(bf16[160,256]{1,0:T(8,128)(2,1)S(1)} %get-tuple-element.65), channel_id=1, source_target_pairs={{0,16},{8,24},{16,0},{24,8},{1,17},{9,25},{17,1},{25,9},{2,18},{10... | collective-permute-start | bytes 245768 | tf_op jit(solution)/shard_map/ppermute | solution.py:424
  51.8 0.5 collective-permute-start.19
  52.6 1.5 %collective-permute-start.14 = (bf16[160,256]{1,0:T(8,128)(2,1)S(1)}, bf16[160,256]{1,0:T(8,128)(2,1)S(1)}, u32[]{:S(2)}, u32[]{:S(2)}) collective-permute-start(bf16[160,256]{1,0:T(8,128)(2,1)S(1)} %get-tuple-element.60), channel_id=1, source_target_pairs={{0,8},{8,0},{16,24},{24,16},{1,9},{9,1},{17,25},{25,17},{2,10},{10... | collective-permute-start | bytes 245768 | tf_op jit(solution)/shard_map/ppermute | solution.py:424
  54.2 1.6 %collective-permute-start.15 = (bf16[160,256]{1,0:T(8,128)(2,1)S(1)}, bf16[160,256]{1,0:T(8,128)(2,1)S(1)}, u32[]{:S(2)}, u32[]{:S(2)}) collective-permute-start(bf16[160,256]{1,0:T(8,128)(2,1)S(1)} %get-tuple-element.61), channel_id=1, source_target_pairs={{0,16},{8,24},{16,0},{24,8},{1,17},{9,25},{17,1},{25,9},{2,18},{10... | collective-permute-start | bytes 245768 | tf_op jit(solution)/shard_map/ppermute | solution.py:424
  55.7 0.5 collective-permute-start.16
  56.2 1.6 %collective-permute-done.19.refs_4_ = bf16[160,256]{1,0:T(8,128)(2,1)S(1)} collective-permute-done((bf16[160,256]{1,0:T(8,128)(2,1)S(1)}, bf16[160,256]{1,0:T(8,128)(2,1)S(1)}, u32[]{:S(2)}, u32[]{:S(2)}) %collective-permute-start.19) | collective-permute-done | bytes 81952 | tf_op jit(solution)/shard_map/ppermute | solution.py:424
  57.8 1.0 %gated_traces.2.refs_5_ = f32[8,160,256]{2,1,0:T(8,128)} custom-call(s32[160,256]{1,0:T(8,128)S(1)} %copy-done.1, bf16[160,256]{1,0:T(8,128)(2,1)S(1)} %get-tuple-element.63.refs_1_, bf16[160,256]{1,0:T(8,128)(2,1)S(1)} %collective-permute-done.17.refs_2_, bf16[160,256]{1,0:T(8,128)(2,1)S(1)} %collective-permute-done.18.refs_3_, ...), custom_call_target="tpu_custom_call" | custom-call | flops 500000000 | bytes 10000000 | tf_op jit(solution)/shard_map/gated_traces/pallas_call | solution.py:406
  58.9 2.2 %collective-permute-done.16.refs_4_ = bf16[160,256]{1,0:T(8,128)(2,1)S(1)} collective-permute-done((bf16[160,256]{1,0:T(8,128)(2,1)S(1)}, bf16[160,256]{1,0:T(8,128)(2,1)S(1)}, u32[]{:S(2)}, u32[]{:S(2)}) %collective-permute-start.16) | collective-permute-done | bytes 81952 | tf_op jit(solution)/shard_map/ppermute | solution.py:424
  61.1 1.0 %gated_traces.3 = f32[8,160,256]{2,1,0:T(8,128)} custom-call(s32[160,256]{1,0:T(8,128)S(1)} %copy-done.1, bf16[160,256]{1,0:T(8,128)(2,1)S(1)} %get-tuple-element.59.refs_1_, bf16[160,256]{1,0:T(8,128)(2,1)S(1)} %collective-permute-done.14.refs_2_, bf16[160,256]{1,0:T(8,128)(2,1)S(1)} %collective-permute-done.15.refs_3_, ...), custom_call_target="tpu_custom_call", output_to_operand_aliasing={{}: (5, {})} | custom-call | flops 500000000 | bytes 10000000 | tf_op jit(solution)/shard_map/gated_traces/pallas_call | solution.py:406
  (26 shorter events, 1.3 us)
Async XLA Ops:
  2.4 10.1 %copy-start.2 = (s32[1,8,8]{2,1,0:T(8,128)S(1)}, s32[1,8,8]{2,1,0:T(8,128)}, u32[]{:S(2)}) copy-start(s32[1,8,8]{2,1,0:T(8,128)} %param.10) | copy-start | bytes 772
  3.6 4.2 %collective-permute-start = (bf16[96,512]{1,0:T(8,128)(2,1)S(1)}, bf16[96,512]{1,0:T(8,128)(2,1)S(1)}, u32[]{:S(2)}, u32[]{:S(2)}) collective-permute-start(bf16[96,512]{1,0:T(8,128)(2,1)S(1)} %get-tuple-element.44), channel_id=1, source_target_pairs={{0,1},{1,0},{2,3},{3,2},{4,5},{5,4},{6,7},{7,6},{8,9},{9,8},{10,11... | collective-permute-start | bytes 294920 | tf_op jit(solution)/shard_map/ppermute | solution.py:424
  3.7 7.2 %collective-permute-start.4 = (bf16[96,512]{1,0:T(8,128)(2,1)S(1)}, bf16[96,512]{1,0:T(8,128)(2,1)S(1)}, u32[]{:S(2)}, u32[]{:S(2)}) collective-permute-start(bf16[96,512]{1,0:T(8,128)(2,1)S(1)} %get-tuple-element.47), channel_id=1, source_target_pairs={{0,7},{1,6},{2,5},{3,4},{4,3},{5,2},{6,1},{7,0},{8,15},{9,14},{10,... | collective-permute-start | bytes 294920 | tf_op jit(solution)/shard_map/ppermute | solution.py:424
  4.3 12.2 %collective-permute-start.3 = (bf16[96,512]{1,0:T(8,128)(2,1)S(1)}, bf16[96,512]{1,0:T(8,128)(2,1)S(1)}, u32[]{:S(2)}, u32[]{:S(2)}) collective-permute-start(bf16[96,512]{1,0:T(8,128)(2,1)S(1)} %get-tuple-element.39.refs_2_), channel_id=1, source_target_pairs={{0,6},{1,7},{2,4},{3,5},{4,2},{5,3},{6,0},{7,1},{8,14},{9,15},{10,... | collective-permute-start | bytes 294920 | tf_op jit(solution)/shard_map/ppermute | solution.py:424
  5.8 14.1 %collective-permute-start.1 = (bf16[96,512]{1,0:T(8,128)(2,1)S(1)}, bf16[96,512]{1,0:T(8,128)(2,1)S(1)}, u32[]{:S(2)}, u32[]{:S(2)}) collective-permute-start(bf16[96,512]{1,0:T(8,128)(2,1)S(1)} %get-tuple-element.45), channel_id=1, source_target_pairs={{0,2},{1,3},{2,6},{3,7},{4,0},{5,1},{6,4},{7,5},{8,10},{9,11},{10,... | collective-permute-start | bytes 294920 | tf_op jit(solution)/shard_map/ppermute | solution.py:424
  7.8 13.8 %collective-permute-start.2 = (bf16[96,512]{1,0:T(8,128)(2,1)S(1)}, bf16[96,512]{1,0:T(8,128)(2,1)S(1)}, u32[]{:S(2)}, u32[]{:S(2)}) collective-permute-start(bf16[96,512]{1,0:T(8,128)(2,1)S(1)} %get-tuple-element.46), channel_id=1, source_target_pairs={{0,3},{1,2},{2,7},{3,6},{4,1},{5,0},{6,5},{7,4},{8,11},{9,10},{10,... | collective-permute-start | bytes 294920 | tf_op jit(solution)/shard_map/ppermute | solution.py:424
  7.8 15.0 %collective-permute-start.5 = (bf16[96,512]{1,0:T(8,128)(2,1)S(1)}, bf16[96,512]{1,0:T(8,128)(2,1)S(1)}, u32[]{:S(2)}, u32[]{:S(2)}) collective-permute-start(bf16[96,512]{1,0:T(8,128)(2,1)S(1)} %get-tuple-element.48), channel_id=1, source_target_pairs={{0,4},{1,5},{2,0},{3,1},{4,6},{5,7},{6,2},{7,3},{8,12},{9,13},{10,... | collective-permute-start | bytes 294920 | tf_op jit(solution)/shard_map/ppermute | solution.py:424
  10.9 11.8 %collective-permute-start.6 = (bf16[96,512]{1,0:T(8,128)(2,1)S(1)}, bf16[96,512]{1,0:T(8,128)(2,1)S(1)}, u32[]{:S(2)}, u32[]{:S(2)}) collective-permute-start(bf16[96,512]{1,0:T(8,128)(2,1)S(1)} %get-tuple-element.49), channel_id=1, source_target_pairs={{0,5},{1,4},{2,1},{3,0},{4,7},{5,6},{6,3},{7,2},{8,13},{9,12},{10,... | collective-permute-start | bytes 294920 | tf_op jit(solution)/shard_map/ppermute | solution.py:424
  21.6 1.2 %copy-start = (bf16[1,2,640,256]{3,2,1,0:T(8,128)(2,1)S(1)}, bf16[1,2,640,256]{3,2,1,0:T(8,128)(2,1)}, u32[]{:S(2)}) copy-start(bf16[1,2,640,256]{3,2,1,0:T(8,128)(2,1)} %param.7) | copy-start | bytes 1966084
  23.7 6.6 %collective-permute-start.10 = (bf16[96,512]{1,0:T(8,128)(2,1)S(1)}, bf16[96,512]{1,0:T(8,128)(2,1)S(1)}, u32[]{:S(2)}, u32[]{:S(2)}) collective-permute-start(bf16[96,512]{1,0:T(8,128)(2,1)S(1)} %get-tuple-element.55), channel_id=1, source_target_pairs={{0,2},{1,3},{2,6},{3,7},{4,0},{5,1},{6,4},{7,5},{8,10},{9,11},{10,... | collective-permute-start | bytes 294920 | tf_op jit(solution)/shard_map/ppermute | solution.py:424
  26.5 6.7 %collective-permute-start.11 = (bf16[96,512]{1,0:T(8,128)(2,1)S(1)}, bf16[96,512]{1,0:T(8,128)(2,1)S(1)}, u32[]{:S(2)}, u32[]{:S(2)}) collective-permute-start(bf16[96,512]{1,0:T(8,128)(2,1)S(1)} %get-tuple-element.56), channel_id=1, source_target_pairs={{0,3},{1,2},{2,7},{3,6},{4,1},{5,0},{6,5},{7,4},{8,11},{9,10},{10,... | collective-permute-start | bytes 294920 | tf_op jit(solution)/shard_map/ppermute | solution.py:424
  27.5 19.5 %collective-permute-start.7 = (bf16[96,512]{1,0:T(8,128)(2,1)S(1)}, bf16[96,512]{1,0:T(8,128)(2,1)S(1)}, u32[]{:S(2)}, u32[]{:S(2)}) collective-permute-start(bf16[96,512]{1,0:T(8,128)(2,1)S(1)} %get-tuple-element.52), channel_id=1, source_target_pairs={{0,1},{1,0},{2,3},{3,2},{4,5},{5,4},{6,7},{7,6},{8,9},{9,8},{10,11... | collective-permute-start | bytes 294920 | tf_op jit(solution)/shard_map/ppermute | solution.py:424
  27.9 19.2 %collective-permute-start.8 = (bf16[96,512]{1,0:T(8,128)(2,1)S(1)}, bf16[96,512]{1,0:T(8,128)(2,1)S(1)}, u32[]{:S(2)}, u32[]{:S(2)}) collective-permute-start(bf16[96,512]{1,0:T(8,128)(2,1)S(1)} %get-tuple-element.53), channel_id=1, source_target_pairs={{0,6},{1,7},{2,4},{3,5},{4,2},{5,3},{6,0},{7,1},{8,14},{9,15},{10,... | collective-permute-start | bytes 294920 | tf_op jit(solution)/shard_map/ppermute | solution.py:424
  29.3 17.8 %collective-permute-start.9 = (bf16[96,512]{1,0:T(8,128)(2,1)S(1)}, bf16[96,512]{1,0:T(8,128)(2,1)S(1)}, u32[]{:S(2)}, u32[]{:S(2)}) collective-permute-start(bf16[96,512]{1,0:T(8,128)(2,1)S(1)} %get-tuple-element.54), channel_id=1, source_target_pairs={{0,7},{1,6},{2,5},{3,4},{4,3},{5,2},{6,1},{7,0},{8,15},{9,14},{10,... | collective-permute-start | bytes 294920 | tf_op jit(solution)/shard_map/ppermute | solution.py:424
  30.3 18.0 %collective-permute-start.12 = (bf16[96,512]{1,0:T(8,128)(2,1)S(1)}, bf16[96,512]{1,0:T(8,128)(2,1)S(1)}, u32[]{:S(2)}, u32[]{:S(2)}) collective-permute-start(bf16[96,512]{1,0:T(8,128)(2,1)S(1)} %get-tuple-element.57), channel_id=1, source_target_pairs={{0,4},{1,5},{2,0},{3,1},{4,6},{5,7},{6,2},{7,3},{8,12},{9,13},{10,... | collective-permute-start | bytes 294920 | tf_op jit(solution)/shard_map/ppermute | solution.py:424
  33.2 15.1 %collective-permute-start.13 = (bf16[96,512]{1,0:T(8,128)(2,1)S(1)}, bf16[96,512]{1,0:T(8,128)(2,1)S(1)}, u32[]{:S(2)}, u32[]{:S(2)}) collective-permute-start(bf16[96,512]{1,0:T(8,128)(2,1)S(1)} %get-tuple-element.58), channel_id=1, source_target_pairs={{0,5},{1,4},{2,1},{3,0},{4,7},{5,6},{6,3},{7,2},{8,13},{9,12},{10,... | collective-permute-start | bytes 294920 | tf_op jit(solution)/shard_map/ppermute | solution.py:424
  48.7 7.0 %collective-permute-start.17 = (bf16[160,256]{1,0:T(8,128)(2,1)S(1)}, bf16[160,256]{1,0:T(8,128)(2,1)S(1)}, u32[]{:S(2)}, u32[]{:S(2)}) collective-permute-start(bf16[160,256]{1,0:T(8,128)(2,1)S(1)} %get-tuple-element.64), channel_id=1, source_target_pairs={{0,8},{8,0},{16,24},{24,16},{1,9},{9,1},{17,25},{25,17},{2,10},{10... | collective-permute-start | bytes 245768 | tf_op jit(solution)/shard_map/ppermute | solution.py:424
  50.2 6.0 %collective-permute-start.18 = (bf16[160,256]{1,0:T(8,128)(2,1)S(1)}, bf16[160,256]{1,0:T(8,128)(2,1)S(1)}, u32[]{:S(2)}, u32[]{:S(2)}) collective-permute-start(bf16[160,256]{1,0:T(8,128)(2,1)S(1)} %get-tuple-element.65), channel_id=1, source_target_pairs={{0,16},{8,24},{16,0},{24,8},{1,17},{9,25},{17,1},{25,9},{2,18},{10... | collective-permute-start | bytes 245768 | tf_op jit(solution)/shard_map/ppermute | solution.py:424
  51.8 6.0 %copy-start.1 = (s32[160,256]{1,0:T(8,128)S(1)}, s32[160,256]{1,0:T(8,128)}, u32[]{:S(2)}) copy-start(s32[160,256]{1,0:T(8,128)} %refs_0_.3) | copy-start | bytes 491524
  51.8 6.0 %collective-permute-start.19 = (bf16[160,256]{1,0:T(8,128)(2,1)S(1)}, bf16[160,256]{1,0:T(8,128)(2,1)S(1)}, u32[]{:S(2)}, u32[]{:S(2)}) collective-permute-start(bf16[160,256]{1,0:T(8,128)(2,1)S(1)} %get-tuple-element.66), channel_id=1, source_target_pairs={{0,24},{8,16},{16,8},{24,0},{1,25},{9,17},{17,9},{25,1},{2,26},{10... | collective-permute-start | bytes 245768 | tf_op jit(solution)/shard_map/ppermute | solution.py:424
  52.6 6.1 %collective-permute-start.14 = (bf16[160,256]{1,0:T(8,128)(2,1)S(1)}, bf16[160,256]{1,0:T(8,128)(2,1)S(1)}, u32[]{:S(2)}, u32[]{:S(2)}) collective-permute-start(bf16[160,256]{1,0:T(8,128)(2,1)S(1)} %get-tuple-element.60), channel_id=1, source_target_pairs={{0,8},{8,0},{16,24},{24,16},{1,9},{9,1},{17,25},{25,17},{2,10},{10... | collective-permute-start | bytes 245768 | tf_op jit(solution)/shard_map/ppermute | solution.py:424
  54.2 4.7 %collective-permute-start.15 = (bf16[160,256]{1,0:T(8,128)(2,1)S(1)}, bf16[160,256]{1,0:T(8,128)(2,1)S(1)}, u32[]{:S(2)}, u32[]{:S(2)}) collective-permute-start(bf16[160,256]{1,0:T(8,128)(2,1)S(1)} %get-tuple-element.61), channel_id=1, source_target_pairs={{0,16},{8,24},{16,0},{24,8},{1,17},{9,25},{17,1},{25,9},{2,18},{10... | collective-permute-start | bytes 245768 | tf_op jit(solution)/shard_map/ppermute | solution.py:424
  55.7 5.3 %collective-permute-start.16 = (bf16[160,256]{1,0:T(8,128)(2,1)S(1)}, bf16[160,256]{1,0:T(8,128)(2,1)S(1)}, u32[]{:S(2)}, u32[]{:S(2)}) collective-permute-start(bf16[160,256]{1,0:T(8,128)(2,1)S(1)} %get-tuple-element.62), channel_id=1, source_target_pairs={{0,24},{8,16},{16,8},{24,0},{1,25},{9,17},{17,9},{25,1},{2,26},{10... | collective-permute-start | bytes 245768 | tf_op jit(solution)/shard_map/ppermute | solution.py:424

commit v2 on v0

--- a/solution.py
+++ b/solution.py
@@ -21,6 +21,19 @@
 
 def params():
     return pltpu.CompilerParams(vmem_limit_bytes=20 * 1024 * 1024)
+
+
+def swapped(k, freqs):
+    bits = freqs.bit_length() - 1
+    if bits % 2:
+        return k
+    half = bits // 2
+    return (k % (1 << half) << half) | (k >> half)
+
+
+def freq_peer(k, freqs):
+    turn = jnp.where(lax.axis_index("tile") % 2 == 0, k, swapped(k, freqs))
+    return lax.axis_index("freq") ^ turn
 
 
 def level_mask(rank):
@@ -294,7 +307,6 @@
     pair = refs[2:4]
     outs = refs[4 : 4 + freqs]
     spectrum = refs[4 + freqs]
-    mine = lax.axis_index("freq")
     virtual = partial_ref.shape[1] // 2
     real = slice(chunk * LANES, (chunk + 1) * LANES)
     imag = slice(virtual + chunk * LANES, virtual + (chunk + 1) * LANES)
@@ -307,7 +319,7 @@
     spectrum[:, LANES:] = partial_ref[:, imag] + late[:, LANES:]
     share = outs[0].shape[0]
     for k in range(freqs):
-        rows = pl.ds(pl.multiple_of((mine ^ k) * share, 8), share)
+        rows = pl.ds(pl.multiple_of(freq_peer(k, freqs) * share, 8), share)
         outs[k][...] = spectrum[rows, :].astype(BF16)
 
 
@@ -331,9 +343,8 @@
     onset_ref = refs[0]
     blocks = refs[1 : 1 + freqs]
     out_hbm, gathered, traces, sems = refs[-4:]
-    mine = lax.axis_index("freq")
     for k in range(freqs):
-        gathered[mine ^ k] = blocks[k][...]
+        gathered[freq_peer(k, freqs)] = blocks[k][...]
     times = 2 * freqs
     scaling = 1.0 / math.sqrt(freqs)
     lanes = pl.ds(chunk * LANES, LANES)
@@ -397,6 +408,17 @@
     return lax.ppermute(block, axis, [(i, i ^ k) for i in range(count)])
 
 
+def send_freq(block, k):
+    count = lax.axis_size("tile")
+    freqs = lax.axis_size("freq")
+    pairs = [
+        (f * count + tile, (f ^ (swapped(k, freqs) if tile % 2 else k)) * count + tile)
+        for f in range(freqs)
+        for tile in range(count)
+    ]
+    return lax.ppermute(block, ("freq", "tile"), pairs)
+
+
 def exchange(ks, blocks):
     return {k: send(b, "tile", k) if k else b for k, b in zip(ks, blocks)}
 
@@ -448,7 +470,7 @@
         blocks = spectrum_blocks(
             v_turned, partial, late, pick(returned, (late,)), freqs, chunk
         )
-        spectra.append([send(b, "freq", k) if k else b for k, b in enumerate(blocks)])
+        spectra.append([send_freq(b, k) if k else b for k, b in enumerate(blocks)])
     result = None
     for chunk, blocks in enumerate(spectra):
         result = gated_traces(onset, blocks, chunk, result)

time: 61.4 us -> 61.4 us (level)
    ppermute x20 -> x14, starting transfers between devices: 25.6 us -> 18.2 us  [send(): return lax.ppermute(block, axis, [(i, i ^ k) for i in range(count)])]
    ppermute x0 -> x6, starting transfers between devices: none -> 7.36 us  [send_freq(): return lax.ppermute(block, ('freq', 'tile'), pairs)]
    ppermute x0 -> x6, waiting for transfers between devices: none -> 3.65 us  [send_freq(): return lax.ppermute(block, ('freq', 'tile'), pairs)]
    ppermute x20 -> x14, waiting for transfers between devices: 17 us -> 13.4 us  [send(): return lax.ppermute(block, axis, [(i, i ^ k) for i in range(count)])]
  transfers between devices with their start and end apart: 20 -> 20, of which waited for: 9 -> 10; matrix products, arithmetic and copies ran while one was open for 0% -> 0% of each run, Pallas kernels for 21% -> 21%
where the time goes in v2:
time: 61.4 us; the launch traced here: 61.2 us
  starting transfers between devices  25.6 us (42%)
  Pallas kernels  18.4 us (30%)
  waiting for transfers between devices  17.1 us (28%)
    ppermute x14, starting transfers between devices, send(): return lax.ppermute(block, axis, [(i, i ^ k) for i in range(count)])  18.2 us
    ppermute x14, waiting for transfers between devices, send(): return lax.ppermute(block, axis, [(i, i ^ k) for i in range(count)])  13.4 us
    pallas_call x2, Pallas kernels, prepare(): pl.pallas_call(functools.partial(prepare_kernel, want_rows), out_shape=ou...  7.97 us
    ppermute x6, starting transfers between devices, send_freq(): return lax.ppermute(block, ('freq', 'tile'), pairs)  7.36 us
    ppermute x6, waiting for transfers between devices, send_freq(): return lax.ppermute(block, ('freq', 'tile'), pairs)  3.65 us
    pallas_call x2, Pallas kernels, partial_sum(): pl.pallas_call(functools.partial(partial_kernel, bases), out_shape=jax.Sh...  2.35 us
    pallas_call x1, Pallas kernels, coeff_first(): pl.pallas_call(functools.partial(coeff_first_kernel, first, rest), out_sh...  2.35 us
    pallas_call x2, Pallas kernels, gated_traces(): pl.pallas_call(functools.partial(traces_kernel, freqs, chunk), out_shape=...  1.94 us
  transfers between devices with their start and end apart: 20, of which 10 were waited for; matrix products, arithmetic and copies ran while one was open for 0% of the time, Pallas kernels for 21%

profile of v2, /device:TPU:0, one launch (start us, length us, event | category | flops | bytes accessed | tf_op | source)
XLA Modules:
  0.0 61.2 jit_solution(8590332103626152063)
XLA Ops:
  0.0 2.4 %coeff_first.1 = (bf16[96,512]{1,0:T(8,128)(2,1)S(1)}, bf16[96,512]{1,0:T(8,128)(2,1)S(1)}, bf16[2,640,256]{2,1,0:T(8,128)(2,1)S(1)}, bf16[6,96,2,640]{3,2,1,0:T(2,128)(2,1)S(1)}, f32[6,96,128]{2,1,0:T(8,128)S(1)}) custom-call(s32[8,8]{1,0:T(8,128)} %bitcast.6, bf16[8,128,2,640]{3,2,1,0:T(2,128)(2,1)} %bitcast.9, bf16[2,640,256]{2,1,0:T(8,128)(2,1)} %bitcast.12), custom_call_target="tpu_custom_call" | custom-call | flops 1000000000 | bytes 10000000 | tf_op jit(solution)/shard_map/coeff_first/pallas_call | solution.py:112
  2.4 1.3 %coeff_rest.1 = (bf16[96,512]{1,0:T(8,128)(2,1)S(1)}, bf16[96,512]{1,0:T(8,128)(2,1)S(1)}, bf16[96,512]{1,0:T(8,128)(2,1)S(1)}, bf16[96,512]{1,0:T(8,128)(2,1)S(...) custom-call(f32[6,96,128]{2,1,0:T(8,128)S(1)} %get-tuple-element.36.refs_0_, ...), custom_call_target="tpu_custom_call" | custom-call | flops 1000000000 | bytes 10000000 | tf_op jit(solution)/shard_map/coeff_rest/pallas_call | solution.py:140
  3.6 3.1 %collective-permute-start.2 = (bf16[96,512]{1,0:T(8,128)(2,1)S(1)}, bf16[96,512]{1,0:T(8,128)(2,1)S(1)}, u32[]{:S(2)}, u32[]{:S(2)}) collective-permute-start(bf16[96,512]{1,0:T(8,128)(2,1)S(1)} %get-tuple-element.45), channel_id=1, source_target_pairs={{0,2},{1,3},{2,0},{3,1},{4,6},{5,7},{6,4},{7,5},{8,10},{9,11},{10,... | collective-permute-start | bytes 294920 | tf_op jit(solution)/shard_map/ppermute | solution.py:408
  7.0 4.0 %collective-permute-start = (bf16[96,512]{1,0:T(8,128)(2,1)S(1)}, bf16[96,512]{1,0:T(8,128)(2,1)S(1)}, u32[]{:S(2)}, u32[]{:S(2)}) collective-permute-start(bf16[96,512]{1,0:T(8,128)(2,1)S(1)} %get-tuple-element.43), channel_id=1, source_target_pairs={{0,6},{1,7},{2,4},{3,5},{4,2},{5,3},{6,0},{7,1},{8,14},{9,15},{10,... | collective-permute-start | bytes 294920 | tf_op jit(solution)/shard_map/ppermute | solution.py:408
  10.9 0.7 %collective-permute-start.6 = (bf16[96,512]{1,0:T(8,128)(2,1)S(1)}, bf16[96,512]{1,0:T(8,128)(2,1)S(1)}, u32[]{:S(2)}, u32[]{:S(2)}) collective-permute-start(bf16[96,512]{1,0:T(8,128)(2,1)S(1)} %get-tuple-element.49), channel_id=1, source_target_pairs={{0,5},{1,4},{2,7},{3,6},{4,1},{5,0},{6,3},{7,2},{8,13},{9,12},{10,... | collective-permute-start | bytes 294920 | tf_op jit(solution)/shard_map/ppermute | solution.py:408
  11.7 2.8 %collective-permute-start.5 = (bf16[96,512]{1,0:T(8,128)(2,1)S(1)}, bf16[96,512]{1,0:T(8,128)(2,1)S(1)}, u32[]{:S(2)}, u32[]{:S(2)}) collective-permute-start(bf16[96,512]{1,0:T(8,128)(2,1)S(1)} %get-tuple-element.39.refs_2_), channel_id=1, source_target_pairs={{0,4},{1,5},{2,6},{3,7},{4,0},{5,1},{6,2},{7,3},{8,12},{9,13},{10,... | collective-permute-start | bytes 294920 | tf_op jit(solution)/shard_map/ppermute | solution.py:408
  14.4 4.1 %prepare.2 = (bf16[4,640,384]{2,1,0:T(8,128)(2,1)S(1)}, bf16[768,1280]{1,0:T(8,128)(2,1)S(1)}, f32[8,96,128]{2,1,0:T(8,128)S(1)}) custom-call(bf16[8,128,2,640]{3,2,1,0:T(2,128)(2,1)} %bitcast.11, s32[8,8]{1,0:T(8,128)S(1)} %bitcast.7, bf16[96,512]{1,0:T(8,128)(2,1)S(1)} %get-tuple-element.39.refs_2_), custom_call_target="tpu_custom_call" | custom-call | flops 1000000000 | bytes 10000000 | tf_op jit(solution)/shard_map/prepare/pallas_call | solution.py:199
  18.6 1.2 %partial_sum.2.refs_4_ = f32[640,512]{1,0:T(8,128)S(1)} custom-call(bf16[4,640,384]{2,1,0:T(8,128)(2,1)S(1)} %get-tuple-element.42.refs_0_.refs_2_, bf16[96,512]{1,0:T(8,128)(2,1)S(1)} %collective-permute-done.refs_1_, bf16[96,512]{1,0:T(8,128)(2,1)S(1)} %collective-permute-done.1.refs_2_, bf16[96,512]{1,0:T(8,128)(2,1)S(1)} %collective-permute-done.2.refs_3_, ...), custom_call_target="tpu_custom_call" | custom-call | flops 1000000000 | bytes 10000000 | tf_op jit(solution)/shard_map/partial_sum/pallas_call | solution.py:237
  19.7 5.8 %collective-permute-done.6.refs_6_ = bf16[96,512]{1,0:T(8,128)(2,1)S(1)} collective-permute-done((bf16[96,512]{1,0:T(8,128)(2,1)S(1)}, bf16[96,512]{1,0:T(8,128)(2,1)S(1)}, u32[]{:S(2)}, u32[]{:S(2)}) %collective-permute-start.6) | collective-permute-done | bytes 98336 | tf_op jit(solution)/shard_map/ppermute | solution.py:408
  25.5 2.2 %collective-permute-done.5.refs_5_ = bf16[96,512]{1,0:T(8,128)(2,1)S(1)} collective-permute-done((bf16[96,512]{1,0:T(8,128)(2,1)S(1)}, bf16[96,512]{1,0:T(8,128)(2,1)S(1)}, u32[]{:S(2)}, u32[]{:S(2)}) %collective-permute-start.5) | collective-permute-done | bytes 98336 | tf_op jit(solution)/shard_map/ppermute | solution.py:408
  27.8 0.9 %residual_blocks.1 = (bf16[96,512]{1,0:T(8,128)(2,1)S(1)}, bf16[96,512]{1,0:T(8,128)(2,1)S(1)}, bf16[1280,512]{1,0:T(8,128)(2,1)S(1)}) custom-call(f32[8,96,128]{2,1,0:T(8,128)S(1)} %get-tuple-element.40.refs_0_, bf16[768,1280]{1,0:T(8,128)(2,1)S(1)} %get-tuple-element.41.refs_1_, bf16[4,640,384]{2,1,0:T(8,128)(2,1)S(1)} %get-tuple-element.42.refs_0_.refs_2_, ...), custom_call_target="tpu_custom_call" | custom-call | flops 1000000000 | bytes 10000000 | tf_op jit(solution)/shard_map/residual_blocks/pallas_call | solution.py:277
  28.6 2.5 %collective-permute-start.7 = (bf16[96,512]{1,0:T(8,128)(2,1)S(1)}, bf16[96,512]{1,0:T(8,128)(2,1)S(1)}, u32[]{:S(2)}, u32[]{:S(2)}) collective-permute-start(bf16[96,512]{1,0:T(8,128)(2,1)S(1)} %get-tuple-element.51), channel_id=1, source_target_pairs={{0,6},{1,7},{2,4},{3,5},{4,2},{5,3},{6,0},{7,1},{8,14},{9,15},{10,... | collective-permute-start | bytes 294920 | tf_op jit(solution)/shard_map/ppermute | solution.py:408
  31.2 0.7 %collective-permute-start.8 = (bf16[96,512]{1,0:T(8,128)(2,1)S(1)}, bf16[96,512]{1,0:T(8,128)(2,1)S(1)}, u32[]{:S(2)}, u32[]{:S(2)}) collective-permute-start(bf16[96,512]{1,0:T(8,128)(2,1)S(1)} %get-tuple-element.52), channel_id=1, source_target_pairs={{0,7},{1,6},{2,5},{3,4},{4,3},{5,2},{6,1},{7,0},{8,15},{9,14},{10,... | collective-permute-start | bytes 294920 | tf_op jit(solution)/shard_map/ppermute | solution.py:408
  31.8 0.9 %adjoint_blocks.1 = (bf16[96,512]{1,0:T(8,128)(2,1)S(1)}, bf16[96,512]{1,0:T(8,128)(2,1)S(1)}, bf16[96,512]{1,0:T(8,128)(2,1)S(1)}, bf16[96,512]{1,0:T(8,128)(2,...) custom-call(f32[8,96,128]{2,1,0:T(8,128)S(1)} %get-tuple-element.40.refs_0_, ...), custom_call_target="tpu_custom_call" | custom-call | flops 1000000000 | bytes 10000000 | tf_op jit(solution)/shard_map/adjoint_blocks/pallas_call | solution.py:294
  32.8 2.1 %collective-permute-start.10 = (bf16[96,512]{1,0:T(8,128)(2,1)S(1)}, bf16[96,512]{1,0:T(8,128)(2,1)S(1)}, u32[]{:S(2)}, u32[]{:S(2)}) collective-permute-start(bf16[96,512]{1,0:T(8,128)(2,1)S(1)} %get-tuple-element.54), channel_id=1, source_target_pairs={{0,3},{1,2},{2,1},{3,0},{4,7},{5,6},{6,5},{7,4},{8,11},{9,10},{10,... | collective-permute-start | bytes 294920 | tf_op jit(solution)/shard_map/ppermute | solution.py:408
  35.3 1.1 %collective-permute-start.12 = (bf16[96,512]{1,0:T(8,128)(2,1)S(1)}, bf16[96,512]{1,0:T(8,128)(2,1)S(1)}, u32[]{:S(2)}, u32[]{:S(2)}) collective-permute-start(bf16[96,512]{1,0:T(8,128)(2,1)S(1)} %get-tuple-element.57), channel_id=1, source_target_pairs={{0,4},{1,5},{2,6},{3,7},{4,0},{5,1},{6,2},{7,3},{8,12},{9,13},{10,... | collective-permute-start | bytes 294920 | tf_op jit(solution)/shard_map/ppermute | solution.py:408
  36.4 1.7 %collective-permute-done.8.refs_2_ = bf16[96,512]{1,0:T(8,128)(2,1)S(1)} collective-permute-done((bf16[96,512]{1,0:T(8,128)(2,1)S(1)}, bf16[96,512]{1,0:T(8,128)(2,1)S(1)}, u32[]{:S(2)}, u32[]{:S(2)}) %collective-permute-start.8) | collective-permute-done | bytes 98336 | tf_op jit(solution)/shard_map/ppermute | solution.py:408
  38.1 0.9 %collective-permute-start.13 = (bf16[96,512]{1,0:T(8,128)(2,1)S(1)}, bf16[96,512]{1,0:T(8,128)(2,1)S(1)}, u32[]{:S(2)}, u32[]{:S(2)}) collective-permute-start(bf16[96,512]{1,0:T(8,128)(2,1)S(1)} %get-tuple-element.58), channel_id=1, source_target_pairs={{0,5},{1,4},{2,7},{3,6},{4,1},{5,0},{6,3},{7,2},{8,13},{9,12},{10,... | collective-permute-start | bytes 294920 | tf_op jit(solution)/shard_map/ppermute | solution.py:408
  39.0 3.9 %prepare.3.refs_0_ = bf16[4,640,384]{2,1,0:T(8,128)(2,1)S(1)} custom-call(bf16[8,128,2,640]{3,2,1,0:T(2,128)(2,1)} %bitcast.10, s32[8,8]{1,0:T(8,128)S(1)} %bitcast.8, bf16[1280,512]{1,0:T(8,128)(2,1)S(1)} %get-tuple-element.50.refs_2_), custom_call_target="tpu_custom_call" | custom-call | flops 1000000000 | bytes 10000000 | tf_op jit(solution)/shard_map/prepare/pallas_call | solution.py:199
  42.9 1.3 %collective-permute-done.10.refs_4_ = bf16[96,512]{1,0:T(8,128)(2,1)S(1)} collective-permute-done((bf16[96,512]{1,0:T(8,128)(2,1)S(1)}, bf16[96,512]{1,0:T(8,128)(2,1)S(1)}, u32[]{:S(2)}, u32[]{:S(2)}) %collective-permute-start.10) | collective-permute-done | bytes 98336 | tf_op jit(solution)/shard_map/ppermute | solution.py:408
  44.2 1.2 %partial_sum.3.refs_1_ = f32[640,512]{1,0:T(8,128)S(1)} custom-call(bf16[4,640,384]{2,1,0:T(8,128)(2,1)S(1)} %prepare.3.refs_0_, bf16[96,512]{1,0:T(8,128)(2,1)S(1)} %collective-permute-done.7.refs_1_, bf16[96,512]{1,0:T(8,128)(2,1)S(1)} %collective-permute-done.8.refs_2_, bf16[96,512]{1,0:T(8,128)(2,1)S(1)} %collective-permute-done.9.refs_3_, ...), custom_call_target="tpu_custom_call" | custom-call | flops 1000000000 | bytes 10000000 | tf_op jit(solution)/shard_map/partial_sum/pallas_call | solution.py:237
  45.4 2.1 %collective-permute-done.13.refs_3_ = bf16[96,512]{1,0:T(8,128)(2,1)S(1)} collective-permute-done((bf16[96,512]{1,0:T(8,128)(2,1)S(1)}, bf16[96,512]{1,0:T(8,128)(2,1)S(1)}, u32[]{:S(2)}, u32[]{:S(2)}) %collective-permute-start.13) | collective-permute-done | bytes 98336 | tf_op jit(solution)/shard_map/ppermute | solution.py:408
  47.9 1.6 %collective-permute-start.17 = (bf16[160,256]{1,0:T(8,128)(2,1)S(1)}, bf16[160,256]{1,0:T(8,128)(2,1)S(1)}, u32[]{:S(2)}, u32[]{:S(2)}) collective-permute-start(bf16[160,256]{1,0:T(8,128)(2,1)S(1)} %get-tuple-element.64), channel_id=1, source_target_pairs={{0,8},{1,17},{2,10},{3,19},{4,12},{5,21},{6,14},{7,23},{8,0},{9,25... | collective-permute-start | bytes 245768 | tf_op jit(solution)/shard_map/ppermute | solution.py:419
  49.4 1.5 %collective-permute-start.18 = (bf16[160,256]{1,0:T(8,128)(2,1)S(1)}, bf16[160,256]{1,0:T(8,128)(2,1)S(1)}, u32[]{:S(2)}, u32[]{:S(2)}) collective-permute-start(bf16[160,256]{1,0:T(8,128)(2,1)S(1)} %get-tuple-element.65), channel_id=1, source_target_pairs={{0,16},{1,9},{2,18},{3,11},{4,20},{5,13},{6,22},{7,15},{8,24},{9,1... | collective-permute-start | bytes 245768 | tf_op jit(solution)/shard_map/ppermute | solution.py:419
  51.8 1.6 %collective-permute-start.14 = (bf16[160,256]{1,0:T(8,128)(2,1)S(1)}, bf16[160,256]{1,0:T(8,128)(2,1)S(1)}, u32[]{:S(2)}, u32[]{:S(2)}) collective-permute-start(bf16[160,256]{1,0:T(8,128)(2,1)S(1)} %get-tuple-element.60), channel_id=1, source_target_pairs={{0,8},{1,17},{2,10},{3,19},{4,12},{5,21},{6,14},{7,23},{8,0},{9,25... | collective-permute-start | bytes 245768 | tf_op jit(solution)/shard_map/ppermute | solution.py:419
  53.4 1.6 %collective-permute-start.15 = (bf16[160,256]{1,0:T(8,128)(2,1)S(1)}, bf16[160,256]{1,0:T(8,128)(2,1)S(1)}, u32[]{:S(2)}, u32[]{:S(2)}) collective-permute-start(bf16[160,256]{1,0:T(8,128)(2,1)S(1)} %get-tuple-element.61), channel_id=1, source_target_pairs={{0,16},{1,9},{2,18},{3,11},{4,20},{5,13},{6,22},{7,15},{8,24},{9,1... | collective-permute-start | bytes 245768 | tf_op jit(solution)/shard_map/ppermute | solution.py:419
  54.9 0.7 %collective-permute-start.16 = (bf16[160,256]{1,0:T(8,128)(2,1)S(1)}, bf16[160,256]{1,0:T(8,128)(2,1)S(1)}, u32[]{:S(2)}, u32[]{:S(2)}) collective-permute-start(bf16[160,256]{1,0:T(8,128)(2,1)S(1)} %get-tuple-element.62), channel_id=1, source_target_pairs={{0,24},{1,25},{2,26},{3,27},{4,28},{5,29},{6,30},{7,31},{8,16},{9,... | collective-permute-start | bytes 245768 | tf_op jit(solution)/shard_map/ppermute | solution.py:419
  55.6 0.8 %collective-permute-done.19.refs_4_ = bf16[160,256]{1,0:T(8,128)(2,1)S(1)} collective-permute-done((bf16[160,256]{1,0:T(8,128)(2,1)S(1)}, bf16[160,256]{1,0:T(8,128)(2,1)S(1)}, u32[]{:S(2)}, u32[]{:S(2)}) %collective-permute-start.19) | collective-permute-done | bytes 81952 | tf_op jit(solution)/shard_map/ppermute | solution.py:419
  56.4 1.0 %gated_traces.2.refs_5_ = f32[8,160,256]{2,1,0:T(8,128)} custom-call(s32[160,256]{1,0:T(8,128)S(1)} %copy-done.1, bf16[160,256]{1,0:T(8,128)(2,1)S(1)} %get-tuple-element.63.refs_1_, bf16[160,256]{1,0:T(8,128)(2,1)S(1)} %collective-permute-done.17.refs_2_, bf16[160,256]{1,0:T(8,128)(2,1)S(1)} %collective-permute-done.18.refs_3_, ...), custom_call_target="tpu_custom_call" | custom-call | flops 500000000 | bytes 10000000 | tf_op jit(solution)/shard_map/gated_traces/pallas_call | solution.py:389
  57.9 0.6 %collective-permute-done.15.refs_3_ = bf16[160,256]{1,0:T(8,128)(2,1)S(1)} collective-permute-done((bf16[160,256]{1,0:T(8,128)(2,1)S(1)}, bf16[160,256]{1,0:T(8,128)(2,1)S(1)}, u32[]{:S(2)}, u32[]{:S(2)}) %collective-permute-start.15) | collective-permute-done | bytes 81952 | tf_op jit(solution)/shard_map/ppermute | solution.py:419
  58.5 1.7 %collective-permute-done.16.refs_4_ = bf16[160,256]{1,0:T(8,128)(2,1)S(1)} collective-permute-done((bf16[160,256]{1,0:T(8,128)(2,1)S(1)}, bf16[160,256]{1,0:T(8,128)(2,1)S(1)}, u32[]{:S(2)}, u32[]{:S(2)}) %collective-permute-start.16) | collective-permute-done | bytes 81952 | tf_op jit(solution)/shard_map/ppermute | solution.py:419
  60.3 1.0 %gated_traces.3 = f32[8,160,256]{2,1,0:T(8,128)} custom-call(s32[160,256]{1,0:T(8,128)S(1)} %copy-done.1, bf16[160,256]{1,0:T(8,128)(2,1)S(1)} %get-tuple-element.59.refs_1_, bf16[160,256]{1,0:T(8,128)(2,1)S(1)} %collective-permute-done.14.refs_2_, bf16[160,256]{1,0:T(8,128)(2,1)S(1)} %collective-permute-done.15.refs_3_, ...), custom_call_target="tpu_custom_call", output_to_operand_aliasing={{}: (5, {})} | custom-call | flops 500000000 | bytes 10000000 | tf_op jit(solution)/shard_map/gated_traces/pallas_call | solution.py:389
  (26 shorter events, 2.4 us)
Async XLA Ops:
  2.4 12.1 %copy-start.2 = (s32[1,8,8]{2,1,0:T(8,128)S(1)}, s32[1,8,8]{2,1,0:T(8,128)}, u32[]{:S(2)}) copy-start(s32[1,8,8]{2,1,0:T(8,128)} %param.10) | copy-start | bytes 772
  3.6 7.3 %collective-permute-start.2 = (bf16[96,512]{1,0:T(8,128)(2,1)S(1)}, bf16[96,512]{1,0:T(8,128)(2,1)S(1)}, u32[]{:S(2)}, u32[]{:S(2)}) collective-permute-start(bf16[96,512]{1,0:T(8,128)(2,1)S(1)} %get-tuple-element.45), channel_id=1, source_target_pairs={{0,2},{1,3},{2,0},{3,1},{4,6},{5,7},{6,4},{7,5},{8,10},{9,11},{10,... | collective-permute-start | bytes 294920 | tf_op jit(solution)/shard_map/ppermute | solution.py:408
  6.8 4.9 %collective-permute-start.3 = (bf16[96,512]{1,0:T(8,128)(2,1)S(1)}, bf16[96,512]{1,0:T(8,128)(2,1)S(1)}, u32[]{:S(2)}, u32[]{:S(2)}) collective-permute-start(bf16[96,512]{1,0:T(8,128)(2,1)S(1)} %get-tuple-element.46), channel_id=1, source_target_pairs={{0,3},{1,2},{2,1},{3,0},{4,7},{5,6},{6,5},{7,4},{8,11},{9,10},{10,... | collective-permute-start | bytes 294920 | tf_op jit(solution)/shard_map/ppermute | solution.py:408
  6.8 11.8 %collective-permute-start.4 = (bf16[96,512]{1,0:T(8,128)(2,1)S(1)}, bf16[96,512]{1,0:T(8,128)(2,1)S(1)}, u32[]{:S(2)}, u32[]{:S(2)}) collective-permute-start(bf16[96,512]{1,0:T(8,128)(2,1)S(1)} %get-tuple-element.48), channel_id=1, source_target_pairs={{0,1},{1,0},{2,3},{3,2},{4,5},{5,4},{6,7},{7,6},{8,9},{9,8},{10,11... | collective-permute-start | bytes 294920 | tf_op jit(solution)/shard_map/ppermute | solution.py:408
  7.0 11.6 %collective-permute-start = (bf16[96,512]{1,0:T(8,128)(2,1)S(1)}, bf16[96,512]{1,0:T(8,128)(2,1)S(1)}, u32[]{:S(2)}, u32[]{:S(2)}) collective-permute-start(bf16[96,512]{1,0:T(8,128)(2,1)S(1)} %get-tuple-element.43), channel_id=1, source_target_pairs={{0,6},{1,7},{2,4},{3,5},{4,2},{5,3},{6,0},{7,1},{8,14},{9,15},{10,... | collective-permute-start | bytes 294920 | tf_op jit(solution)/shard_map/ppermute | solution.py:408
  10.9 7.6 %collective-permute-start.1 = (bf16[96,512]{1,0:T(8,128)(2,1)S(1)}, bf16[96,512]{1,0:T(8,128)(2,1)S(1)}, u32[]{:S(2)}, u32[]{:S(2)}) collective-permute-start(bf16[96,512]{1,0:T(8,128)(2,1)S(1)} %get-tuple-element.44), channel_id=1, source_target_pairs={{0,7},{1,6},{2,5},{3,4},{4,3},{5,2},{6,1},{7,0},{8,15},{9,14},{10,... | collective-permute-start | bytes 294920 | tf_op jit(solution)/shard_map/ppermute | solution.py:408
  10.9 14.6 %collective-permute-start.6 = (bf16[96,512]{1,0:T(8,128)(2,1)S(1)}, bf16[96,512]{1,0:T(8,128)(2,1)S(1)}, u32[]{:S(2)}, u32[]{:S(2)}) collective-permute-start(bf16[96,512]{1,0:T(8,128)(2,1)S(1)} %get-tuple-element.49), channel_id=1, source_target_pairs={{0,5},{1,4},{2,7},{3,6},{4,1},{5,0},{6,3},{7,2},{8,13},{9,12},{10,... | collective-permute-start | bytes 294920 | tf_op jit(solution)/shard_map/ppermute | solution.py:408
  11.7 16.1 %collective-permute-start.5 = (bf16[96,512]{1,0:T(8,128)(2,1)S(1)}, bf16[96,512]{1,0:T(8,128)(2,1)S(1)}, u32[]{:S(2)}, u32[]{:S(2)}) collective-permute-start(bf16[96,512]{1,0:T(8,128)(2,1)S(1)} %get-tuple-element.39.refs_2_), channel_id=1, source_target_pairs={{0,4},{1,5},{2,6},{3,7},{4,0},{5,1},{6,2},{7,3},{8,12},{9,13},{10,... | collective-permute-start | bytes 294920 | tf_op jit(solution)/shard_map/ppermute | solution.py:408
  18.5 9.2 %copy-start = (bf16[1,2,640,256]{3,2,1,0:T(8,128)(2,1)S(1)}, bf16[1,2,640,256]{3,2,1,0:T(8,128)(2,1)}, u32[]{:S(2)}) copy-start(bf16[1,2,640,256]{3,2,1,0:T(8,128)(2,1)} %param.7) | copy-start | bytes 1966084
  28.6 6.6 %collective-permute-start.7 = (bf16[96,512]{1,0:T(8,128)(2,1)S(1)}, bf16[96,512]{1,0:T(8,128)(2,1)S(1)}, u32[]{:S(2)}, u32[]{:S(2)}) collective-permute-start(bf16[96,512]{1,0:T(8,128)(2,1)S(1)} %get-tuple-element.51), channel_id=1, source_target_pairs={{0,6},{1,7},{2,4},{3,5},{4,2},{5,3},{6,0},{7,1},{8,14},{9,15},{10,... | collective-permute-start | bytes 294920 | tf_op jit(solution)/shard_map/ppermute | solution.py:408
  31.2 6.9 %collective-permute-start.8 = (bf16[96,512]{1,0:T(8,128)(2,1)S(1)}, bf16[96,512]{1,0:T(8,128)(2,1)S(1)}, u32[]{:S(2)}, u32[]{:S(2)}) collective-permute-start(bf16[96,512]{1,0:T(8,128)(2,1)S(1)} %get-tuple-element.52), channel_id=1, source_target_pairs={{0,7},{1,6},{2,5},{3,4},{4,3},{5,2},{6,1},{7,0},{8,15},{9,14},{10,... | collective-permute-start | bytes 294920 | tf_op jit(solution)/shard_map/ppermute | solution.py:408
  32.8 10.1 %collective-permute-start.9 = (bf16[96,512]{1,0:T(8,128)(2,1)S(1)}, bf16[96,512]{1,0:T(8,128)(2,1)S(1)}, u32[]{:S(2)}, u32[]{:S(2)}) collective-permute-start(bf16[96,512]{1,0:T(8,128)(2,1)S(1)} %get-tuple-element.53), channel_id=1, source_target_pairs={{0,2},{1,3},{2,0},{3,1},{4,6},{5,7},{6,4},{7,5},{8,10},{9,11},{10,... | collective-permute-start | bytes 294920 | tf_op jit(solution)/shard_map/ppermute | solution.py:408
  32.8 11.3 %collective-permute-start.10 = (bf16[96,512]{1,0:T(8,128)(2,1)S(1)}, bf16[96,512]{1,0:T(8,128)(2,1)S(1)}, u32[]{:S(2)}, u32[]{:S(2)}) collective-permute-start(bf16[96,512]{1,0:T(8,128)(2,1)S(1)} %get-tuple-element.54), channel_id=1, source_target_pairs={{0,3},{1,2},{2,1},{3,0},{4,7},{5,6},{6,5},{7,4},{8,11},{9,10},{10,... | collective-permute-start | bytes 294920 | tf_op jit(solution)/shard_map/ppermute | solution.py:408
  35.0 9.2 %collective-permute-start.11 = (bf16[96,512]{1,0:T(8,128)(2,1)S(1)}, bf16[96,512]{1,0:T(8,128)(2,1)S(1)}, u32[]{:S(2)}, u32[]{:S(2)}) collective-permute-start(bf16[96,512]{1,0:T(8,128)(2,1)S(1)} %get-tuple-element.56), channel_id=1, source_target_pairs={{0,1},{1,0},{2,3},{3,2},{4,5},{5,4},{6,7},{7,6},{8,9},{9,8},{10,11... | collective-permute-start | bytes 294920 | tf_op jit(solution)/shard_map/ppermute | solution.py:408
  35.3 10.1 %collective-permute-start.12 = (bf16[96,512]{1,0:T(8,128)(2,1)S(1)}, bf16[96,512]{1,0:T(8,128)(2,1)S(1)}, u32[]{:S(2)}, u32[]{:S(2)}) collective-permute-start(bf16[96,512]{1,0:T(8,128)(2,1)S(1)} %get-tuple-element.57), channel_id=1, source_target_pairs={{0,4},{1,5},{2,6},{3,7},{4,0},{5,1},{6,2},{7,3},{8,12},{9,13},{10,... | collective-permute-start | bytes 294920 | tf_op jit(solution)/shard_map/ppermute | solution.py:408
  38.1 9.4 %collective-permute-start.13 = (bf16[96,512]{1,0:T(8,128)(2,1)S(1)}, bf16[96,512]{1,0:T(8,128)(2,1)S(1)}, u32[]{:S(2)}, u32[]{:S(2)}) collective-permute-start(bf16[96,512]{1,0:T(8,128)(2,1)S(1)} %get-tuple-element.58), channel_id=1, source_target_pairs={{0,5},{1,4},{2,7},{3,6},{4,1},{5,0},{6,3},{7,2},{8,13},{9,12},{10,... | collective-permute-start | bytes 294920 | tf_op jit(solution)/shard_map/ppermute | solution.py:408
  47.9 7.0 %collective-permute-start.17 = (bf16[160,256]{1,0:T(8,128)(2,1)S(1)}, bf16[160,256]{1,0:T(8,128)(2,1)S(1)}, u32[]{:S(2)}, u32[]{:S(2)}) collective-permute-start(bf16[160,256]{1,0:T(8,128)(2,1)S(1)} %get-tuple-element.64), channel_id=1, source_target_pairs={{0,8},{1,17},{2,10},{3,19},{4,12},{5,21},{6,14},{7,23},{8,0},{9,25... | collective-permute-start | bytes 245768 | tf_op jit(solution)/shard_map/ppermute | solution.py:419
  49.4 6.2 %collective-permute-start.18 = (bf16[160,256]{1,0:T(8,128)(2,1)S(1)}, bf16[160,256]{1,0:T(8,128)(2,1)S(1)}, u32[]{:S(2)}, u32[]{:S(2)}) collective-permute-start(bf16[160,256]{1,0:T(8,128)(2,1)S(1)} %get-tuple-element.65), channel_id=1, source_target_pairs={{0,16},{1,9},{2,18},{3,11},{4,20},{5,13},{6,22},{7,15},{8,24},{9,1... | collective-permute-start | bytes 245768 | tf_op jit(solution)/shard_map/ppermute | solution.py:419
  51.0 5.4 %copy-start.1 = (s32[160,256]{1,0:T(8,128)S(1)}, s32[160,256]{1,0:T(8,128)}, u32[]{:S(2)}) copy-start(s32[160,256]{1,0:T(8,128)} %refs_0_.3) | copy-start | bytes 491524
  51.0 5.4 %collective-permute-start.19 = (bf16[160,256]{1,0:T(8,128)(2,1)S(1)}, bf16[160,256]{1,0:T(8,128)(2,1)S(1)}, u32[]{:S(2)}, u32[]{:S(2)}) collective-permute-start(bf16[160,256]{1,0:T(8,128)(2,1)S(1)} %get-tuple-element.66), channel_id=1, source_target_pairs={{0,24},{1,25},{2,26},{3,27},{4,28},{5,29},{6,30},{7,31},{8,16},{9,... | collective-permute-start | bytes 245768 | tf_op jit(solution)/shard_map/ppermute | solution.py:419
  51.8 6.1 %collective-permute-start.14 = (bf16[160,256]{1,0:T(8,128)(2,1)S(1)}, bf16[160,256]{1,0:T(8,128)(2,1)S(1)}, u32[]{:S(2)}, u32[]{:S(2)}) collective-permute-start(bf16[160,256]{1,0:T(8,128)(2,1)S(1)} %get-tuple-element.60), channel_id=1, source_target_pairs={{0,8},{1,17},{2,10},{3,19},{4,12},{5,21},{6,14},{7,23},{8,0},{9,25... | collective-permute-start | bytes 245768 | tf_op jit(solution)/shard_map/ppermute | solution.py:419
  53.4 5.2 %collective-permute-start.15 = (bf16[160,256]{1,0:T(8,128)(2,1)S(1)}, bf16[160,256]{1,0:T(8,128)(2,1)S(1)}, u32[]{:S(2)}, u32[]{:S(2)}) collective-permute-start(bf16[160,256]{1,0:T(8,128)(2,1)S(1)} %get-tuple-element.61), channel_id=1, source_target_pairs={{0,16},{1,9},{2,18},{3,11},{4,20},{5,13},{6,22},{7,15},{8,24},{9,1... | collective-permute-start | bytes 245768 | tf_op jit(solution)/shard_map/ppermute | solution.py:419
  54.9 5.3 %collective-permute-start.16 = (bf16[160,256]{1,0:T(8,128)(2,1)S(1)}, bf16[160,256]{1,0:T(8,128)(2,1)S(1)}, u32[]{:S(2)}, u32[]{:S(2)}) collective-permute-start(bf16[160,256]{1,0:T(8,128)(2,1)S(1)} %get-tuple-element.62), channel_id=1, source_target_pairs={{0,24},{1,25},{2,26},{3,27},{4,28},{5,29},{6,30},{7,31},{8,16},{9,... | collective-permute-start | bytes 245768 | tf_op jit(solution)/shard_map/ppermute | solution.py:419

commit v3 on v2

--- a/solution.py
+++ b/solution.py
@@ -11,6 +11,7 @@
 
 RMAX = 96
 LANES = 128
+CHUNKS = 1
 BF16 = jnp.bfloat16
 F32 = jnp.float32
 VMEM = pl.BlockSpec(memory_space=pltpu.VMEM)
@@ -308,15 +309,16 @@
     outs = refs[4 : 4 + freqs]
     spectrum = refs[4 + freqs]
     virtual = partial_ref.shape[1] // 2
-    real = slice(chunk * LANES, (chunk + 1) * LANES)
-    imag = slice(virtual + chunk * LANES, virtual + (chunk + 1) * LANES)
+    width = outs[0].shape[1] // 2
+    real = slice(chunk * width, (chunk + 1) * width)
+    imag = slice(virtual + chunk * width, virtual + (chunk + 1) * width)
     stack = [jnp.concatenate([b[:, real], b[:, imag]], axis=1) for b in pair]
     stack += [jnp.concatenate([-b[:, imag], b[:, real]], axis=1) for b in pair]
     late = jnp.dot(
         turned_ref[base // 2], jnp.concatenate(stack, axis=0), preferred_element_type=F32
     )
-    spectrum[:, :LANES] = partial_ref[:, real] + late[:, :LANES]
-    spectrum[:, LANES:] = partial_ref[:, imag] + late[:, LANES:]
+    spectrum[:, :width] = partial_ref[:, real] + late[:, :width]
+    spectrum[:, width:] = partial_ref[:, imag] + late[:, width:]
     share = outs[0].shape[0]
     for k in range(freqs):
         rows = pl.ds(pl.multiple_of(freq_peer(k, freqs) * share, 8), share)
@@ -324,15 +326,16 @@
 
 
 def spectrum_blocks(turned, partial, base, blocks, freqs, chunk):
-    stations = partial.shape[0]
+    stations, columns = partial.shape
+    columns //= CHUNKS
     return pl.pallas_call(
         functools.partial(spectrum_kernel, base, freqs, chunk),
         out_shape=[
-            jax.ShapeDtypeStruct((stations // freqs, 2 * LANES), BF16) for _ in range(freqs)
+            jax.ShapeDtypeStruct((stations // freqs, columns), BF16) for _ in range(freqs)
         ],
         in_specs=[VMEM] * 4,
         out_specs=[VMEM] * freqs,
-        scratch_shapes=[pltpu.VMEM((stations, 2 * LANES), F32)],
+        scratch_shapes=[pltpu.VMEM((stations, columns), F32)],
         compiler_params=params(),
         cost_estimate=cost(5 * 10**8),
         name="spectrum_blocks",
@@ -347,7 +350,8 @@
         gathered[freq_peer(k, freqs)] = blocks[k][...]
     times = 2 * freqs
     scaling = 1.0 / math.sqrt(freqs)
-    lanes = pl.ds(chunk * LANES, LANES)
+    width = blocks[0].shape[1] // 2
+    lanes = pl.ds(chunk * width, width)
     copies = [
         pltpu.make_async_copy(traces.at[t], out_hbm.at[t, :, lanes], sems.at[t])
         for t in range(times)
@@ -363,7 +367,7 @@
                 if quarter:
                     weight = float(round(weight))
                 if weight != 0.0:
-                    value = gathered[f, :, part * LANES : (part + 1) * LANES]
+                    value = gathered[f, :, part * width : (part + 1) * width]
                     term = value.astype(F32) * (weight * scaling)
                     old = sums[f % 2]
                     sums[f % 2] = term if old is None else old + term
@@ -392,8 +396,8 @@
         in_specs=specs,
         out_specs=HBM,
         scratch_shapes=[
-            pltpu.VMEM((freqs, share, 2 * LANES), BF16),
-            pltpu.VMEM((2 * freqs, share, LANES), F32),
+            pltpu.VMEM((freqs, *blocks[0].shape), BF16),
+            pltpu.VMEM((2 * freqs, share, blocks[0].shape[1] // 2), F32),
             pltpu.SemaphoreType.DMA((2 * freqs,)),
         ],
         input_output_aliases=aliases,
@@ -466,7 +470,7 @@
     (v_turned,) = prepare(v, table, stacked, False)
     partial = partial_sum(v_turned, early, pick(returned, early))
     spectra = []
-    for chunk in range(x.shape[2] // LANES):
+    for chunk in range(CHUNKS):
         blocks = spectrum_blocks(
             v_turned, partial, late, pick(returned, (late,)), freqs, chunk
         )

time: 61.4 us -> 60.1 us (0.979)
  starting transfers between devices: 25.6 us -> 21.8 us
  waiting for transfers between devices: 17.1 us -> 20.3 us
  Pallas kernels: 18.4 us -> 17.7 us
    ppermute x6 -> x3, starting transfers between devices: 7.36 us -> 3.55 us  [send_freq(): return lax.ppermute(block, ('freq', 'tile'), pairs)]
    ppermute x6 -> x3, waiting for transfers between devices: 3.65 us -> 6.93 us  [send_freq(): return lax.ppermute(block, ('freq', 'tile'), pairs)]
    pallas_call x2 -> x1, Pallas kernels: 1.94 us -> 1.33 us  [gated_traces(): pl.pallas_call(functools.partial(traces_kernel, freqs, chunk), out_shape=...]
  transfers between devices with their start and end apart: 20 -> 17, of which waited for: 10 -> 9; matrix products, arithmetic and copies ran while one was open for 0% -> 0% of each run, Pallas kernels for 21% -> 19%
where the time goes in v3:
time: 60.1 us; the launch traced here: 59.9 us
  starting transfers between devices  21.8 us (36%)
  waiting for transfers between devices  20.3 us (34%)
  Pallas kernels  17.7 us (29%)
    ppermute x14, starting transfers between devices, send(): return lax.ppermute(block, axis, [(i, i ^ k) for i in range(count)])  18.2 us
    ppermute x14, waiting for transfers between devices, send(): return lax.ppermute(block, axis, [(i, i ^ k) for i in range(count)])  13.4 us
    pallas_call x2, Pallas kernels, prepare(): pl.pallas_call(functools.partial(prepare_kernel, want_rows), out_shape=ou...  7.97 us
    ppermute x3, waiting for transfers between devices, send_freq(): return lax.ppermute(block, ('freq', 'tile'), pairs)  6.93 us
    ppermute x3, starting transfers between devices, send_freq(): return lax.ppermute(block, ('freq', 'tile'), pairs)  3.55 us
    pallas_call x2, Pallas kernels, partial_sum(): pl.pallas_call(functools.partial(partial_kernel, bases), out_shape=jax.Sh...  2.35 us
    pallas_call x1, Pallas kernels, coeff_first(): pl.pallas_call(functools.partial(coeff_first_kernel, first, rest), out_sh...  2.35 us
    pallas_call x1, Pallas kernels, gated_traces(): pl.pallas_call(functools.partial(traces_kernel, freqs, chunk), out_shape=...  1.33 us
  transfers between devices with their start and end apart: 17, of which 9 were waited for; matrix products, arithmetic and copies ran while one was open for 0% of the time, Pallas kernels for 19%

profile of v3, /device:TPU:0, one launch (start us, length us, event | category | flops | bytes accessed | tf_op | source)
XLA Modules:
  0.0 59.9 jit_solution(9461403433152874099)
XLA Ops:
  0.0 2.4 %coeff_first.1 = (bf16[96,512]{1,0:T(8,128)(2,1)S(1)}, bf16[96,512]{1,0:T(8,128)(2,1)S(1)}, bf16[2,640,256]{2,1,0:T(8,128)(2,1)S(1)}, bf16[6,96,2,640]{3,2,1,0:T(2,128)(2,1)S(1)}, f32[6,96,128]{2,1,0:T(8,128)S(1)}) custom-call(s32[8,8]{1,0:T(8,128)} %bitcast.6, bf16[8,128,2,640]{3,2,1,0:T(2,128)(2,1)} %bitcast.9, bf16[2,640,256]{2,1,0:T(8,128)(2,1)} %bitcast.12), custom_call_target="tpu_custom_call" | custom-call | flops 1000000000 | bytes 10000000 | tf_op jit(solution)/shard_map/coeff_first/pallas_call | solution.py:113
  2.4 1.3 %coeff_rest.1 = (bf16[96,512]{1,0:T(8,128)(2,1)S(1)}, bf16[96,512]{1,0:T(8,128)(2,1)S(1)}, bf16[96,512]{1,0:T(8,128)(2,1)S(1)}, bf16[96,512]{1,0:T(8,128)(2,1)S(...) custom-call(f32[6,96,128]{2,1,0:T(8,128)S(1)} %get-tuple-element.32.refs_0_, ...), custom_call_target="tpu_custom_call" | custom-call | flops 1000000000 | bytes 10000000 | tf_op jit(solution)/shard_map/coeff_rest/pallas_call | solution.py:141
  3.6 3.1 %collective-permute-start.2 = (bf16[96,512]{1,0:T(8,128)(2,1)S(1)}, bf16[96,512]{1,0:T(8,128)(2,1)S(1)}, u32[]{:S(2)}, u32[]{:S(2)}) collective-permute-start(bf16[96,512]{1,0:T(8,128)(2,1)S(1)} %get-tuple-element.41), channel_id=1, source_target_pairs={{0,2},{1,3},{2,0},{3,1},{4,6},{5,7},{6,4},{7,5},{8,10},{9,11},{10,... | collective-permute-start | bytes 294920 | tf_op jit(solution)/shard_map/ppermute | solution.py:412
  6.8 0.2 collective-permute-start.4
  7.0 4.0 %collective-permute-start = (bf16[96,512]{1,0:T(8,128)(2,1)S(1)}, bf16[96,512]{1,0:T(8,128)(2,1)S(1)}, u32[]{:S(2)}, u32[]{:S(2)}) collective-permute-start(bf16[96,512]{1,0:T(8,128)(2,1)S(1)} %get-tuple-element.39), channel_id=1, source_target_pairs={{0,6},{1,7},{2,4},{3,5},{4,2},{5,3},{6,0},{7,1},{8,14},{9,15},{10,... | collective-permute-start | bytes 294920 | tf_op jit(solution)/shard_map/ppermute | solution.py:412
  10.9 0.7 %collective-permute-start.6 = (bf16[96,512]{1,0:T(8,128)(2,1)S(1)}, bf16[96,512]{1,0:T(8,128)(2,1)S(1)}, u32[]{:S(2)}, u32[]{:S(2)}) collective-permute-start(bf16[96,512]{1,0:T(8,128)(2,1)S(1)} %get-tuple-element.45), channel_id=1, source_target_pairs={{0,5},{1,4},{2,7},{3,6},{4,1},{5,0},{6,3},{7,2},{8,13},{9,12},{10,... | collective-permute-start | bytes 294920 | tf_op jit(solution)/shard_map/ppermute | solution.py:412
  11.7 2.8 %collective-permute-start.5 = (bf16[96,512]{1,0:T(8,128)(2,1)S(1)}, bf16[96,512]{1,0:T(8,128)(2,1)S(1)}, u32[]{:S(2)}, u32[]{:S(2)}) collective-permute-start(bf16[96,512]{1,0:T(8,128)(2,1)S(1)} %get-tuple-element.35.refs_2_), channel_id=1, source_target_pairs={{0,4},{1,5},{2,6},{3,7},{4,0},{5,1},{6,2},{7,3},{8,12},{9,13},{10,... | collective-permute-start | bytes 294920 | tf_op jit(solution)/shard_map/ppermute | solution.py:412
  14.4 4.1 %prepare.2 = (bf16[4,640,384]{2,1,0:T(8,128)(2,1)S(1)}, bf16[768,1280]{1,0:T(8,128)(2,1)S(1)}, f32[8,96,128]{2,1,0:T(8,128)S(1)}) custom-call(bf16[8,128,2,640]{3,2,1,0:T(2,128)(2,1)} %bitcast.11, s32[8,8]{1,0:T(8,128)S(1)} %bitcast.7, bf16[96,512]{1,0:T(8,128)(2,1)S(1)} %get-tuple-element.35.refs_2_), custom_call_target="tpu_custom_call" | custom-call | flops 1000000000 | bytes 10000000 | tf_op jit(solution)/shard_map/prepare/pallas_call | solution.py:200
  18.6 1.2 %partial_sum.2.refs_4_ = f32[640,512]{1,0:T(8,128)S(1)} custom-call(bf16[4,640,384]{2,1,0:T(8,128)(2,1)S(1)} %get-tuple-element.38.refs_0_.refs_2_, bf16[96,512]{1,0:T(8,128)(2,1)S(1)} %collective-permute-done.refs_1_, bf16[96,512]{1,0:T(8,128)(2,1)S(1)} %collective-permute-done.1.refs_2_, bf16[96,512]{1,0:T(8,128)(2,1)S(1)} %collective-permute-done.2.refs_3_, ...), custom_call_target="tpu_custom_call" | custom-call | flops 1000000000 | bytes 10000000 | tf_op jit(solution)/shard_map/partial_sum/pallas_call | solution.py:238
  19.7 5.8 %collective-permute-done.6.refs_6_ = bf16[96,512]{1,0:T(8,128)(2,1)S(1)} collective-permute-done((bf16[96,512]{1,0:T(8,128)(2,1)S(1)}, bf16[96,512]{1,0:T(8,128)(2,1)S(1)}, u32[]{:S(2)}, u32[]{:S(2)}) %collective-permute-start.6) | collective-permute-done | bytes 98336 | tf_op jit(solution)/shard_map/ppermute | solution.py:412
  25.5 2.2 %collective-permute-done.5.refs_5_ = bf16[96,512]{1,0:T(8,128)(2,1)S(1)} collective-permute-done((bf16[96,512]{1,0:T(8,128)(2,1)S(1)}, bf16[96,512]{1,0:T(8,128)(2,1)S(1)}, u32[]{:S(2)}, u32[]{:S(2)}) %collective-permute-start.5) | collective-permute-done | bytes 98336 | tf_op jit(solution)/shard_map/ppermute | solution.py:412
  27.8 0.9 %residual_blocks.1 = (bf16[96,512]{1,0:T(8,128)(2,1)S(1)}, bf16[96,512]{1,0:T(8,128)(2,1)S(1)}, bf16[1280,512]{1,0:T(8,128)(2,1)S(1)}) custom-call(f32[8,96,128]{2,1,0:T(8,128)S(1)} %get-tuple-element.36.refs_0_, bf16[768,1280]{1,0:T(8,128)(2,1)S(1)} %get-tuple-element.37.refs_1_, bf16[4,640,384]{2,1,0:T(8,128)(2,1)S(1)} %get-tuple-element.38.refs_0_.refs_2_, ...), custom_call_target="tpu_custom_call" | custom-call | flops 1000000000 | bytes 10000000 | tf_op jit(solution)/shard_map/residual_blocks/pallas_call | solution.py:278
  28.6 2.5 %collective-permute-start.7 = (bf16[96,512]{1,0:T(8,128)(2,1)S(1)}, bf16[96,512]{1,0:T(8,128)(2,1)S(1)}, u32[]{:S(2)}, u32[]{:S(2)}) collective-permute-start(bf16[96,512]{1,0:T(8,128)(2,1)S(1)} %get-tuple-element.47), channel_id=1, source_target_pairs={{0,6},{1,7},{2,4},{3,5},{4,2},{5,3},{6,0},{7,1},{8,14},{9,15},{10,... | collective-permute-start | bytes 294920 | tf_op jit(solution)/shard_map/ppermute | solution.py:412
  31.2 0.7 %collective-permute-start.8 = (bf16[96,512]{1,0:T(8,128)(2,1)S(1)}, bf16[96,512]{1,0:T(8,128)(2,1)S(1)}, u32[]{:S(2)}, u32[]{:S(2)}) collective-permute-start(bf16[96,512]{1,0:T(8,128)(2,1)S(1)} %get-tuple-element.48), channel_id=1, source_target_pairs={{0,7},{1,6},{2,5},{3,4},{4,3},{5,2},{6,1},{7,0},{8,15},{9,14},{10,... | collective-permute-start | bytes 294920 | tf_op jit(solution)/shard_map/ppermute | solution.py:412
  31.8 0.9 %adjoint_blocks.1 = (bf16[96,512]{1,0:T(8,128)(2,1)S(1)}, bf16[96,512]{1,0:T(8,128)(2,1)S(1)}, bf16[96,512]{1,0:T(8,128)(2,1)S(1)}, bf16[96,512]{1,0:T(8,128)(2,...) custom-call(f32[8,96,128]{2,1,0:T(8,128)S(1)} %get-tuple-element.36.refs_0_, ...), custom_call_target="tpu_custom_call" | custom-call | flops 1000000000 | bytes 10000000 | tf_op jit(solution)/shard_map/adjoint_blocks/pallas_call | solution.py:295
  32.8 2.1 %collective-permute-start.10 = (bf16[96,512]{1,0:T(8,128)(2,1)S(1)}, bf16[96,512]{1,0:T(8,128)(2,1)S(1)}, u32[]{:S(2)}, u32[]{:S(2)}) collective-permute-start(bf16[96,512]{1,0:T(8,128)(2,1)S(1)} %get-tuple-element.50), channel_id=1, source_target_pairs={{0,3},{1,2},{2,1},{3,0},{4,7},{5,6},{6,5},{7,4},{8,11},{9,10},{10,... | collective-permute-start | bytes 294920 | tf_op jit(solution)/shard_map/ppermute | solution.py:412
  35.0 0.3 collective-permute-done.7.refs_1_
  35.3 1.1 %collective-permute-start.12 = (bf16[96,512]{1,0:T(8,128)(2,1)S(1)}, bf16[96,512]{1,0:T(8,128)(2,1)S(1)}, u32[]{:S(2)}, u32[]{:S(2)}) collective-permute-start(bf16[96,512]{1,0:T(8,128)(2,1)S(1)} %get-tuple-element.53), channel_id=1, source_target_pairs={{0,4},{1,5},{2,6},{3,7},{4,0},{5,1},{6,2},{7,3},{8,12},{9,13},{10,... | collective-permute-start | bytes 294920 | tf_op jit(solution)/shard_map/ppermute | solution.py:412
  36.4 1.7 %collective-permute-done.8.refs_2_ = bf16[96,512]{1,0:T(8,128)(2,1)S(1)} collective-permute-done((bf16[96,512]{1,0:T(8,128)(2,1)S(1)}, bf16[96,512]{1,0:T(8,128)(2,1)S(1)}, u32[]{:S(2)}, u32[]{:S(2)}) %collective-permute-start.8) | collective-permute-done | bytes 98336 | tf_op jit(solution)/shard_map/ppermute | solution.py:412
  38.1 0.9 %collective-permute-start.13 = (bf16[96,512]{1,0:T(8,128)(2,1)S(1)}, bf16[96,512]{1,0:T(8,128)(2,1)S(1)}, u32[]{:S(2)}, u32[]{:S(2)}) collective-permute-start(bf16[96,512]{1,0:T(8,128)(2,1)S(1)} %get-tuple-element.54), channel_id=1, source_target_pairs={{0,5},{1,4},{2,7},{3,6},{4,1},{5,0},{6,3},{7,2},{8,13},{9,12},{10,... | collective-permute-start | bytes 294920 | tf_op jit(solution)/shard_map/ppermute | solution.py:412
  39.0 3.9 %prepare.3.refs_0_ = bf16[4,640,384]{2,1,0:T(8,128)(2,1)S(1)} custom-call(bf16[8,128,2,640]{3,2,1,0:T(2,128)(2,1)} %bitcast.10, s32[8,8]{1,0:T(8,128)S(1)} %bitcast.8, bf16[1280,512]{1,0:T(8,128)(2,1)S(1)} %get-tuple-element.46.refs_2_), custom_call_target="tpu_custom_call" | custom-call | flops 1000000000 | bytes 10000000 | tf_op jit(solution)/shard_map/prepare/pallas_call | solution.py:200
  42.9 1.3 %collective-permute-done.10.refs_4_ = bf16[96,512]{1,0:T(8,128)(2,1)S(1)} collective-permute-done((bf16[96,512]{1,0:T(8,128)(2,1)S(1)}, bf16[96,512]{1,0:T(8,128)(2,1)S(1)}, u32[]{:S(2)}, u32[]{:S(2)}) %collective-permute-start.10) | collective-permute-done | bytes 98336 | tf_op jit(solution)/shard_map/ppermute | solution.py:412
  44.2 1.2 %partial_sum.3.refs_1_ = f32[640,512]{1,0:T(8,128)S(1)} custom-call(bf16[4,640,384]{2,1,0:T(8,128)(2,1)S(1)} %prepare.3.refs_0_, bf16[96,512]{1,0:T(8,128)(2,1)S(1)} %collective-permute-done.7.refs_1_, bf16[96,512]{1,0:T(8,128)(2,1)S(1)} %collective-permute-done.8.refs_2_, bf16[96,512]{1,0:T(8,128)(2,1)S(1)} %collective-permute-done.9.refs_3_, ...), custom_call_target="tpu_custom_call" | custom-call | flops 1000000000 | bytes 10000000 | tf_op jit(solution)/shard_map/partial_sum/pallas_call | solution.py:238
  45.4 2.1 %collective-permute-done.13.refs_3_ = bf16[96,512]{1,0:T(8,128)(2,1)S(1)} collective-permute-done((bf16[96,512]{1,0:T(8,128)(2,1)S(1)}, bf16[96,512]{1,0:T(8,128)(2,1)S(1)}, u32[]{:S(2)}, u32[]{:S(2)}) %collective-permute-start.13) | collective-permute-done | bytes 98336 | tf_op jit(solution)/shard_map/ppermute | solution.py:412
  47.5 0.6 %spectrum_blocks.1 = (bf16[160,512]{1,0:T(8,128)(2,1)S(1)}, bf16[160,512]{1,0:T(8,128)(2,1)S(1)}, bf16[160,512]{1,0:T(8,128)(2,1)S(1)}, bf16[160,512]{1,0:T(8,128)(2,1)S(1)}) custom-call(bf16[4,640,384]{2,1,0:T(8,128)(2,1)S(1)} %prepare.3.refs_0_, f32[640,512]{1,0:T(8,128)S(1)} %partial_sum.3.refs_1_, bf16[96,512]{1,0:T(8,128)(2,1)S(1)} %collective-permute-done.12.refs_2_, ...), custom_call_target="tpu_custom_call" | custom-call | flops 500000000 | bytes 10000000 | tf_op jit(solution)/shard_map/spectrum_blocks/pallas_call | solution.py:331
  48.1 1.6 %collective-permute-start.14 = (bf16[160,512]{1,0:T(8,128)(2,1)S(1)}, bf16[160,512]{1,0:T(8,128)(2,1)S(1)}, u32[]{:S(2)}, u32[]{:S(2)}) collective-permute-start(bf16[160,512]{1,0:T(8,128)(2,1)S(1)} %get-tuple-element.56), channel_id=1, source_target_pairs={{0,8},{1,17},{2,10},{3,19},{4,12},{5,21},{6,14},{7,23},{8,0},{9,25... | collective-permute-start | bytes 491528 | tf_op jit(solution)/shard_map/ppermute | solution.py:423
  49.7 1.5 %collective-permute-start.15 = (bf16[160,512]{1,0:T(8,128)(2,1)S(1)}, bf16[160,512]{1,0:T(8,128)(2,1)S(1)}, u32[]{:S(2)}, u32[]{:S(2)}) collective-permute-start(bf16[160,512]{1,0:T(8,128)(2,1)S(1)} %get-tuple-element.57), channel_id=1, source_target_pairs={{0,16},{1,9},{2,18},{3,11},{4,20},{5,13},{6,22},{7,15},{8,24},{9,1... | collective-permute-start | bytes 491528 | tf_op jit(solution)/shard_map/ppermute | solution.py:423
  51.2 0.5 collective-permute-start.16
  51.7 3.6 %collective-permute-done.14.refs_2_ = bf16[160,512]{1,0:T(8,128)(2,1)S(1)} collective-permute-done((bf16[160,512]{1,0:T(8,128)(2,1)S(1)}, bf16[160,512]{1,0:T(8,128)(2,1)S(1)}, u32[]{:S(2)}, u32[]{:S(2)}) %collective-permute-start.14) | collective-permute-done | bytes 163872 | tf_op jit(solution)/shard_map/ppermute | solution.py:423
  55.2 0.8 %collective-permute-done.15.refs_3_ = bf16[160,512]{1,0:T(8,128)(2,1)S(1)} collective-permute-done((bf16[160,512]{1,0:T(8,128)(2,1)S(1)}, bf16[160,512]{1,0:T(8,128)(2,1)S(1)}, u32[]{:S(2)}, u32[]{:S(2)}) %collective-permute-start.15) | collective-permute-done | bytes 163872 | tf_op jit(solution)/shard_map/ppermute | solution.py:423
  56.0 2.6 %collective-permute-done.16.refs_4_ = bf16[160,512]{1,0:T(8,128)(2,1)S(1)} collective-permute-done((bf16[160,512]{1,0:T(8,128)(2,1)S(1)}, bf16[160,512]{1,0:T(8,128)(2,1)S(1)}, u32[]{:S(2)}, u32[]{:S(2)}) %collective-permute-start.16) | collective-permute-done | bytes 163872 | tf_op jit(solution)/shard_map/ppermute | solution.py:423
  58.6 1.3 %gated_traces.1 = f32[8,160,256]{2,1,0:T(8,128)} custom-call(s32[160,256]{1,0:T(8,128)S(1)} %copy-done.1, bf16[160,512]{1,0:T(8,128)(2,1)S(1)} %get-tuple-element.55.refs_1_, bf16[160,512]{1,0:T(8,128)(2,1)S(1)} %collective-permute-done.14.refs_2_, bf16[160,512]{1,0:T(8,128)(2,1)S(1)} %collective-permute-done.15.refs_3_, ...), custom_call_target="tpu_custom_call" | custom-call | flops 500000000 | bytes 10000000 | tf_op jit(solution)/shard_map/gated_traces/pallas_call | solution.py:393
  (18 shorter events, 0.1 us)
Async XLA Ops:
  2.4 12.1 %copy-start.2 = (s32[1,8,8]{2,1,0:T(8,128)S(1)}, s32[1,8,8]{2,1,0:T(8,128)}, u32[]{:S(2)}) copy-start(s32[1,8,8]{2,1,0:T(8,128)} %param.10) | copy-start | bytes 772
  3.6 7.3 %collective-permute-start.2 = (bf16[96,512]{1,0:T(8,128)(2,1)S(1)}, bf16[96,512]{1,0:T(8,128)(2,1)S(1)}, u32[]{:S(2)}, u32[]{:S(2)}) collective-permute-start(bf16[96,512]{1,0:T(8,128)(2,1)S(1)} %get-tuple-element.41), channel_id=1, source_target_pairs={{0,2},{1,3},{2,0},{3,1},{4,6},{5,7},{6,4},{7,5},{8,10},{9,11},{10,... | collective-permute-start | bytes 294920 | tf_op jit(solution)/shard_map/ppermute | solution.py:412
  6.8 4.9 %collective-permute-start.3 = (bf16[96,512]{1,0:T(8,128)(2,1)S(1)}, bf16[96,512]{1,0:T(8,128)(2,1)S(1)}, u32[]{:S(2)}, u32[]{:S(2)}) collective-permute-start(bf16[96,512]{1,0:T(8,128)(2,1)S(1)} %get-tuple-element.42), channel_id=1, source_target_pairs={{0,3},{1,2},{2,1},{3,0},{4,7},{5,6},{6,5},{7,4},{8,11},{9,10},{10,... | collective-permute-start | bytes 294920 | tf_op jit(solution)/shard_map/ppermute | solution.py:412
  6.8 11.8 %collective-permute-start.4 = (bf16[96,512]{1,0:T(8,128)(2,1)S(1)}, bf16[96,512]{1,0:T(8,128)(2,1)S(1)}, u32[]{:S(2)}, u32[]{:S(2)}) collective-permute-start(bf16[96,512]{1,0:T(8,128)(2,1)S(1)} %get-tuple-element.44), channel_id=1, source_target_pairs={{0,1},{1,0},{2,3},{3,2},{4,5},{5,4},{6,7},{7,6},{8,9},{9,8},{10,11... | collective-permute-start | bytes 294920 | tf_op jit(solution)/shard_map/ppermute | solution.py:412
  7.0 11.6 %collective-permute-start = (bf16[96,512]{1,0:T(8,128)(2,1)S(1)}, bf16[96,512]{1,0:T(8,128)(2,1)S(1)}, u32[]{:S(2)}, u32[]{:S(2)}) collective-permute-start(bf16[96,512]{1,0:T(8,128)(2,1)S(1)} %get-tuple-element.39), channel_id=1, source_target_pairs={{0,6},{1,7},{2,4},{3,5},{4,2},{5,3},{6,0},{7,1},{8,14},{9,15},{10,... | collective-permute-start | bytes 294920 | tf_op jit(solution)/shard_map/ppermute | solution.py:412
  10.9 7.6 %collective-permute-start.1 = (bf16[96,512]{1,0:T(8,128)(2,1)S(1)}, bf16[96,512]{1,0:T(8,128)(2,1)S(1)}, u32[]{:S(2)}, u32[]{:S(2)}) collective-permute-start(bf16[96,512]{1,0:T(8,128)(2,1)S(1)} %get-tuple-element.40), channel_id=1, source_target_pairs={{0,7},{1,6},{2,5},{3,4},{4,3},{5,2},{6,1},{7,0},{8,15},{9,14},{10,... | collective-permute-start | bytes 294920 | tf_op jit(solution)/shard_map/ppermute | solution.py:412
  10.9 14.6 %collective-permute-start.6 = (bf16[96,512]{1,0:T(8,128)(2,1)S(1)}, bf16[96,512]{1,0:T(8,128)(2,1)S(1)}, u32[]{:S(2)}, u32[]{:S(2)}) collective-permute-start(bf16[96,512]{1,0:T(8,128)(2,1)S(1)} %get-tuple-element.45), channel_id=1, source_target_pairs={{0,5},{1,4},{2,7},{3,6},{4,1},{5,0},{6,3},{7,2},{8,13},{9,12},{10,... | collective-permute-start | bytes 294920 | tf_op jit(solution)/shard_map/ppermute | solution.py:412
  11.7 16.1 %collective-permute-start.5 = (bf16[96,512]{1,0:T(8,128)(2,1)S(1)}, bf16[96,512]{1,0:T(8,128)(2,1)S(1)}, u32[]{:S(2)}, u32[]{:S(2)}) collective-permute-start(bf16[96,512]{1,0:T(8,128)(2,1)S(1)} %get-tuple-element.35.refs_2_), channel_id=1, source_target_pairs={{0,4},{1,5},{2,6},{3,7},{4,0},{5,1},{6,2},{7,3},{8,12},{9,13},{10,... | collective-permute-start | bytes 294920 | tf_op jit(solution)/shard_map/ppermute | solution.py:412
  18.5 9.3 %copy-start = (bf16[1,2,640,256]{3,2,1,0:T(8,128)(2,1)S(1)}, bf16[1,2,640,256]{3,2,1,0:T(8,128)(2,1)}, u32[]{:S(2)}) copy-start(bf16[1,2,640,256]{3,2,1,0:T(8,128)(2,1)} %param.7) | copy-start | bytes 1966084
  28.6 6.6 %collective-permute-start.7 = (bf16[96,512]{1,0:T(8,128)(2,1)S(1)}, bf16[96,512]{1,0:T(8,128)(2,1)S(1)}, u32[]{:S(2)}, u32[]{:S(2)}) collective-permute-start(bf16[96,512]{1,0:T(8,128)(2,1)S(1)} %get-tuple-element.47), channel_id=1, source_target_pairs={{0,6},{1,7},{2,4},{3,5},{4,2},{5,3},{6,0},{7,1},{8,14},{9,15},{10,... | collective-permute-start | bytes 294920 | tf_op jit(solution)/shard_map/ppermute | solution.py:412
  31.2 6.9 %collective-permute-start.8 = (bf16[96,512]{1,0:T(8,128)(2,1)S(1)}, bf16[96,512]{1,0:T(8,128)(2,1)S(1)}, u32[]{:S(2)}, u32[]{:S(2)}) collective-permute-start(bf16[96,512]{1,0:T(8,128)(2,1)S(1)} %get-tuple-element.48), channel_id=1, source_target_pairs={{0,7},{1,6},{2,5},{3,4},{4,3},{5,2},{6,1},{7,0},{8,15},{9,14},{10,... | collective-permute-start | bytes 294920 | tf_op jit(solution)/shard_map/ppermute | solution.py:412
  32.8 10.1 %collective-permute-start.9 = (bf16[96,512]{1,0:T(8,128)(2,1)S(1)}, bf16[96,512]{1,0:T(8,128)(2,1)S(1)}, u32[]{:S(2)}, u32[]{:S(2)}) collective-permute-start(bf16[96,512]{1,0:T(8,128)(2,1)S(1)} %get-tuple-element.49), channel_id=1, source_target_pairs={{0,2},{1,3},{2,0},{3,1},{4,6},{5,7},{6,4},{7,5},{8,10},{9,11},{10,... | collective-permute-start | bytes 294920 | tf_op jit(solution)/shard_map/ppermute | solution.py:412
  32.8 11.3 %collective-permute-start.10 = (bf16[96,512]{1,0:T(8,128)(2,1)S(1)}, bf16[96,512]{1,0:T(8,128)(2,1)S(1)}, u32[]{:S(2)}, u32[]{:S(2)}) collective-permute-start(bf16[96,512]{1,0:T(8,128)(2,1)S(1)} %get-tuple-element.50), channel_id=1, source_target_pairs={{0,3},{1,2},{2,1},{3,0},{4,7},{5,6},{6,5},{7,4},{8,11},{9,10},{10,... | collective-permute-start | bytes 294920 | tf_op jit(solution)/shard_map/ppermute | solution.py:412
  35.0 9.2 %collective-permute-start.11 = (bf16[96,512]{1,0:T(8,128)(2,1)S(1)}, bf16[96,512]{1,0:T(8,128)(2,1)S(1)}, u32[]{:S(2)}, u32[]{:S(2)}) collective-permute-start(bf16[96,512]{1,0:T(8,128)(2,1)S(1)} %get-tuple-element.52), channel_id=1, source_target_pairs={{0,1},{1,0},{2,3},{3,2},{4,5},{5,4},{6,7},{7,6},{8,9},{9,8},{10,11... | collective-permute-start | bytes 294920 | tf_op jit(solution)/shard_map/ppermute | solution.py:412
  35.3 10.1 %collective-permute-start.12 = (bf16[96,512]{1,0:T(8,128)(2,1)S(1)}, bf16[96,512]{1,0:T(8,128)(2,1)S(1)}, u32[]{:S(2)}, u32[]{:S(2)}) collective-permute-start(bf16[96,512]{1,0:T(8,128)(2,1)S(1)} %get-tuple-element.53), channel_id=1, source_target_pairs={{0,4},{1,5},{2,6},{3,7},{4,0},{5,1},{6,2},{7,3},{8,12},{9,13},{10,... | collective-permute-start | bytes 294920 | tf_op jit(solution)/shard_map/ppermute | solution.py:412
  38.1 9.4 %collective-permute-start.13 = (bf16[96,512]{1,0:T(8,128)(2,1)S(1)}, bf16[96,512]{1,0:T(8,128)(2,1)S(1)}, u32[]{:S(2)}, u32[]{:S(2)}) collective-permute-start(bf16[96,512]{1,0:T(8,128)(2,1)S(1)} %get-tuple-element.54), channel_id=1, source_target_pairs={{0,5},{1,4},{2,7},{3,6},{4,1},{5,0},{6,3},{7,2},{8,13},{9,12},{10,... | collective-permute-start | bytes 294920 | tf_op jit(solution)/shard_map/ppermute | solution.py:412
  45.4 13.2 %copy-start.1 = (s32[160,256]{1,0:T(8,128)S(1)}, s32[160,256]{1,0:T(8,128)}, u32[]{:S(2)}) copy-start(s32[160,256]{1,0:T(8,128)} %refs_0_.1) | copy-start | bytes 491524
  48.1 7.1 %collective-permute-start.14 = (bf16[160,512]{1,0:T(8,128)(2,1)S(1)}, bf16[160,512]{1,0:T(8,128)(2,1)S(1)}, u32[]{:S(2)}, u32[]{:S(2)}) collective-permute-start(bf16[160,512]{1,0:T(8,128)(2,1)S(1)} %get-tuple-element.56), channel_id=1, source_target_pairs={{0,8},{1,17},{2,10},{3,19},{4,12},{5,21},{6,14},{7,23},{8,0},{9,25... | collective-permute-start | bytes 491528 | tf_op jit(solution)/shard_map/ppermute | solution.py:423
  49.7 6.3 %collective-permute-start.15 = (bf16[160,512]{1,0:T(8,128)(2,1)S(1)}, bf16[160,512]{1,0:T(8,128)(2,1)S(1)}, u32[]{:S(2)}, u32[]{:S(2)}) collective-permute-start(bf16[160,512]{1,0:T(8,128)(2,1)S(1)} %get-tuple-element.57), channel_id=1, source_target_pairs={{0,16},{1,9},{2,18},{3,11},{4,20},{5,13},{6,22},{7,15},{8,24},{9,1... | collective-permute-start | bytes 491528 | tf_op jit(solution)/shard_map/ppermute | solution.py:423
  51.2 7.4 %collective-permute-start.16 = (bf16[160,512]{1,0:T(8,128)(2,1)S(1)}, bf16[160,512]{1,0:T(8,128)(2,1)S(1)}, u32[]{:S(2)}, u32[]{:S(2)}) collective-permute-start(bf16[160,512]{1,0:T(8,128)(2,1)S(1)} %get-tuple-element.58), channel_id=1, source_target_pairs={{0,24},{1,25},{2,26},{3,27},{4,28},{5,29},{6,30},{7,31},{8,16},{9,... | collective-permute-start | bytes 491528 | tf_op jit(solution)/shard_map/ppermute | solution.py:423

commit v4 on v3

--- a/solution.py
+++ b/solution.py
@@ -455,10 +455,11 @@
     late = count // 2
     early = tuple(base for base in pair_bases(count) if base != late)
     first, rest = peer_order(count)
-    *blocks, field, rest_factors, rest_masks = coeff_first(hbm(table), v, x, first, rest)
-    arrived = exchange(first, blocks)
-    blocks = coeff_rest(rest_masks, field, rest_factors, rest)
-    arrived |= exchange(rest, blocks)
+    alone, others = first[:1], first[1:] + rest
+    *blocks, field, rest_factors, rest_masks = coeff_first(hbm(table), v, x, alone, others)
+    arrived = exchange(alone, blocks)
+    blocks = coeff_rest(rest_masks, field, rest_factors, others)
+    arrived |= exchange(others, blocks)
     u_turned, u_rows, masks = prepare(u, table, blocks[0], True)
     partial = partial_sum(u_turned, early, pick(arrived, early))
     *blocks, stacked = residual_blocks(

time: 60.1 us -> 61.7 us (1.027)
  waiting for transfers between devices: 20.3 us -> 22.3 us
    ppermute x14, waiting for transfers between devices: 13.4 us -> 14.9 us  [send(): return lax.ppermute(block, axis, [(i, i ^ k) for i in range(count)])]
  transfers between devices with their start and end apart: 17 -> 17, of which waited for: 9 -> 9; matrix products, arithmetic and copies ran while one was open for 0% -> 0% of each run, Pallas kernels for 19% -> 18%
where the time goes in v4:
time: 61.7 us; the launch traced here: 61.5 us
  waiting for transfers between devices  22.3 us (36%)
  starting transfers between devices  21.4 us (35%)
  Pallas kernels  17.7 us (29%)
    ppermute x14, starting transfers between devices, send(): return lax.ppermute(block, axis, [(i, i ^ k) for i in range(count)])  17.8 us
    ppermute x14, waiting for transfers between devices, send(): return lax.ppermute(block, axis, [(i, i ^ k) for i in range(count)])  14.9 us
    pallas_call x2, Pallas kernels, prepare(): pl.pallas_call(functools.partial(prepare_kernel, want_rows), out_shape=ou...  7.97 us
    ppermute x3, waiting for transfers between devices, send_freq(): return lax.ppermute(block, ('freq', 'tile'), pairs)  7.42 us
    ppermute x3, starting transfers between devices, send_freq(): return lax.ppermute(block, ('freq', 'tile'), pairs)  3.55 us
    pallas_call x2, Pallas kernels, partial_sum(): pl.pallas_call(functools.partial(partial_kernel, bases), out_shape=jax.Sh...  2.35 us
    pallas_call x1, Pallas kernels, coeff_first(): pl.pallas_call(functools.partial(coeff_first_kernel, first, rest), out_sh...  2.18 us
    pallas_call x1, Pallas kernels, coeff_rest(): pl.pallas_call(functools.partial(coeff_rest_kernel, rest), out_shape=[jax...  1.47 us
  transfers between devices with their start and end apart: 17, of which 9 were waited for; matrix products, arithmetic and copies ran while one was open for 0% of the time, Pallas kernels for 18%

profile of v4, /device:TPU:0, one launch (start us, length us, event | category | flops | bytes accessed | tf_op | source)
XLA Modules:
  0.0 61.5 jit_solution(13372718918929389066)
XLA Ops:
  0.0 2.2 %coeff_first.1 = (bf16[96,512]{1,0:T(8,128)(2,1)S(1)}, bf16[2,640,256]{2,1,0:T(8,128)(2,1)S(1)}, bf16[7,96,2,640]{3,2,1,0:T(2,128)(2,1)S(1)}, f32[7,96,128]{2,1,0:T(8,128)S(1)}) custom-call(s32[8,8]{1,0:T(8,128)} %bitcast.6, bf16[8,128,2,640]{3,2,1,0:T(2,128)(2,1)} %bitcast.9, bf16[2,640,256]{2,1,0:T(8,128)(2,1)} %bitcast.12), custom_call_target="tpu_custom_call" | custom-call | flops 1000000000 | bytes 10000000 | tf_op jit(solution)/shard_map/coeff_first/pallas_call | solution.py:113
  2.2 1.5 %coeff_rest.1 = (bf16[96,512]{1,0:T(8,128)(2,1)S(1)}, bf16[96,512]{1,0:T(8,128)(2,1)S(1)}, bf16[96,512]{1,0:T(8,128)(2,1)S(1)}, bf16[96,512]{1,0:T(8,128)(2,1)S(...) custom-call(f32[7,96,128]{2,1,0:T(8,128)S(1)} %get-tuple-element.32.refs_0_, ...), custom_call_target="tpu_custom_call" | custom-call | flops 1000000000 | bytes 10000000 | tf_op jit(solution)/shard_map/coeff_rest/pallas_call | solution.py:141
  3.7 3.1 %collective-permute-start.2 = (bf16[96,512]{1,0:T(8,128)(2,1)S(1)}, bf16[96,512]{1,0:T(8,128)(2,1)S(1)}, u32[]{:S(2)}, u32[]{:S(2)}) collective-permute-start(bf16[96,512]{1,0:T(8,128)(2,1)S(1)} %get-tuple-element.40), channel_id=1, source_target_pairs={{0,2},{1,3},{2,0},{3,1},{4,6},{5,7},{6,4},{7,5},{8,10},{9,11},{10,... | collective-permute-start | bytes 294920 | tf_op jit(solution)/shard_map/ppermute | solution.py:412
  6.8 0.2 collective-permute-start.4
  7.0 3.6 %collective-permute-start.1 = (bf16[96,512]{1,0:T(8,128)(2,1)S(1)}, bf16[96,512]{1,0:T(8,128)(2,1)S(1)}, u32[]{:S(2)}, u32[]{:S(2)}) collective-permute-start(bf16[96,512]{1,0:T(8,128)(2,1)S(1)} %get-tuple-element.35.refs_2_), channel_id=1, source_target_pairs={{0,7},{1,6},{2,5},{3,4},{4,3},{5,2},{6,1},{7,0},{8,15},{9,14},{10,... | collective-permute-start | bytes 294920 | tf_op jit(solution)/shard_map/ppermute | solution.py:412
  10.6 0.4 collective-permute-start
  11.0 1.5 %collective-permute-start.5 = (bf16[96,512]{1,0:T(8,128)(2,1)S(1)}, bf16[96,512]{1,0:T(8,128)(2,1)S(1)}, u32[]{:S(2)}, u32[]{:S(2)}) collective-permute-start(bf16[96,512]{1,0:T(8,128)(2,1)S(1)} %get-tuple-element.44), channel_id=1, source_target_pairs={{0,4},{1,5},{2,6},{3,7},{4,0},{5,1},{6,2},{7,3},{8,12},{9,13},{10,... | collective-permute-start | bytes 294920 | tf_op jit(solution)/shard_map/ppermute | solution.py:412
  12.5 1.8 %collective-permute-start.6 = (bf16[96,512]{1,0:T(8,128)(2,1)S(1)}, bf16[96,512]{1,0:T(8,128)(2,1)S(1)}, u32[]{:S(2)}, u32[]{:S(2)}) collective-permute-start(bf16[96,512]{1,0:T(8,128)(2,1)S(1)} %get-tuple-element.45), channel_id=1, source_target_pairs={{0,5},{1,4},{2,7},{3,6},{4,1},{5,0},{6,3},{7,2},{8,13},{9,12},{10,... | collective-permute-start | bytes 294920 | tf_op jit(solution)/shard_map/ppermute | solution.py:412
  14.3 4.1 %prepare.2 = (bf16[4,640,384]{2,1,0:T(8,128)(2,1)S(1)}, bf16[768,1280]{1,0:T(8,128)(2,1)S(1)}, f32[8,96,128]{2,1,0:T(8,128)S(1)}) custom-call(bf16[8,128,2,640]{3,2,1,0:T(2,128)(2,1)} %bitcast.11, s32[8,8]{1,0:T(8,128)S(1)} %bitcast.7, bf16[96,512]{1,0:T(8,128)(2,1)S(1)} %get-tuple-element.35.refs_2_), custom_call_target="tpu_custom_call" | custom-call | flops 1000000000 | bytes 10000000 | tf_op jit(solution)/shard_map/prepare/pallas_call | solution.py:200
  18.4 1.2 %partial_sum.2.refs_4_ = f32[640,512]{1,0:T(8,128)S(1)} custom-call(bf16[4,640,384]{2,1,0:T(8,128)(2,1)S(1)} %get-tuple-element.38.refs_0_.refs_2_, bf16[96,512]{1,0:T(8,128)(2,1)S(1)} %collective-permute-done.refs_1_, bf16[96,512]{1,0:T(8,128)(2,1)S(1)} %collective-permute-done.1.refs_2_, bf16[96,512]{1,0:T(8,128)(2,1)S(1)} %collective-permute-done.2.refs_3_, ...), custom_call_target="tpu_custom_call" | custom-call | flops 1000000000 | bytes 10000000 | tf_op jit(solution)/shard_map/partial_sum/pallas_call | solution.py:238
  19.6 6.7 %collective-permute-done.5.refs_5_ = bf16[96,512]{1,0:T(8,128)(2,1)S(1)} collective-permute-done((bf16[96,512]{1,0:T(8,128)(2,1)S(1)}, bf16[96,512]{1,0:T(8,128)(2,1)S(1)}, u32[]{:S(2)}, u32[]{:S(2)}) %collective-permute-start.5) | collective-permute-done | bytes 98336 | tf_op jit(solution)/shard_map/ppermute | solution.py:412
  26.3 1.7 %collective-permute-done.6.refs_6_ = bf16[96,512]{1,0:T(8,128)(2,1)S(1)} collective-permute-done((bf16[96,512]{1,0:T(8,128)(2,1)S(1)}, bf16[96,512]{1,0:T(8,128)(2,1)S(1)}, u32[]{:S(2)}, u32[]{:S(2)}) %collective-permute-start.6) | collective-permute-done | bytes 98336 | tf_op jit(solution)/shard_map/ppermute | solution.py:412
  28.0 0.9 %residual_blocks.1 = (bf16[96,512]{1,0:T(8,128)(2,1)S(1)}, bf16[96,512]{1,0:T(8,128)(2,1)S(1)}, bf16[1280,512]{1,0:T(8,128)(2,1)S(1)}) custom-call(f32[8,96,128]{2,1,0:T(8,128)S(1)} %get-tuple-element.36.refs_0_, bf16[768,1280]{1,0:T(8,128)(2,1)S(1)} %get-tuple-element.37.refs_1_, bf16[4,640,384]{2,1,0:T(8,128)(2,1)S(1)} %get-tuple-element.38.refs_0_.refs_2_, ...), custom_call_target="tpu_custom_call" | custom-call | flops 1000000000 | bytes 10000000 | tf_op jit(solution)/shard_map/residual_blocks/pallas_call | solution.py:278
  28.9 2.5 %collective-permute-start.7 = (bf16[96,512]{1,0:T(8,128)(2,1)S(1)}, bf16[96,512]{1,0:T(8,128)(2,1)S(1)}, u32[]{:S(2)}, u32[]{:S(2)}) collective-permute-start(bf16[96,512]{1,0:T(8,128)(2,1)S(1)} %get-tuple-element.47), channel_id=1, source_target_pairs={{0,6},{1,7},{2,4},{3,5},{4,2},{5,3},{6,0},{7,1},{8,14},{9,15},{10,... | collective-permute-start | bytes 294920 | tf_op jit(solution)/shard_map/ppermute | solution.py:412
  31.4 0.8 %collective-permute-start.8 = (bf16[96,512]{1,0:T(8,128)(2,1)S(1)}, bf16[96,512]{1,0:T(8,128)(2,1)S(1)}, u32[]{:S(2)}, u32[]{:S(2)}) collective-permute-start(bf16[96,512]{1,0:T(8,128)(2,1)S(1)} %get-tuple-element.48), channel_id=1, source_target_pairs={{0,7},{1,6},{2,5},{3,4},{4,3},{5,2},{6,1},{7,0},{8,15},{9,14},{10,... | collective-permute-start | bytes 294920 | tf_op jit(solution)/shard_map/ppermute | solution.py:412
  32.2 0.9 %adjoint_blocks.1 = (bf16[96,512]{1,0:T(8,128)(2,1)S(1)}, bf16[96,512]{1,0:T(8,128)(2,1)S(1)}, bf16[96,512]{1,0:T(8,128)(2,1)S(1)}, bf16[96,512]{1,0:T(8,128)(2,...) custom-call(f32[8,96,128]{2,1,0:T(8,128)S(1)} %get-tuple-element.36.refs_0_, ...), custom_call_target="tpu_custom_call" | custom-call | flops 1000000000 | bytes 10000000 | tf_op jit(solution)/shard_map/adjoint_blocks/pallas_call | solution.py:295
  33.2 2.0 %collective-permute-start.10 = (bf16[96,512]{1,0:T(8,128)(2,1)S(1)}, bf16[96,512]{1,0:T(8,128)(2,1)S(1)}, u32[]{:S(2)}, u32[]{:S(2)}) collective-permute-start(bf16[96,512]{1,0:T(8,128)(2,1)S(1)} %get-tuple-element.50), channel_id=1, source_target_pairs={{0,3},{1,2},{2,1},{3,0},{4,7},{5,6},{6,5},{7,4},{8,11},{9,10},{10,... | collective-permute-start | bytes 294920 | tf_op jit(solution)/shard_map/ppermute | solution.py:412
  35.4 0.3 collective-permute-done.7.refs_1_
  35.7 1.0 %collective-permute-start.12 = (bf16[96,512]{1,0:T(8,128)(2,1)S(1)}, bf16[96,512]{1,0:T(8,128)(2,1)S(1)}, u32[]{:S(2)}, u32[]{:S(2)}) collective-permute-start(bf16[96,512]{1,0:T(8,128)(2,1)S(1)} %get-tuple-element.53), channel_id=1, source_target_pairs={{0,4},{1,5},{2,6},{3,7},{4,0},{5,1},{6,2},{7,3},{8,12},{9,13},{10,... | collective-permute-start | bytes 294920 | tf_op jit(solution)/shard_map/ppermute | solution.py:412
  36.7 1.9 %collective-permute-done.8.refs_2_ = bf16[96,512]{1,0:T(8,128)(2,1)S(1)} collective-permute-done((bf16[96,512]{1,0:T(8,128)(2,1)S(1)}, bf16[96,512]{1,0:T(8,128)(2,1)S(1)}, u32[]{:S(2)}, u32[]{:S(2)}) %collective-permute-start.8) | collective-permute-done | bytes 98336 | tf_op jit(solution)/shard_map/ppermute | solution.py:412
  38.5 0.7 %collective-permute-start.13 = (bf16[96,512]{1,0:T(8,128)(2,1)S(1)}, bf16[96,512]{1,0:T(8,128)(2,1)S(1)}, u32[]{:S(2)}, u32[]{:S(2)}) collective-permute-start(bf16[96,512]{1,0:T(8,128)(2,1)S(1)} %get-tuple-element.54), channel_id=1, source_target_pairs={{0,5},{1,4},{2,7},{3,6},{4,1},{5,0},{6,3},{7,2},{8,13},{9,12},{10,... | collective-permute-start | bytes 294920 | tf_op jit(solution)/shard_map/ppermute | solution.py:412
  39.2 3.9 %prepare.3.refs_0_ = bf16[4,640,384]{2,1,0:T(8,128)(2,1)S(1)} custom-call(bf16[8,128,2,640]{3,2,1,0:T(2,128)(2,1)} %bitcast.10, s32[8,8]{1,0:T(8,128)S(1)} %bitcast.8, bf16[1280,512]{1,0:T(8,128)(2,1)S(1)} %get-tuple-element.46.refs_2_), custom_call_target="tpu_custom_call" | custom-call | flops 1000000000 | bytes 10000000 | tf_op jit(solution)/shard_map/prepare/pallas_call | solution.py:200
  43.1 1.9 %collective-permute-done.10.refs_4_ = bf16[96,512]{1,0:T(8,128)(2,1)S(1)} collective-permute-done((bf16[96,512]{1,0:T(8,128)(2,1)S(1)}, bf16[96,512]{1,0:T(8,128)(2,1)S(1)}, u32[]{:S(2)}, u32[]{:S(2)}) %collective-permute-start.10) | collective-permute-done | bytes 98336 | tf_op jit(solution)/shard_map/ppermute | solution.py:412
  45.0 1.2 %partial_sum.3.refs_1_ = f32[640,512]{1,0:T(8,128)S(1)} custom-call(bf16[4,640,384]{2,1,0:T(8,128)(2,1)S(1)} %prepare.3.refs_0_, bf16[96,512]{1,0:T(8,128)(2,1)S(1)} %collective-permute-done.7.refs_1_, bf16[96,512]{1,0:T(8,128)(2,1)S(1)} %collective-permute-done.8.refs_2_, bf16[96,512]{1,0:T(8,128)(2,1)S(1)} %collective-permute-done.9.refs_3_, ...), custom_call_target="tpu_custom_call" | custom-call | flops 1000000000 | bytes 10000000 | tf_op jit(solution)/shard_map/partial_sum/pallas_call | solution.py:238
  46.2 2.4 %collective-permute-done.13.refs_3_ = bf16[96,512]{1,0:T(8,128)(2,1)S(1)} collective-permute-done((bf16[96,512]{1,0:T(8,128)(2,1)S(1)}, bf16[96,512]{1,0:T(8,128)(2,1)S(1)}, u32[]{:S(2)}, u32[]{:S(2)}) %collective-permute-start.13) | collective-permute-done | bytes 98336 | tf_op jit(solution)/shard_map/ppermute | solution.py:412
  48.6 0.6 %spectrum_blocks.1 = (bf16[160,512]{1,0:T(8,128)(2,1)S(1)}, bf16[160,512]{1,0:T(8,128)(2,1)S(1)}, bf16[160,512]{1,0:T(8,128)(2,1)S(1)}, bf16[160,512]{1,0:T(8,128)(2,1)S(1)}) custom-call(bf16[4,640,384]{2,1,0:T(8,128)(2,1)S(1)} %prepare.3.refs_0_, f32[640,512]{1,0:T(8,128)S(1)} %partial_sum.3.refs_1_, bf16[96,512]{1,0:T(8,128)(2,1)S(1)} %collective-permute-done.12.refs_2_, ...), custom_call_target="tpu_custom_call" | custom-call | flops 500000000 | bytes 10000000 | tf_op jit(solution)/shard_map/spectrum_blocks/pallas_call | solution.py:331
  49.2 1.6 %collective-permute-start.14 = (bf16[160,512]{1,0:T(8,128)(2,1)S(1)}, bf16[160,512]{1,0:T(8,128)(2,1)S(1)}, u32[]{:S(2)}, u32[]{:S(2)}) collective-permute-start(bf16[160,512]{1,0:T(8,128)(2,1)S(1)} %get-tuple-element.56), channel_id=1, source_target_pairs={{0,8},{1,17},{2,10},{3,19},{4,12},{5,21},{6,14},{7,23},{8,0},{9,25... | collective-permute-start | bytes 491528 | tf_op jit(solution)/shard_map/ppermute | solution.py:423
  50.8 1.5 %collective-permute-start.15 = (bf16[160,512]{1,0:T(8,128)(2,1)S(1)}, bf16[160,512]{1,0:T(8,128)(2,1)S(1)}, u32[]{:S(2)}, u32[]{:S(2)}) collective-permute-start(bf16[160,512]{1,0:T(8,128)(2,1)S(1)} %get-tuple-element.57), channel_id=1, source_target_pairs={{0,16},{1,9},{2,18},{3,11},{4,20},{5,13},{6,22},{7,15},{8,24},{9,1... | collective-permute-start | bytes 491528 | tf_op jit(solution)/shard_map/ppermute | solution.py:423
  52.3 0.5 collective-permute-start.16
  52.8 3.2 %collective-permute-done.14.refs_2_ = bf16[160,512]{1,0:T(8,128)(2,1)S(1)} collective-permute-done((bf16[160,512]{1,0:T(8,128)(2,1)S(1)}, bf16[160,512]{1,0:T(8,128)(2,1)S(1)}, u32[]{:S(2)}, u32[]{:S(2)}) %collective-permute-start.14) | collective-permute-done | bytes 163872 | tf_op jit(solution)/shard_map/ppermute | solution.py:423
  56.1 4.1 %collective-permute-done.16.refs_4_ = bf16[160,512]{1,0:T(8,128)(2,1)S(1)} collective-permute-done((bf16[160,512]{1,0:T(8,128)(2,1)S(1)}, bf16[160,512]{1,0:T(8,128)(2,1)S(1)}, u32[]{:S(2)}, u32[]{:S(2)}) %collective-permute-start.16) | collective-permute-done | bytes 163872 | tf_op jit(solution)/shard_map/ppermute | solution.py:423
  60.2 1.3 %gated_traces.1 = f32[8,160,256]{2,1,0:T(8,128)} custom-call(s32[160,256]{1,0:T(8,128)S(1)} %copy-done.1, bf16[160,512]{1,0:T(8,128)(2,1)S(1)} %get-tuple-element.55.refs_1_, bf16[160,512]{1,0:T(8,128)(2,1)S(1)} %collective-permute-done.14.refs_2_, bf16[160,512]{1,0:T(8,128)(2,1)S(1)} %collective-permute-done.15.refs_3_, ...), custom_call_target="tpu_custom_call" | custom-call | flops 500000000 | bytes 10000000 | tf_op jit(solution)/shard_map/gated_traces/pallas_call | solution.py:393
  (18 shorter events, 0.4 us)
Async XLA Ops:
  2.2 12.1 %copy-start.2 = (s32[1,8,8]{2,1,0:T(8,128)S(1)}, s32[1,8,8]{2,1,0:T(8,128)}, u32[]{:S(2)}) copy-start(s32[1,8,8]{2,1,0:T(8,128)} %param.10) | copy-start | bytes 772
  3.7 7.3 %collective-permute-start.2 = (bf16[96,512]{1,0:T(8,128)(2,1)S(1)}, bf16[96,512]{1,0:T(8,128)(2,1)S(1)}, u32[]{:S(2)}, u32[]{:S(2)}) collective-permute-start(bf16[96,512]{1,0:T(8,128)(2,1)S(1)} %get-tuple-element.40), channel_id=1, source_target_pairs={{0,2},{1,3},{2,0},{3,1},{4,6},{5,7},{6,4},{7,5},{8,10},{9,11},{10,... | collective-permute-start | bytes 294920 | tf_op jit(solution)/shard_map/ppermute | solution.py:412
  6.8 5.7 %collective-permute-start.3 = (bf16[96,512]{1,0:T(8,128)(2,1)S(1)}, bf16[96,512]{1,0:T(8,128)(2,1)S(1)}, u32[]{:S(2)}, u32[]{:S(2)}) collective-permute-start(bf16[96,512]{1,0:T(8,128)(2,1)S(1)} %get-tuple-element.41), channel_id=1, source_target_pairs={{0,3},{1,2},{2,1},{3,0},{4,7},{5,6},{6,5},{7,4},{8,11},{9,10},{10,... | collective-permute-start | bytes 294920 | tf_op jit(solution)/shard_map/ppermute | solution.py:412
  6.8 11.6 %collective-permute-start.4 = (bf16[96,512]{1,0:T(8,128)(2,1)S(1)}, bf16[96,512]{1,0:T(8,128)(2,1)S(1)}, u32[]{:S(2)}, u32[]{:S(2)}) collective-permute-start(bf16[96,512]{1,0:T(8,128)(2,1)S(1)} %get-tuple-element.43), channel_id=1, source_target_pairs={{0,1},{1,0},{2,3},{3,2},{4,5},{5,4},{6,7},{7,6},{8,9},{9,8},{10,11... | collective-permute-start | bytes 294920 | tf_op jit(solution)/shard_map/ppermute | solution.py:412
  7.0 11.4 %collective-permute-start.1 = (bf16[96,512]{1,0:T(8,128)(2,1)S(1)}, bf16[96,512]{1,0:T(8,128)(2,1)S(1)}, u32[]{:S(2)}, u32[]{:S(2)}) collective-permute-start(bf16[96,512]{1,0:T(8,128)(2,1)S(1)} %get-tuple-element.35.refs_2_), channel_id=1, source_target_pairs={{0,7},{1,6},{2,5},{3,4},{4,3},{5,2},{6,1},{7,0},{8,15},{9,14},{10,... | collective-permute-start | bytes 294920 | tf_op jit(solution)/shard_map/ppermute | solution.py:412
  10.6 7.8 %collective-permute-start = (bf16[96,512]{1,0:T(8,128)(2,1)S(1)}, bf16[96,512]{1,0:T(8,128)(2,1)S(1)}, u32[]{:S(2)}, u32[]{:S(2)}) collective-permute-start(bf16[96,512]{1,0:T(8,128)(2,1)S(1)} %get-tuple-element.39), channel_id=1, source_target_pairs={{0,6},{1,7},{2,4},{3,5},{4,2},{5,3},{6,0},{7,1},{8,14},{9,15},{10,... | collective-permute-start | bytes 294920 | tf_op jit(solution)/shard_map/ppermute | solution.py:412
  11.0 15.3 %collective-permute-start.5 = (bf16[96,512]{1,0:T(8,128)(2,1)S(1)}, bf16[96,512]{1,0:T(8,128)(2,1)S(1)}, u32[]{:S(2)}, u32[]{:S(2)}) collective-permute-start(bf16[96,512]{1,0:T(8,128)(2,1)S(1)} %get-tuple-element.44), channel_id=1, source_target_pairs={{0,4},{1,5},{2,6},{3,7},{4,0},{5,1},{6,2},{7,3},{8,12},{9,13},{10,... | collective-permute-start | bytes 294920 | tf_op jit(solution)/shard_map/ppermute | solution.py:412
  12.5 15.5 %collective-permute-start.6 = (bf16[96,512]{1,0:T(8,128)(2,1)S(1)}, bf16[96,512]{1,0:T(8,128)(2,1)S(1)}, u32[]{:S(2)}, u32[]{:S(2)}) collective-permute-start(bf16[96,512]{1,0:T(8,128)(2,1)S(1)} %get-tuple-element.45), channel_id=1, source_target_pairs={{0,5},{1,4},{2,7},{3,6},{4,1},{5,0},{6,3},{7,2},{8,13},{9,12},{10,... | collective-permute-start | bytes 294920 | tf_op jit(solution)/shard_map/ppermute | solution.py:412
  18.4 9.7 %copy-start = (bf16[1,2,640,256]{3,2,1,0:T(8,128)(2,1)S(1)}, bf16[1,2,640,256]{3,2,1,0:T(8,128)(2,1)}, u32[]{:S(2)}) copy-start(bf16[1,2,640,256]{3,2,1,0:T(8,128)(2,1)} %param.7) | copy-start | bytes 1966084
  28.9 6.8 %collective-permute-start.7 = (bf16[96,512]{1,0:T(8,128)(2,1)S(1)}, bf16[96,512]{1,0:T(8,128)(2,1)S(1)}, u32[]{:S(2)}, u32[]{:S(2)}) collective-permute-start(bf16[96,512]{1,0:T(8,128)(2,1)S(1)} %get-tuple-element.47), channel_id=1, source_target_pairs={{0,6},{1,7},{2,4},{3,5},{4,2},{5,3},{6,0},{7,1},{8,14},{9,15},{10,... | collective-permute-start | bytes 294920 | tf_op jit(solution)/shard_map/ppermute | solution.py:412
  31.4 7.1 %collective-permute-start.8 = (bf16[96,512]{1,0:T(8,128)(2,1)S(1)}, bf16[96,512]{1,0:T(8,128)(2,1)S(1)}, u32[]{:S(2)}, u32[]{:S(2)}) collective-permute-start(bf16[96,512]{1,0:T(8,128)(2,1)S(1)} %get-tuple-element.48), channel_id=1, source_target_pairs={{0,7},{1,6},{2,5},{3,4},{4,3},{5,2},{6,1},{7,0},{8,15},{9,14},{10,... | collective-permute-start | bytes 294920 | tf_op jit(solution)/shard_map/ppermute | solution.py:412
  33.2 10.0 %collective-permute-start.9 = (bf16[96,512]{1,0:T(8,128)(2,1)S(1)}, bf16[96,512]{1,0:T(8,128)(2,1)S(1)}, u32[]{:S(2)}, u32[]{:S(2)}) collective-permute-start(bf16[96,512]{1,0:T(8,128)(2,1)S(1)} %get-tuple-element.49), channel_id=1, source_target_pairs={{0,2},{1,3},{2,0},{3,1},{4,6},{5,7},{6,4},{7,5},{8,10},{9,11},{10,... | collective-permute-start | bytes 294920 | tf_op jit(solution)/shard_map/ppermute | solution.py:412
  33.2 11.8 %collective-permute-start.10 = (bf16[96,512]{1,0:T(8,128)(2,1)S(1)}, bf16[96,512]{1,0:T(8,128)(2,1)S(1)}, u32[]{:S(2)}, u32[]{:S(2)}) collective-permute-start(bf16[96,512]{1,0:T(8,128)(2,1)S(1)} %get-tuple-element.50), channel_id=1, source_target_pairs={{0,3},{1,2},{2,1},{3,0},{4,7},{5,6},{6,5},{7,4},{8,11},{9,10},{10,... | collective-permute-start | bytes 294920 | tf_op jit(solution)/shard_map/ppermute | solution.py:412
  35.2 9.8 %collective-permute-start.11 = (bf16[96,512]{1,0:T(8,128)(2,1)S(1)}, bf16[96,512]{1,0:T(8,128)(2,1)S(1)}, u32[]{:S(2)}, u32[]{:S(2)}) collective-permute-start(bf16[96,512]{1,0:T(8,128)(2,1)S(1)} %get-tuple-element.52), channel_id=1, source_target_pairs={{0,1},{1,0},{2,3},{3,2},{4,5},{5,4},{6,7},{7,6},{8,9},{9,8},{10,11... | collective-permute-start | bytes 294920 | tf_op jit(solution)/shard_map/ppermute | solution.py:412
  35.7 10.5 %collective-permute-start.12 = (bf16[96,512]{1,0:T(8,128)(2,1)S(1)}, bf16[96,512]{1,0:T(8,128)(2,1)S(1)}, u32[]{:S(2)}, u32[]{:S(2)}) collective-permute-start(bf16[96,512]{1,0:T(8,128)(2,1)S(1)} %get-tuple-element.53), channel_id=1, source_target_pairs={{0,4},{1,5},{2,6},{3,7},{4,0},{5,1},{6,2},{7,3},{8,12},{9,13},{10,... | collective-permute-start | bytes 294920 | tf_op jit(solution)/shard_map/ppermute | solution.py:412
  38.5 10.1 %collective-permute-start.13 = (bf16[96,512]{1,0:T(8,128)(2,1)S(1)}, bf16[96,512]{1,0:T(8,128)(2,1)S(1)}, u32[]{:S(2)}, u32[]{:S(2)}) collective-permute-start(bf16[96,512]{1,0:T(8,128)(2,1)S(1)} %get-tuple-element.54), channel_id=1, source_target_pairs={{0,5},{1,4},{2,7},{3,6},{4,1},{5,0},{6,3},{7,2},{8,13},{9,12},{10,... | collective-permute-start | bytes 294920 | tf_op jit(solution)/shard_map/ppermute | solution.py:412
  46.2 14.0 %copy-start.1 = (s32[160,256]{1,0:T(8,128)S(1)}, s32[160,256]{1,0:T(8,128)}, u32[]{:S(2)}) copy-start(s32[160,256]{1,0:T(8,128)} %refs_0_.1) | copy-start | bytes 491524
  49.2 6.8 %collective-permute-start.14 = (bf16[160,512]{1,0:T(8,128)(2,1)S(1)}, bf16[160,512]{1,0:T(8,128)(2,1)S(1)}, u32[]{:S(2)}, u32[]{:S(2)}) collective-permute-start(bf16[160,512]{1,0:T(8,128)(2,1)S(1)} %get-tuple-element.56), channel_id=1, source_target_pairs={{0,8},{1,17},{2,10},{3,19},{4,12},{5,21},{6,14},{7,23},{8,0},{9,25... | collective-permute-start | bytes 491528 | tf_op jit(solution)/shard_map/ppermute | solution.py:423
  50.8 5.3 %collective-permute-start.15 = (bf16[160,512]{1,0:T(8,128)(2,1)S(1)}, bf16[160,512]{1,0:T(8,128)(2,1)S(1)}, u32[]{:S(2)}, u32[]{:S(2)}) collective-permute-start(bf16[160,512]{1,0:T(8,128)(2,1)S(1)} %get-tuple-element.57), channel_id=1, source_target_pairs={{0,16},{1,9},{2,18},{3,11},{4,20},{5,13},{6,22},{7,15},{8,24},{9,1... | collective-permute-start | bytes 491528 | tf_op jit(solution)/shard_map/ppermute | solution.py:423
  52.3 7.9 %collective-permute-start.16 = (bf16[160,512]{1,0:T(8,128)(2,1)S(1)}, bf16[160,512]{1,0:T(8,128)(2,1)S(1)}, u32[]{:S(2)}, u32[]{:S(2)}) collective-permute-start(bf16[160,512]{1,0:T(8,128)(2,1)S(1)} %get-tuple-element.58), channel_id=1, source_target_pairs={{0,24},{1,25},{2,26},{3,27},{4,28},{5,29},{6,30},{7,31},{8,16},{9,... | collective-permute-start | bytes 491528 | tf_op jit(solution)/shard_map/ppermute | solution.py:423

commit v5 on v3

--- a/solution.py
+++ b/solution.py
@@ -22,19 +22,6 @@
 
 def params():
     return pltpu.CompilerParams(vmem_limit_bytes=20 * 1024 * 1024)
-
-
-def swapped(k, freqs):
-    bits = freqs.bit_length() - 1
-    if bits % 2:
-        return k
-    half = bits // 2
-    return (k % (1 << half) << half) | (k >> half)
-
-
-def freq_peer(k, freqs):
-    turn = jnp.where(lax.axis_index("tile") % 2 == 0, k, swapped(k, freqs))
-    return lax.axis_index("freq") ^ turn
 
 
 def level_mask(rank):
@@ -308,6 +295,7 @@
     pair = refs[2:4]
     outs = refs[4 : 4 + freqs]
     spectrum = refs[4 + freqs]
+    mine = lax.axis_index("freq")
     virtual = partial_ref.shape[1] // 2
     width = outs[0].shape[1] // 2
     real = slice(chunk * width, (chunk + 1) * width)
@@ -321,7 +309,7 @@
     spectrum[:, width:] = partial_ref[:, imag] + late[:, width:]
     share = outs[0].shape[0]
     for k in range(freqs):
-        rows = pl.ds(pl.multiple_of(freq_peer(k, freqs) * share, 8), share)
+        rows = pl.ds(pl.multiple_of((mine ^ k) * share, 8), share)
         outs[k][...] = spectrum[rows, :].astype(BF16)
 
 
@@ -346,8 +334,9 @@
     onset_ref = refs[0]
     blocks = refs[1 : 1 + freqs]
     out_hbm, gathered, traces, sems = refs[-4:]
+    mine = lax.axis_index("freq")
     for k in range(freqs):
-        gathered[freq_peer(k, freqs)] = blocks[k][...]
+        gathered[mine ^ k] = blocks[k][...]
     times = 2 * freqs
     scaling = 1.0 / math.sqrt(freqs)
     width = blocks[0].shape[1] // 2
@@ -412,17 +401,6 @@
     return lax.ppermute(block, axis, [(i, i ^ k) for i in range(count)])
 
 
-def send_freq(block, k):
-    count = lax.axis_size("tile")
-    freqs = lax.axis_size("freq")
-    pairs = [
-        (f * count + tile, (f ^ (swapped(k, freqs) if tile % 2 else k)) * count + tile)
-        for f in range(freqs)
-        for tile in range(count)
-    ]
-    return lax.ppermute(block, ("freq", "tile"), pairs)
-
-
 def exchange(ks, blocks):
     return {k: send(b, "tile", k) if k else b for k, b in zip(ks, blocks)}
 
@@ -468,13 +446,15 @@
     blocks = adjoint_blocks(masks, u_rows, stacked, rest)
     returned |= exchange(rest, blocks)
     (v_turned,) = prepare(v, table, stacked, False)
+    late = first[0]
+    early = tuple(base for base in pair_bases(count) if base != late)
     partial = partial_sum(v_turned, early, pick(returned, early))
     spectra = []
     for chunk in range(CHUNKS):
         blocks = spectrum_blocks(
             v_turned, partial, late, pick(returned, (late,)), freqs, chunk
         )
-        spectra.append([send_freq(b, k) if k else b for k, b in enumerate(blocks)])
+        spectra.append([send(b, "freq", k) if k else b for k, b in enumerate(blocks)])
     result = None
     for chunk, blocks in enumerate(spectra):
         result = gated_traces(onset, blocks, chunk, result)

time: 60.1 us -> 61.3 us (1.020)
  waiting for transfers between devices: 20.3 us -> 21.2 us
    ppermute x14 -> x17, waiting for transfers between devices: 13.4 us -> 21.2 us  [send(): return lax.ppermute(block, axis, [(i, i ^ k) for i in range(count)])]
    ppermute x3 -> x0, waiting for transfers between devices: 6.93 us -> none  [send_freq(): return lax.ppermute(block, ('freq', 'tile'), pairs)]
    ppermute x14 -> x17, starting transfers between devices: 18.2 us -> 22 us  [send(): return lax.ppermute(block, axis, [(i, i ^ k) for i in range(count)])]
    ppermute x3 -> x0, starting transfers between devices: 3.55 us -> none  [send_freq(): return lax.ppermute(block, ('freq', 'tile'), pairs)]
  transfers between devices with their start and end apart: 17 -> 17, of which waited for: 9 -> 5; matrix products, arithmetic and copies ran while one was open for 0% -> 0% of each run, Pallas kernels for 19% -> 17%
where the time goes in v5:
time: 61.3 us; the launch traced here: 61.1 us
  starting transfers between devices  22 us (36%)
  waiting for transfers between devices  21.2 us (35%)
  Pallas kernels  17.7 us (29%)
    ppermute x17, starting transfers between devices, send(): return lax.ppermute(block, axis, [(i, i ^ k) for i in range(count)])  22 us
    ppermute x17, waiting for transfers between devices, send(): return lax.ppermute(block, axis, [(i, i ^ k) for i in range(count)])  21.2 us
    pallas_call x2, Pallas kernels, prepare(): pl.pallas_call(functools.partial(prepare_kernel, want_rows), out_shape=ou...  7.97 us
    pallas_call x2, Pallas kernels, partial_sum(): pl.pallas_call(functools.partial(partial_kernel, bases), out_shape=jax.Sh...  2.35 us
    pallas_call x1, Pallas kernels, coeff_first(): pl.pallas_call(functools.partial(coeff_first_kernel, first, rest), out_sh...  2.35 us
    pallas_call x1, Pallas kernels, gated_traces(): pl.pallas_call(functools.partial(traces_kernel, freqs, chunk), out_shape=...  1.34 us
    pallas_call x1, Pallas kernels, coeff_rest(): pl.pallas_call(functools.partial(coeff_rest_kernel, rest), out_shape=[jax...  1.26 us
  transfers between devices with their start and end apart: 17, of which 5 were waited for; matrix products, arithmetic and copies ran while one was open for 0% of the time, Pallas kernels for 17%

profile of v5, /device:TPU:0, one launch (start us, length us, event | category | flops | bytes accessed | tf_op | source)
XLA Modules:
  0.0 61.1 jit_solution(5173434317416950556)
XLA Ops:
  0.0 2.4 %coeff_first.1 = (bf16[96,512]{1,0:T(8,128)(2,1)S(1)}, bf16[96,512]{1,0:T(8,128)(2,1)S(1)}, bf16[2,640,256]{2,1,0:T(8,128)(2,1)S(1)}, bf16[6,96,2,640]{3,2,1,0:T(2,128)(2,1)S(1)}, f32[6,96,128]{2,1,0:T(8,128)S(1)}) custom-call(s32[8,8]{1,0:T(8,128)} %bitcast.6, bf16[8,128,2,640]{3,2,1,0:T(2,128)(2,1)} %bitcast.9, bf16[2,640,256]{2,1,0:T(8,128)(2,1)} %bitcast.12), custom_call_target="tpu_custom_call" | custom-call | flops 1000000000 | bytes 10000000 | tf_op jit(solution)/shard_map/coeff_first/pallas_call | solution.py:100
  2.4 0.0 copy-start.2
  2.4 1.3 %coeff_rest.1 = (bf16[96,512]{1,0:T(8,128)(2,1)S(1)}, bf16[96,512]{1,0:T(8,128)(2,1)S(1)}, bf16[96,512]{1,0:T(8,128)(2,1)S(1)}, bf16[96,512]{1,0:T(8,128)(2,1)S(...) custom-call(f32[6,96,128]{2,1,0:T(8,128)S(1)} %get-tuple-element.32.refs_0_, ...), custom_call_target="tpu_custom_call" | custom-call | flops 1000000000 | bytes 10000000 | tf_op jit(solution)/shard_map/coeff_rest/pallas_call | solution.py:128
  3.6 3.1 %collective-permute-start.2 = (bf16[96,512]{1,0:T(8,128)(2,1)S(1)}, bf16[96,512]{1,0:T(8,128)(2,1)S(1)}, u32[]{:S(2)}, u32[]{:S(2)}) collective-permute-start(bf16[96,512]{1,0:T(8,128)(2,1)S(1)} %get-tuple-element.41), channel_id=1, source_target_pairs={{0,2},{1,3},{2,0},{3,1},{4,6},{5,7},{6,4},{7,5},{8,10},{9,11},{10,... | collective-permute-start | bytes 294920 | tf_op jit(solution)/shard_map/ppermute | solution.py:401
  6.8 0.2 collective-permute-start.4
  7.0 4.0 %collective-permute-start = (bf16[96,512]{1,0:T(8,128)(2,1)S(1)}, bf16[96,512]{1,0:T(8,128)(2,1)S(1)}, u32[]{:S(2)}, u32[]{:S(2)}) collective-permute-start(bf16[96,512]{1,0:T(8,128)(2,1)S(1)} %get-tuple-element.39), channel_id=1, source_target_pairs={{0,6},{1,7},{2,4},{3,5},{4,2},{5,3},{6,0},{7,1},{8,14},{9,15},{10,... | collective-permute-start | bytes 294920 | tf_op jit(solution)/shard_map/ppermute | solution.py:401
  10.9 0.7 %collective-permute-start.6 = (bf16[96,512]{1,0:T(8,128)(2,1)S(1)}, bf16[96,512]{1,0:T(8,128)(2,1)S(1)}, u32[]{:S(2)}, u32[]{:S(2)}) collective-permute-start(bf16[96,512]{1,0:T(8,128)(2,1)S(1)} %get-tuple-element.45), channel_id=1, source_target_pairs={{0,5},{1,4},{2,7},{3,6},{4,1},{5,0},{6,3},{7,2},{8,13},{9,12},{10,... | collective-permute-start | bytes 294920 | tf_op jit(solution)/shard_map/ppermute | solution.py:401
  11.7 2.8 %collective-permute-start.5 = (bf16[96,512]{1,0:T(8,128)(2,1)S(1)}, bf16[96,512]{1,0:T(8,128)(2,1)S(1)}, u32[]{:S(2)}, u32[]{:S(2)}) collective-permute-start(bf16[96,512]{1,0:T(8,128)(2,1)S(1)} %get-tuple-element.35.refs_2_), channel_id=1, source_target_pairs={{0,4},{1,5},{2,6},{3,7},{4,0},{5,1},{6,2},{7,3},{8,12},{9,13},{10,... | collective-permute-start | bytes 294920 | tf_op jit(solution)/shard_map/ppermute | solution.py:401
  14.4 4.1 %prepare.2 = (bf16[4,640,384]{2,1,0:T(8,128)(2,1)S(1)}, bf16[768,1280]{1,0:T(8,128)(2,1)S(1)}, f32[8,96,128]{2,1,0:T(8,128)S(1)}) custom-call(bf16[8,128,2,640]{3,2,1,0:T(2,128)(2,1)} %bitcast.11, s32[8,8]{1,0:T(8,128)S(1)} %bitcast.7, bf16[96,512]{1,0:T(8,128)(2,1)S(1)} %get-tuple-element.35.refs_2_), custom_call_target="tpu_custom_call" | custom-call | flops 1000000000 | bytes 10000000 | tf_op jit(solution)/shard_map/prepare/pallas_call | solution.py:187
  18.5 0.0 copy-start
  18.6 1.2 %partial_sum.2.refs_4_ = f32[640,512]{1,0:T(8,128)S(1)} custom-call(bf16[4,640,384]{2,1,0:T(8,128)(2,1)S(1)} %get-tuple-element.38.refs_0_.refs_2_, bf16[96,512]{1,0:T(8,128)(2,1)S(1)} %collective-permute-done.refs_1_, bf16[96,512]{1,0:T(8,128)(2,1)S(1)} %collective-permute-done.1.refs_2_, bf16[96,512]{1,0:T(8,128)(2,1)S(1)} %collective-permute-done.2.refs_3_, ...), custom_call_target="tpu_custom_call" | custom-call | flops 1000000000 | bytes 10000000 | tf_op jit(solution)/shard_map/partial_sum/pallas_call | solution.py:225
  19.7 5.8 %collective-permute-done.6.refs_6_ = bf16[96,512]{1,0:T(8,128)(2,1)S(1)} collective-permute-done((bf16[96,512]{1,0:T(8,128)(2,1)S(1)}, bf16[96,512]{1,0:T(8,128)(2,1)S(1)}, u32[]{:S(2)}, u32[]{:S(2)}) %collective-permute-start.6) | collective-permute-done | bytes 98336 | tf_op jit(solution)/shard_map/ppermute | solution.py:401
  25.5 2.2 %collective-permute-done.5.refs_5_ = bf16[96,512]{1,0:T(8,128)(2,1)S(1)} collective-permute-done((bf16[96,512]{1,0:T(8,128)(2,1)S(1)}, bf16[96,512]{1,0:T(8,128)(2,1)S(1)}, u32[]{:S(2)}, u32[]{:S(2)}) %collective-permute-start.5) | collective-permute-done | bytes 98336 | tf_op jit(solution)/shard_map/ppermute | solution.py:401
  27.8 0.9 %residual_blocks.1 = (bf16[96,512]{1,0:T(8,128)(2,1)S(1)}, bf16[96,512]{1,0:T(8,128)(2,1)S(1)}, bf16[1280,512]{1,0:T(8,128)(2,1)S(1)}) custom-call(f32[8,96,128]{2,1,0:T(8,128)S(1)} %get-tuple-element.36.refs_0_, bf16[768,1280]{1,0:T(8,128)(2,1)S(1)} %get-tuple-element.37.refs_1_, bf16[4,640,384]{2,1,0:T(8,128)(2,1)S(1)} %get-tuple-element.38.refs_0_.refs_2_, ...), custom_call_target="tpu_custom_call" | custom-call | flops 1000000000 | bytes 10000000 | tf_op jit(solution)/shard_map/residual_blocks/pallas_call | solution.py:265
  28.6 0.9 %adjoint_blocks.1 = (bf16[96,512]{1,0:T(8,128)(2,1)S(1)}, bf16[96,512]{1,0:T(8,128)(2,1)S(1)}, bf16[96,512]{1,0:T(8,128)(2,1)S(1)}, bf16[96,512]{1,0:T(8,128)(2,...) custom-call(f32[8,96,128]{2,1,0:T(8,128)S(1)} %get-tuple-element.36.refs_0_, ...), custom_call_target="tpu_custom_call" | custom-call | flops 1000000000 | bytes 10000000 | tf_op jit(solution)/shard_map/adjoint_blocks/pallas_call | solution.py:282
  29.6 0.1 collective-permute-start.7
  29.7 2.2 %collective-permute-start.8 = (bf16[96,512]{1,0:T(8,128)(2,1)S(1)}, bf16[96,512]{1,0:T(8,128)(2,1)S(1)}, u32[]{:S(2)}, u32[]{:S(2)}) collective-permute-start(bf16[96,512]{1,0:T(8,128)(2,1)S(1)} %get-tuple-element.48), channel_id=1, source_target_pairs={{0,5},{1,4},{2,7},{3,6},{4,1},{5,0},{6,3},{7,2},{8,13},{9,12},{10,... | collective-permute-start | bytes 294920 | tf_op jit(solution)/shard_map/ppermute | solution.py:401
  31.9 0.8 %collective-permute-start.9 = (bf16[96,512]{1,0:T(8,128)(2,1)S(1)}, bf16[96,512]{1,0:T(8,128)(2,1)S(1)}, u32[]{:S(2)}, u32[]{:S(2)}) collective-permute-start(bf16[96,512]{1,0:T(8,128)(2,1)S(1)} %get-tuple-element.49), channel_id=1, source_target_pairs={{0,2},{1,3},{2,0},{3,1},{4,6},{5,7},{6,4},{7,5},{8,10},{9,11},{10,... | collective-permute-start | bytes 294920 | tf_op jit(solution)/shard_map/ppermute | solution.py:401
  32.7 1.3 %collective-permute-start.10 = (bf16[96,512]{1,0:T(8,128)(2,1)S(1)}, bf16[96,512]{1,0:T(8,128)(2,1)S(1)}, u32[]{:S(2)}, u32[]{:S(2)}) collective-permute-start(bf16[96,512]{1,0:T(8,128)(2,1)S(1)} %get-tuple-element.50), channel_id=1, source_target_pairs={{0,3},{1,2},{2,1},{3,0},{4,7},{5,6},{6,5},{7,4},{8,11},{9,10},{10,... | collective-permute-start | bytes 294920 | tf_op jit(solution)/shard_map/ppermute | solution.py:401
  34.0 5.1 %collective-permute-done.7.refs_1_ = bf16[96,512]{1,0:T(8,128)(2,1)S(1)} collective-permute-done((bf16[96,512]{1,0:T(8,128)(2,1)S(1)}, bf16[96,512]{1,0:T(8,128)(2,1)S(1)}, u32[]{:S(2)}, u32[]{:S(2)}) %collective-permute-start.7) | collective-permute-done | bytes 98336 | tf_op jit(solution)/shard_map/ppermute | solution.py:401
  39.1 1.8 %collective-permute-start.12 = (bf16[96,512]{1,0:T(8,128)(2,1)S(1)}, bf16[96,512]{1,0:T(8,128)(2,1)S(1)}, u32[]{:S(2)}, u32[]{:S(2)}) collective-permute-start(bf16[96,512]{1,0:T(8,128)(2,1)S(1)} %get-tuple-element.53), channel_id=1, source_target_pairs={{0,6},{1,7},{2,4},{3,5},{4,2},{5,3},{6,0},{7,1},{8,14},{9,15},{10,... | collective-permute-start | bytes 294920 | tf_op jit(solution)/shard_map/ppermute | solution.py:401
  40.9 1.5 %collective-permute-start.13 = (bf16[96,512]{1,0:T(8,128)(2,1)S(1)}, bf16[96,512]{1,0:T(8,128)(2,1)S(1)}, u32[]{:S(2)}, u32[]{:S(2)}) collective-permute-start(bf16[96,512]{1,0:T(8,128)(2,1)S(1)} %get-tuple-element.54), channel_id=1, source_target_pairs={{0,7},{1,6},{2,5},{3,4},{4,3},{5,2},{6,1},{7,0},{8,15},{9,14},{10,... | collective-permute-start | bytes 294920 | tf_op jit(solution)/shard_map/ppermute | solution.py:401
  42.4 3.9 %prepare.3.refs_0_ = bf16[4,640,384]{2,1,0:T(8,128)(2,1)S(1)} custom-call(bf16[8,128,2,640]{3,2,1,0:T(2,128)(2,1)} %bitcast.10, s32[8,8]{1,0:T(8,128)S(1)} %bitcast.8, bf16[1280,512]{1,0:T(8,128)(2,1)S(1)} %get-tuple-element.46.refs_2_), custom_call_target="tpu_custom_call" | custom-call | flops 1000000000 | bytes 10000000 | tf_op jit(solution)/shard_map/prepare/pallas_call | solution.py:187
  46.3 1.2 %partial_sum.3.refs_1_ = f32[640,512]{1,0:T(8,128)S(1)} custom-call(bf16[4,640,384]{2,1,0:T(8,128)(2,1)S(1)} %prepare.3.refs_0_, bf16[96,512]{1,0:T(8,128)(2,1)S(1)} %collective-permute-done.7.refs_1_, bf16[96,512]{1,0:T(8,128)(2,1)S(1)} %collective-permute-done.8.refs_2_, bf16[96,512]{1,0:T(8,128)(2,1)S(1)} %collective-permute-done.9.refs_3_, ...), custom_call_target="tpu_custom_call" | custom-call | flops 1000000000 | bytes 10000000 | tf_op jit(solution)/shard_map/partial_sum/pallas_call | solution.py:225
  47.5 0.0 copy-start.1
  47.5 0.6 %spectrum_blocks.1 = (bf16[160,512]{1,0:T(8,128)(2,1)S(1)}, bf16[160,512]{1,0:T(8,128)(2,1)S(1)}, bf16[160,512]{1,0:T(8,128)(2,1)S(1)}, bf16[160,512]{1,0:T(8,128)(2,1)S(1)}) custom-call(bf16[4,640,384]{2,1,0:T(8,128)(2,1)S(1)} %prepare.3.refs_0_, f32[640,512]{1,0:T(8,128)S(1)} %partial_sum.3.refs_1_, bf16[96,512]{1,0:T(8,128)(2,1)S(1)} %collective-permute-done.12.refs_2_, ...), custom_call_target="tpu_custom_call" | custom-call | flops 500000000 | bytes 10000000 | tf_op jit(solution)/shard_map/spectrum_blocks/pallas_call | solution.py:319
  48.2 1.6 %collective-permute-start.14 = (bf16[160,512]{1,0:T(8,128)(2,1)S(1)}, bf16[160,512]{1,0:T(8,128)(2,1)S(1)}, u32[]{:S(2)}, u32[]{:S(2)}) collective-permute-start(bf16[160,512]{1,0:T(8,128)(2,1)S(1)} %get-tuple-element.56), channel_id=1, source_target_pairs={{0,8},{8,0},{16,24},{24,16},{1,9},{9,1},{17,25},{25,17},{2,10},{10... | collective-permute-start | bytes 491528 | tf_op jit(solution)/shard_map/ppermute | solution.py:401
  49.7 1.5 %collective-permute-start.15 = (bf16[160,512]{1,0:T(8,128)(2,1)S(1)}, bf16[160,512]{1,0:T(8,128)(2,1)S(1)}, u32[]{:S(2)}, u32[]{:S(2)}) collective-permute-start(bf16[160,512]{1,0:T(8,128)(2,1)S(1)} %get-tuple-element.57), channel_id=1, source_target_pairs={{0,16},{8,24},{16,0},{24,8},{1,17},{9,25},{17,1},{25,9},{2,18},{10... | collective-permute-start | bytes 491528 | tf_op jit(solution)/shard_map/ppermute | solution.py:401
  51.2 0.5 collective-permute-start.16
  51.7 3.6 %collective-permute-done.14.refs_2_ = bf16[160,512]{1,0:T(8,128)(2,1)S(1)} collective-permute-done((bf16[160,512]{1,0:T(8,128)(2,1)S(1)}, bf16[160,512]{1,0:T(8,128)(2,1)S(1)}, u32[]{:S(2)}, u32[]{:S(2)}) %collective-permute-start.14) | collective-permute-done | bytes 163872 | tf_op jit(solution)/shard_map/ppermute | solution.py:401
  55.3 4.5 %collective-permute-done.15.refs_3_ = bf16[160,512]{1,0:T(8,128)(2,1)S(1)} collective-permute-done((bf16[160,512]{1,0:T(8,128)(2,1)S(1)}, bf16[160,512]{1,0:T(8,128)(2,1)S(1)}, u32[]{:S(2)}, u32[]{:S(2)}) %collective-permute-start.15) | collective-permute-done | bytes 163872 | tf_op jit(solution)/shard_map/ppermute | solution.py:401
  59.8 1.3 %gated_traces.1 = f32[8,160,256]{2,1,0:T(8,128)} custom-call(s32[160,256]{1,0:T(8,128)S(1)} %copy-done.1, bf16[160,512]{1,0:T(8,128)(2,1)S(1)} %get-tuple-element.55.refs_1_, bf16[160,512]{1,0:T(8,128)(2,1)S(1)} %collective-permute-done.14.refs_2_, bf16[160,512]{1,0:T(8,128)(2,1)S(1)} %collective-permute-done.15.refs_3_, ...), custom_call_target="tpu_custom_call" | custom-call | flops 500000000 | bytes 10000000 | tf_op jit(solution)/shard_map/gated_traces/pallas_call | solution.py:382
  (18 shorter events, 0.0 us)
Async XLA Ops:
  2.4 12.1 %copy-start.2 = (s32[1,8,8]{2,1,0:T(8,128)S(1)}, s32[1,8,8]{2,1,0:T(8,128)}, u32[]{:S(2)}) copy-start(s32[1,8,8]{2,1,0:T(8,128)} %param.10) | copy-start | bytes 772
  3.6 7.3 %collective-permute-start.2 = (bf16[96,512]{1,0:T(8,128)(2,1)S(1)}, bf16[96,512]{1,0:T(8,128)(2,1)S(1)}, u32[]{:S(2)}, u32[]{:S(2)}) collective-permute-start(bf16[96,512]{1,0:T(8,128)(2,1)S(1)} %get-tuple-element.41), channel_id=1, source_target_pairs={{0,2},{1,3},{2,0},{3,1},{4,6},{5,7},{6,4},{7,5},{8,10},{9,11},{10,... | collective-permute-start | bytes 294920 | tf_op jit(solution)/shard_map/ppermute | solution.py:401
  6.8 4.9 %collective-permute-start.3 = (bf16[96,512]{1,0:T(8,128)(2,1)S(1)}, bf16[96,512]{1,0:T(8,128)(2,1)S(1)}, u32[]{:S(2)}, u32[]{:S(2)}) collective-permute-start(bf16[96,512]{1,0:T(8,128)(2,1)S(1)} %get-tuple-element.42), channel_id=1, source_target_pairs={{0,3},{1,2},{2,1},{3,0},{4,7},{5,6},{6,5},{7,4},{8,11},{9,10},{10,... | collective-permute-start | bytes 294920 | tf_op jit(solution)/shard_map/ppermute | solution.py:401
  6.8 11.8 %collective-permute-start.4 = (bf16[96,512]{1,0:T(8,128)(2,1)S(1)}, bf16[96,512]{1,0:T(8,128)(2,1)S(1)}, u32[]{:S(2)}, u32[]{:S(2)}) collective-permute-start(bf16[96,512]{1,0:T(8,128)(2,1)S(1)} %get-tuple-element.44), channel_id=1, source_target_pairs={{0,1},{1,0},{2,3},{3,2},{4,5},{5,4},{6,7},{7,6},{8,9},{9,8},{10,11... | collective-permute-start | bytes 294920 | tf_op jit(solution)/shard_map/ppermute | solution.py:401
  7.0 11.6 %collective-permute-start = (bf16[96,512]{1,0:T(8,128)(2,1)S(1)}, bf16[96,512]{1,0:T(8,128)(2,1)S(1)}, u32[]{:S(2)}, u32[]{:S(2)}) collective-permute-start(bf16[96,512]{1,0:T(8,128)(2,1)S(1)} %get-tuple-element.39), channel_id=1, source_target_pairs={{0,6},{1,7},{2,4},{3,5},{4,2},{5,3},{6,0},{7,1},{8,14},{9,15},{10,... | collective-permute-start | bytes 294920 | tf_op jit(solution)/shard_map/ppermute | solution.py:401
  10.9 7.6 %collective-permute-start.1 = (bf16[96,512]{1,0:T(8,128)(2,1)S(1)}, bf16[96,512]{1,0:T(8,128)(2,1)S(1)}, u32[]{:S(2)}, u32[]{:S(2)}) collective-permute-start(bf16[96,512]{1,0:T(8,128)(2,1)S(1)} %get-tuple-element.40), channel_id=1, source_target_pairs={{0,7},{1,6},{2,5},{3,4},{4,3},{5,2},{6,1},{7,0},{8,15},{9,14},{10,... | collective-permute-start | bytes 294920 | tf_op jit(solution)/shard_map/ppermute | solution.py:401
  10.9 14.6 %collective-permute-start.6 = (bf16[96,512]{1,0:T(8,128)(2,1)S(1)}, bf16[96,512]{1,0:T(8,128)(2,1)S(1)}, u32[]{:S(2)}, u32[]{:S(2)}) collective-permute-start(bf16[96,512]{1,0:T(8,128)(2,1)S(1)} %get-tuple-element.45), channel_id=1, source_target_pairs={{0,5},{1,4},{2,7},{3,6},{4,1},{5,0},{6,3},{7,2},{8,13},{9,12},{10,... | collective-permute-start | bytes 294920 | tf_op jit(solution)/shard_map/ppermute | solution.py:401
  11.7 16.1 %collective-permute-start.5 = (bf16[96,512]{1,0:T(8,128)(2,1)S(1)}, bf16[96,512]{1,0:T(8,128)(2,1)S(1)}, u32[]{:S(2)}, u32[]{:S(2)}) collective-permute-start(bf16[96,512]{1,0:T(8,128)(2,1)S(1)} %get-tuple-element.35.refs_2_), channel_id=1, source_target_pairs={{0,4},{1,5},{2,6},{3,7},{4,0},{5,1},{6,2},{7,3},{8,12},{9,13},{10,... | collective-permute-start | bytes 294920 | tf_op jit(solution)/shard_map/ppermute | solution.py:401
  18.5 9.3 %copy-start = (bf16[1,2,640,256]{3,2,1,0:T(8,128)(2,1)S(1)}, bf16[1,2,640,256]{3,2,1,0:T(8,128)(2,1)}, u32[]{:S(2)}) copy-start(bf16[1,2,640,256]{3,2,1,0:T(8,128)(2,1)} %param.7) | copy-start | bytes 1966084
  29.6 9.6 %collective-permute-start.7 = (bf16[96,512]{1,0:T(8,128)(2,1)S(1)}, bf16[96,512]{1,0:T(8,128)(2,1)S(1)}, u32[]{:S(2)}, u32[]{:S(2)}) collective-permute-start(bf16[96,512]{1,0:T(8,128)(2,1)S(1)} %get-tuple-element.47), channel_id=1, source_target_pairs={{0,4},{1,5},{2,6},{3,7},{4,0},{5,1},{6,2},{7,3},{8,12},{9,13},{10,... | collective-permute-start | bytes 294920 | tf_op jit(solution)/shard_map/ppermute | solution.py:401
  29.7 11.2 %collective-permute-start.8 = (bf16[96,512]{1,0:T(8,128)(2,1)S(1)}, bf16[96,512]{1,0:T(8,128)(2,1)S(1)}, u32[]{:S(2)}, u32[]{:S(2)}) collective-permute-start(bf16[96,512]{1,0:T(8,128)(2,1)S(1)} %get-tuple-element.48), channel_id=1, source_target_pairs={{0,5},{1,4},{2,7},{3,6},{4,1},{5,0},{6,3},{7,2},{8,13},{9,12},{10,... | collective-permute-start | bytes 294920 | tf_op jit(solution)/shard_map/ppermute | solution.py:401
  31.9 14.4 %collective-permute-start.9 = (bf16[96,512]{1,0:T(8,128)(2,1)S(1)}, bf16[96,512]{1,0:T(8,128)(2,1)S(1)}, u32[]{:S(2)}, u32[]{:S(2)}) collective-permute-start(bf16[96,512]{1,0:T(8,128)(2,1)S(1)} %get-tuple-element.49), channel_id=1, source_target_pairs={{0,2},{1,3},{2,0},{3,1},{4,6},{5,7},{6,4},{7,5},{8,10},{9,11},{10,... | collective-permute-start | bytes 294920 | tf_op jit(solution)/shard_map/ppermute | solution.py:401
  32.7 13.6 %collective-permute-start.10 = (bf16[96,512]{1,0:T(8,128)(2,1)S(1)}, bf16[96,512]{1,0:T(8,128)(2,1)S(1)}, u32[]{:S(2)}, u32[]{:S(2)}) collective-permute-start(bf16[96,512]{1,0:T(8,128)(2,1)S(1)} %get-tuple-element.50), channel_id=1, source_target_pairs={{0,3},{1,2},{2,1},{3,0},{4,7},{5,6},{6,5},{7,4},{8,11},{9,10},{10,... | collective-permute-start | bytes 294920 | tf_op jit(solution)/shard_map/ppermute | solution.py:401
  34.0 12.3 %collective-permute-start.11 = (bf16[96,512]{1,0:T(8,128)(2,1)S(1)}, bf16[96,512]{1,0:T(8,128)(2,1)S(1)}, u32[]{:S(2)}, u32[]{:S(2)}) collective-permute-start(bf16[96,512]{1,0:T(8,128)(2,1)S(1)} %get-tuple-element.52), channel_id=1, source_target_pairs={{0,1},{1,0},{2,3},{3,2},{4,5},{5,4},{6,7},{7,6},{8,9},{9,8},{10,11... | collective-permute-start | bytes 294920 | tf_op jit(solution)/shard_map/ppermute | solution.py:401
  39.1 8.4 %collective-permute-start.12 = (bf16[96,512]{1,0:T(8,128)(2,1)S(1)}, bf16[96,512]{1,0:T(8,128)(2,1)S(1)}, u32[]{:S(2)}, u32[]{:S(2)}) collective-permute-start(bf16[96,512]{1,0:T(8,128)(2,1)S(1)} %get-tuple-element.53), channel_id=1, source_target_pairs={{0,6},{1,7},{2,4},{3,5},{4,2},{5,3},{6,0},{7,1},{8,14},{9,15},{10,... | collective-permute-start | bytes 294920 | tf_op jit(solution)/shard_map/ppermute | solution.py:401
  40.9 6.6 %collective-permute-start.13 = (bf16[96,512]{1,0:T(8,128)(2,1)S(1)}, bf16[96,512]{1,0:T(8,128)(2,1)S(1)}, u32[]{:S(2)}, u32[]{:S(2)}) collective-permute-start(bf16[96,512]{1,0:T(8,128)(2,1)S(1)} %get-tuple-element.54), channel_id=1, source_target_pairs={{0,7},{1,6},{2,5},{3,4},{4,3},{5,2},{6,1},{7,0},{8,15},{9,14},{10,... | collective-permute-start | bytes 294920 | tf_op jit(solution)/shard_map/ppermute | solution.py:401
  47.5 12.3 %copy-start.1 = (s32[160,256]{1,0:T(8,128)S(1)}, s32[160,256]{1,0:T(8,128)}, u32[]{:S(2)}) copy-start(s32[160,256]{1,0:T(8,128)} %refs_0_.1) | copy-start | bytes 491524
  48.2 7.1 %collective-permute-start.14 = (bf16[160,512]{1,0:T(8,128)(2,1)S(1)}, bf16[160,512]{1,0:T(8,128)(2,1)S(1)}, u32[]{:S(2)}, u32[]{:S(2)}) collective-permute-start(bf16[160,512]{1,0:T(8,128)(2,1)S(1)} %get-tuple-element.56), channel_id=1, source_target_pairs={{0,8},{8,0},{16,24},{24,16},{1,9},{9,1},{17,25},{25,17},{2,10},{10... | collective-permute-start | bytes 491528 | tf_op jit(solution)/shard_map/ppermute | solution.py:401
  49.7 10.0 %collective-permute-start.15 = (bf16[160,512]{1,0:T(8,128)(2,1)S(1)}, bf16[160,512]{1,0:T(8,128)(2,1)S(1)}, u32[]{:S(2)}, u32[]{:S(2)}) collective-permute-start(bf16[160,512]{1,0:T(8,128)(2,1)S(1)} %get-tuple-element.57), channel_id=1, source_target_pairs={{0,16},{8,24},{16,0},{24,8},{1,17},{9,25},{17,1},{25,9},{2,18},{10... | collective-permute-start | bytes 491528 | tf_op jit(solution)/shard_map/ppermute | solution.py:401
  51.2 8.5 %collective-permute-start.16 = (bf16[160,512]{1,0:T(8,128)(2,1)S(1)}, bf16[160,512]{1,0:T(8,128)(2,1)S(1)}, u32[]{:S(2)}, u32[]{:S(2)}) collective-permute-start(bf16[160,512]{1,0:T(8,128)(2,1)S(1)} %get-tuple-element.58), channel_id=1, source_target_pairs={{0,24},{8,16},{16,8},{24,0},{1,25},{9,17},{17,9},{25,1},{2,26},{10... | collective-permute-start | bytes 491528 | tf_op jit(solution)/shard_map/ppermute | solution.py:401
